TPU v7x, 32 devices: a whole 2x2x4 slice. The times are simulated.
32 devices in a mesh: dp: 8 (over z, x), seq: 4 (over y, core).
Axes of the slice: x: 2, y: 2, z: 4, core: 2. Of those that a mesh axis runs over, the one named last changes fastest.
Arguments:
- inputs: bfloat16 [192, 1024, 512], P('dp', 'seq'), may hold values from -6 to 6
- lengths: int32 [192], P('dp'), may hold values from 256 to 1024, as said below
- cotangent: bfloat16 [192, 1024, 512], P('dp', 'seq'), may hold values from -6 to 6
- w_query: bfloat16 [512, 512], P(('dp', 'seq')), may hold values from -0.25 to 0.25
- w_key: bfloat16 [512, 512], P(('dp', 'seq')), may hold values from -0.25 to 0.25
- w_value: bfloat16 [512, 512], P(('dp', 'seq')), may hold values from -0.25 to 0.25
- w_out: bfloat16 [512, 512], P(('dp', 'seq')), may hold values from -0.5 to 0.5
- w_up: bfloat16 [512, 2048], P(('dp', 'seq')), may hold values from -0.25 to 0.25
- w_down: bfloat16 [2048, 512], P(('dp', 'seq')), may hold values from -0.125 to 0.125
- gain_attn: bfloat16 [512], P(('dp', 'seq')), may hold values from 0.25 to 1.75
- gain_mlp: bfloat16 [512], P(('dp', 'seq')), may hold values from 0.25 to 1.75
Outputs:
- output: bfloat16 [192, 1024, 512], P('dp', 'seq')
- grad_input: float32 [192, 1024, 512], P('dp', 'seq')
- grad_query: float32 [512, 512], P(('dp', 'seq'))
- grad_key: float32 [512, 512], P(('dp', 'seq'))
- grad_value: float32 [512, 512], P(('dp', 'seq'))
- grad_out: float32 [512, 512], P(('dp', 'seq'))
- grad_up: float32 [512, 2048], P(('dp', 'seq'))
- grad_down: float32 [2048, 512], P(('dp', 'seq'))
- grad_gain_attn: float32 [512], P(('dp', 'seq'))
- grad_gain_mlp: float32 [512], P(('dp', 'seq'))
Inputs may be any that keep to these rules, and one draw needn't show every extreme that they name: Sequence b's valid slots are its first lengths[b]; some sequence has 1024 of them and some has 256.
All inputs are finite; a program needn't handle non-finite values.
Results may differ from a plain program's by a relative error of at most 0.012.
Values may be sent and summed in bfloat16 or wider, within the bound.
A program may use at most 320 MiB of HBM per device.

v0:
```python
from functools import partial
import math

import jax
import jax.numpy as jnp
from jax import lax
from jax.sharding import PartitionSpec as P

H = 8
HD = 64
SPAN = 128


def normed(values, gain_vec):
    return values * lax.rsqrt(jnp.mean(values * values, axis=-1, keepdims=True) + 1e-06) * gain_vec


def span_scores(query_blk, key_blk, key_sum, first_span):
    seq_group, slots_dev, model_width = query_blk.shape
    spans_dev = slots_dev // SPAN
    span_total = key_sum.shape[1]
    query_h = query_blk.reshape(seq_group, spans_dev, SPAN, H, HD)
    key_h = key_blk.reshape(seq_group, spans_dev, SPAN, H, HD)
    key_sh = key_sum.reshape(seq_group, span_total, H, HD)
    near_score = jnp.einsum(
        "bsihd,bsjhd->bshij", query_h, key_h, preferred_element_type=jnp.float32
    ) * HD ** (-0.5)
    far_score = jnp.einsum(
        "bsihd,bthd->bshit", query_h, key_sh, preferred_element_type=jnp.float32
    ) * HD ** (-0.5)
    row_index = lax.broadcasted_iota(jnp.int32, (SPAN, SPAN), 0)
    col_index = lax.broadcasted_iota(jnp.int32, (SPAN, SPAN), 1)
    causal = row_index >= col_index
    span_here = first_span + jnp.arange(spans_dev, dtype=jnp.int32)
    earlier = (jnp.arange(span_total, dtype=jnp.int32)[None, :] < span_here[:, None])[
        :, None, None, :
    ]
    near_score = jnp.where(causal, near_score, -1e30)
    far_score = jnp.where(earlier, far_score, -1e30)
    return (query_h, key_h, key_sh, near_score, far_score, causal, earlier)


def attend_forward(first_span, entry):
    query_blk, key_blk, value_blk, key_sum, value_sum = entry
    query_h, key_h, key_sh, near_score, far_score, causal, earlier = span_scores(
        query_blk, key_blk, key_sum, first_span
    )
    value_h = value_blk.reshape(key_h.shape)
    value_sh = value_sum.reshape(key_sh.shape)
    highest = jnp.maximum(
        jnp.max(near_score, axis=-1, keepdims=True), jnp.max(far_score, axis=-1, keepdims=True)
    )
    near_exp = jnp.exp(near_score - highest)
    far_exp = jnp.exp(far_score - highest)
    denom_sum = jnp.sum(near_exp, axis=-1, keepdims=True) + jnp.sum(far_exp, axis=-1, keepdims=True)
    near_prob = (near_exp / denom_sum).astype(jnp.bfloat16)
    far_prob = (far_exp / denom_sum).astype(jnp.bfloat16)
    attended = jnp.einsum(
        "bshij,bsjhd->bsihd", near_prob, value_h, preferred_element_type=jnp.float32
    )
    attended = attended + jnp.einsum(
        "bshit,bthd->bsihd", far_prob, value_sh, preferred_element_type=jnp.float32
    )
    return (attended.reshape(query_blk.shape).astype(jnp.bfloat16), highest + jnp.log(denom_sum))


def attend_backward(first_span, entry):
    query_blk, key_blk, value_blk, key_sum, value_sum, log_total, grad_att = entry
    query_h, key_h, key_sh, near_score, far_score, causal, earlier = span_scores(
        query_blk, key_blk, key_sum, first_span
    )
    value_h = value_blk.reshape(key_h.shape)
    value_sh = value_sum.reshape(key_sh.shape)
    near_prob = jnp.where(causal, jnp.exp(near_score - log_total), 0.0)
    far_prob = jnp.where(earlier, jnp.exp(far_score - log_total), 0.0)
    near_low = near_prob.astype(jnp.bfloat16)
    far_low = far_prob.astype(jnp.bfloat16)
    grad_h = grad_att.reshape(query_h.shape)
    d_value = jnp.einsum("bshij,bsihd->bsjhd", near_low, grad_h, preferred_element_type=jnp.float32)
    d_value_sum = jnp.einsum(
        "bshit,bsihd->bthd", far_low, grad_h, preferred_element_type=jnp.float32
    )
    d_near = jnp.einsum("bsihd,bsjhd->bshij", grad_h, value_h, preferred_element_type=jnp.float32)
    d_far = jnp.einsum("bsihd,bthd->bshit", grad_h, value_sh, preferred_element_type=jnp.float32)
    center = jnp.sum(d_near * near_prob, axis=-1, keepdims=True) + jnp.sum(
        d_far * far_prob, axis=-1, keepdims=True
    )
    d_near_s = (near_prob * (d_near - center)).astype(jnp.bfloat16)
    d_far_s = (far_prob * (d_far - center)).astype(jnp.bfloat16)
    scale_qk = HD ** (-0.5)
    d_query = jnp.einsum("bshij,bsjhd->bsihd", d_near_s, key_h, preferred_element_type=jnp.float32)
    d_query = (
        d_query
        + jnp.einsum("bshit,bthd->bsihd", d_far_s, key_sh, preferred_element_type=jnp.float32)
    ) * scale_qk
    d_key = (
        jnp.einsum("bshij,bsihd->bsjhd", d_near_s, query_h, preferred_element_type=jnp.float32)
        * scale_qk
    )
    d_key_sum = (
        jnp.einsum("bshit,bsihd->bthd", d_far_s, query_h, preferred_element_type=jnp.float32)
        * scale_qk
    )
    return (
        d_query.reshape(query_blk.shape),
        d_key.reshape(query_blk.shape),
        d_value.reshape(query_blk.shape),
        d_key_sum.reshape(key_sum.shape),
        d_value_sum.reshape(key_sum.shape),
    )


def body(
    inputs, lengths, cotangent, w_query, w_key, w_value, w_out, w_up, w_down, gain_attn, gain_mlp
):
    seq_count, slots_dev, model_width = inputs.shape
    spans_dev = slots_dev // SPAN
    first_span = lax.axis_index("seq") * spans_dev
    places = lax.axis_index("seq") * slots_dev + jnp.arange(slots_dev, dtype=jnp.int32)
    valid_mask = (places[None, :] < lengths[:, None]).astype(jnp.float32).reshape(-1, 1)
    seq_group = math.gcd(seq_count, max(1, 512 // slots_dev))
    blocks = seq_count // seq_group

    def split_blocks(array):
        return array.reshape((blocks, seq_group) + array.shape[1:])

    full_query, full_key, full_value, full_out, full_up, full_down, full_gain_a, full_gain_m = (
        lax.all_gather(w_query, ("dp", "seq"), axis=0, tiled=True),
        lax.all_gather(w_key, ("dp", "seq"), axis=0, tiled=True),
        lax.all_gather(w_value, ("dp", "seq"), axis=0, tiled=True),
        lax.all_gather(w_out, ("dp", "seq"), axis=0, tiled=True),
        lax.all_gather(w_up, ("dp", "seq"), axis=0, tiled=True),
        lax.all_gather(w_down, ("dp", "seq"), axis=0, tiled=True),
        lax.all_gather(gain_attn, ("dp", "seq"), axis=0, tiled=True),
        lax.all_gather(gain_mlp, ("dp", "seq"), axis=0, tiled=True),
    )
    flat_in = inputs.reshape(-1, model_width).astype(jnp.float32)
    normal_f, norm_first = jax.vjp(normed, flat_in, full_gain_a.astype(jnp.float32))
    normal_in = normal_f.astype(jnp.bfloat16)
    query = jnp.dot(normal_in, full_query, preferred_element_type=jnp.float32).astype(jnp.bfloat16)
    keys_all = jnp.dot(normal_in, full_key, preferred_element_type=jnp.float32).astype(jnp.bfloat16)
    values_all = jnp.dot(normal_in, full_value, preferred_element_type=jnp.float32).astype(
        jnp.bfloat16
    )
    key_sum = jnp.mean(
        keys_all.reshape(seq_count, spans_dev, SPAN, model_width), axis=2, dtype=jnp.float32
    ).astype(jnp.bfloat16)
    value_sum = jnp.mean(
        values_all.reshape(seq_count, spans_dev, SPAN, model_width), axis=2, dtype=jnp.float32
    ).astype(jnp.bfloat16)
    key_every, value_every = (
        lax.all_gather(key_sum, "seq", axis=1, tiled=True),
        lax.all_gather(value_sum, "seq", axis=1, tiled=True),
    )
    query_b = split_blocks(query.reshape(seq_count, slots_dev, model_width))
    key_b = split_blocks(keys_all.reshape(seq_count, slots_dev, model_width))
    value_b = split_blocks(values_all.reshape(seq_count, slots_dev, model_width))
    key_every_b = split_blocks(key_every)
    value_every_b = split_blocks(value_every)
    attended, log_total = lax.map(
        partial(attend_forward, first_span), (query_b, key_b, value_b, key_every_b, value_every_b)
    )
    attended = attended.reshape(-1, model_width)
    residual_mid = flat_in + jnp.dot(attended, full_out, preferred_element_type=jnp.float32)
    normal_mf, norm_second = jax.vjp(normed, residual_mid, full_gain_m.astype(jnp.float32))
    normal_mid = normal_mf.astype(jnp.bfloat16)
    up_proj = jnp.dot(normal_mid, full_up, preferred_element_type=jnp.float32)
    activated_f, gelu_back = jax.vjp(jax.nn.gelu, up_proj)
    activated = activated_f.astype(jnp.bfloat16)
    result = (
        residual_mid + jnp.dot(activated, full_down, preferred_element_type=jnp.float32)
    ) * valid_mask
    output = result.reshape(seq_count, slots_dev, model_width).astype(jnp.bfloat16)
    full_query, full_key, full_value, full_out, full_up, full_down, full_gain_a, full_gain_m = (
        lax.all_gather(w_query, ("dp", "seq"), axis=0, tiled=True),
        lax.all_gather(w_key, ("dp", "seq"), axis=0, tiled=True),
        lax.all_gather(w_value, ("dp", "seq"), axis=0, tiled=True),
        lax.all_gather(w_out, ("dp", "seq"), axis=0, tiled=True),
        lax.all_gather(w_up, ("dp", "seq"), axis=0, tiled=True),
        lax.all_gather(w_down, ("dp", "seq"), axis=0, tiled=True),
        lax.all_gather(gain_attn, ("dp", "seq"), axis=0, tiled=True),
        lax.all_gather(gain_mlp, ("dp", "seq"), axis=0, tiled=True),
    )
    grad_res = cotangent.reshape(-1, model_width).astype(jnp.float32) * valid_mask
    grad_branch = grad_res.astype(jnp.bfloat16)
    d_down = jnp.einsum("nf,nd->fd", activated, grad_branch, preferred_element_type=jnp.float32)
    d_act = jnp.einsum("nd,fd->nf", grad_branch, full_down, preferred_element_type=jnp.float32)
    d_upper = gelu_back(d_act)[0].astype(jnp.bfloat16)
    d_up = jnp.einsum("nd,nf->df", normal_mid, d_upper, preferred_element_type=jnp.float32)
    d_hn = jnp.einsum("nf,df->nd", d_upper, full_up, preferred_element_type=jnp.float32)
    d_mid_norm, d_gain_m = norm_second(d_hn)
    d_mid = grad_res + d_mid_norm
    d_branch = d_mid.astype(jnp.bfloat16)
    d_out = jnp.einsum("nd,ne->de", attended, d_branch, preferred_element_type=jnp.float32)
    d_att = jnp.einsum("ne,de->nd", d_branch, full_out, preferred_element_type=jnp.float32).astype(
        jnp.bfloat16
    )
    d_att_b = split_blocks(d_att.reshape(seq_count, slots_dev, model_width))
    d_query, d_key, d_value, d_key_sum, d_value_sum = lax.map(
        partial(attend_backward, first_span),
        (query_b, key_b, value_b, key_every_b, value_every_b, log_total, d_att_b),
    )
    d_key_sum = d_key_sum.reshape(seq_count, -1, model_width)
    d_value_sum = d_value_sum.reshape(seq_count, -1, model_width)
    own_key, own_value = (
        lax.psum_scatter(
            d_key_sum.astype(jnp.bfloat16), "seq", scatter_dimension=1, tiled=True
        ).astype(jnp.float32),
        lax.psum_scatter(
            d_value_sum.astype(jnp.bfloat16), "seq", scatter_dimension=1, tiled=True
        ).astype(jnp.float32),
    )
    d_query = d_query.reshape(-1, model_width).astype(jnp.bfloat16)
    d_key = (
        (d_key.reshape(seq_count, spans_dev, SPAN, model_width) + own_key[:, :, None, :] / SPAN)
        .reshape(-1, model_width)
        .astype(jnp.bfloat16)
    )
    d_value = (
        (d_value.reshape(seq_count, spans_dev, SPAN, model_width) + own_value[:, :, None, :] / SPAN)
        .reshape(-1, model_width)
        .astype(jnp.bfloat16)
    )
    d_wquery = jnp.einsum("nd,ne->de", normal_in, d_query, preferred_element_type=jnp.float32)
    d_wkey = jnp.einsum("nd,ne->de", normal_in, d_key, preferred_element_type=jnp.float32)
    d_wvalue = jnp.einsum("nd,ne->de", normal_in, d_value, preferred_element_type=jnp.float32)
    d_normal = jnp.einsum("ne,de->nd", d_query, full_query, preferred_element_type=jnp.float32)
    d_normal = d_normal + jnp.einsum(
        "ne,de->nd", d_key, full_key, preferred_element_type=jnp.float32
    )
    d_normal = d_normal + jnp.einsum(
        "ne,de->nd", d_value, full_value, preferred_element_type=jnp.float32
    )
    d_in_norm, d_gain_a = norm_first(d_normal)
    grad_input = (d_mid + d_in_norm).reshape(seq_count, slots_dev, model_width)
    sent_query, sent_key, sent_value, sent_out, sent_up, sent_down, sent_gain_a, sent_gain_m = (
        lax.psum_scatter(d_wquery, ("dp", "seq"), scatter_dimension=0, tiled=True),
        lax.psum_scatter(d_wkey, ("dp", "seq"), scatter_dimension=0, tiled=True),
        lax.psum_scatter(d_wvalue, ("dp", "seq"), scatter_dimension=0, tiled=True),
        lax.psum_scatter(d_out, ("dp", "seq"), scatter_dimension=0, tiled=True),
        lax.psum_scatter(d_up, ("dp", "seq"), scatter_dimension=0, tiled=True),
        lax.psum_scatter(d_down, ("dp", "seq"), scatter_dimension=0, tiled=True),
        lax.psum_scatter(d_gain_a, ("dp", "seq"), scatter_dimension=0, tiled=True),
        lax.psum_scatter(d_gain_m, ("dp", "seq"), scatter_dimension=0, tiled=True),
    )
    return (
        output,
        grad_input,
        sent_query,
        sent_key,
        sent_value,
        sent_out,
        sent_up,
        sent_down,
        sent_gain_a,
        sent_gain_m,
    )


def solution(mesh):
    placed = (
        P("dp", "seq", None),
        P("dp"),
        P("dp", "seq", None),
        P(("dp", "seq"), None),
        P(("dp", "seq"), None),
        P(("dp", "seq"), None),
        P(("dp", "seq"), None),
        P(("dp", "seq"), None),
        P(("dp", "seq"), None),
        P(("dp", "seq")),
        P(("dp", "seq")),
    )
    return jax.shard_map(
        body,
        mesh=mesh,
        in_specs=placed,
        out_specs=(
            P("dp", "seq", None),
            P("dp", "seq", None),
            P(("dp", "seq"), None),
            P(("dp", "seq"), None),
            P(("dp", "seq"), None),
            P(("dp", "seq"), None),
            P(("dp", "seq"), None),
            P(("dp", "seq"), None),
            P(("dp", "seq")),
            P(("dp", "seq")),
        ),
        check_vma=False,
    )
```

profile of v0, /device:TPU:0, one launch (start us, length us, event | category | flops | bytes accessed | tf_op | source)
XLA Modules:
  0.0 1910.4 jit_solution(12881387140663863526)
XLA Ops:
  10.5 42.0 %all-reduce.5 = (bf16[512]{0:T(512)(128)(2,1)S(1)}, bf16[512]{0:T(512)(128)(2,1)S(1)}) all-reduce(bf16[512]{0:T(512)(128)(2,1)S(1)} %dynamic-update-slice, bf16[512]{0:T(512)(128)(2,1)S(1)} %dynamic-update-slice.1), channel_id=1, replica_groups=mesh['dp'=8,'seq'=4] {'dp','seq'}, use_global_device_ids=true, to_apply=%add | all-reduce | flops 1024 | bytes 4096
  52.5 4.3 fusion.62
  58.1 42.3 %all_gather.37 = bf16[512,512]{1,0:T(8,128)(2,1)S(1)} all-gather(bf16[16,512]{1,0:T(8,128)(2,1)} %param.20), channel_id=1, replica_groups=mesh['dp'=8,'seq'=4] {'dp','seq'}, dimensions={0}, use_global_device_ids=true | all-gather | bytes 540672 | tf_op jit(solution)/shard_map/all_gather | solution.py:130
  100.4 4.5 fusion.60
  107.6 5.3 convolution_convert_fusion.3
  112.9 8.7 copy.291
  121.6 38.0 %all_gather.39 = bf16[512,512]{1,0:T(8,128)(2,1)S(1)} all-gather(bf16[16,512]{1,0:T(8,128)(2,1)S(1)} %copy-done.27), channel_id=1, replica_groups=mesh['dp'=8,'seq'=4] {'dp','seq'}, dimensions={0}, use_global_device_ids=true | all-gather | bytes 540672 | tf_op jit(solution)/shard_map/all_gather | solution.py:129
  159.6 8.3 convolution_convert_fusion.1
  167.9 8.9 copy.293
  176.8 4.3 convert_reduce_fusion.1
  181.1 5.6 all_gather.40
  187.5 4.1 convert_reduce_fusion
  191.7 5.6 all_gather.41
  198.1 39.5 %all_gather.38 = bf16[512,512]{1,0:T(8,128)(2,1)S(1)} all-gather(bf16[16,512]{1,0:T(8,128)(2,1)S(1)} %copy-done.28), channel_id=1, replica_groups=mesh['dp'=8,'seq'=4] {'dp','seq'}, dimensions={0}, use_global_device_ids=true | all-gather | bytes 540672 | tf_op jit(solution)/shard_map/all_gather | solution.py:128
  237.6 5.3 convolution_convert_fusion.2
  242.9 8.7 copy.292
  251.6 131.3 %while.30 = (s32[]{:T(128)}, bf16[12,2,256,512]{3,2,1,0:T(8,128)(2,1)}, f32[12,2,2,8,128,1]{4,3,2,1,5,0:T(8,128)}, bf16[12,2,256,512]{2,3,1,0:T(8,128)(2,1)}, bf...) while((s32[]{:T(128)}, ...), condition=%wide.region_8.9_spmd, body=%wide.region_3.8_spmd.sunk | while | flops 149696528 | bytes 21431460 | solution.py:160
  382.9 38.0 %all_gather.42 = bf16[512,512]{1,0:T(8,128)(2,1)S(1)} all-gather(bf16[16,512]{1,0:T(8,128)(2,1)S(1)} %copy-done.29), channel_id=1, replica_groups=mesh['dp'=8,'seq'=4] {'dp','seq'}, dimensions={0}, use_global_device_ids=true | all-gather | bytes 540672 | tf_op jit(solution)/shard_map/all_gather | solution.py:131
  420.9 10.5 multiply_reduce_fusion.4
  432.8 7.0 fusion.55
  439.8 34.2 %multiply_convert_fusion.2 = (bf16[6144,2048]{1,0:T(8,128)(2,1)}, f32[6144,2048]{1,0:T(8,128)}) fusion(bf16[512,2048]{1,0:T(8,128)(2,1)} %all-gather.3.cloned.1.call-done, f32[6144,512]{1,0:T(8,128)} %get-tuple-element.331, f32[512]{0:T(512)S(1)} %convert_element_type.181, f32[6144]{0:T(1024)S(1)} %fusion.73), kind=kOutput, calls=%fused_computation.104 | convolution fusion | flops 13007585280 | bytes 90204160 | tf_op jit(solution)/shard_map/dot_general | solution.py:167
  474.1 46.7 %fusion.52 = bf16[6144,2048]{1,0:T(8,128)(2,1)} fusion(f32[6144,2048]{1,0:T(8,128)} %get-tuple-element.333, bf16[6144,512]{1,0:T(8,128)(2,1)} %fusion.55, bf16[2048,512]{1,0:T(8,128)(2,1)} %all-gather.5.cloned.1.call-done), kind=kOutput, calls=%fused_computation.103 | convolution fusion | flops 13136560128 | bytes 83886080 | tf_op jit(solution)/shard_map/nd,fd->nf/dot_general | solution.py:187
  520.7 24.2 %multiply_reduce_fusion.2 = (f32[512]{0:T(512)}, f32[6144]{0:T(1024)S(1)}, f32[6144,512]{1,0:T(8,128)}) fusion(f32[6144,512]{1,0:T(8,128)} %get-tuple-element.331, f32[6144]{0:T(1024)S(1)} %fusion.73, f32[512]{0:T(512)S(1)} %convert_element_type.181, bf16[6144,2048]{1,0:T(8,128)(2,1)} %fusion.52, bf16[512,2048]{1,0:T(8,128)(2,1)S(1)} %copy-done.33), kind=kOutput, calls=%fused_computation.131 | convolution fusion | flops 12903770112 | bytes 52482048 | tf_op jit(solution)/shard_map/nf,df->nd/dot_general | solution.py:190
  545.0 11.9 fusion.53
  556.9 6.0 convolution_convert_fusion
  563.3 481.5 %while.31 = (s32[]{:T(128)}, bf16[12,2,256,512]{3,2,1,0:T(8,128)(2,1)}, f32[12,2,256,512]{3,2,1,0:T(8,128)}, f32[12,2,256,512]{3,2,1,0:T(8,128)}, bf16[12,2,8,51...) while((s32[]{:T(128)}, ...), condition=%wide.region_14.15_spmd, body=%wide.region_11.14_spmd.sunk | while | flops 363163648 | bytes 61441868 | solution.py:199
  1046.7 7.1 fusion.64
  1054.6 9.0 fusion.79
  1064.2 10.8 fusion.66
  1077.6 6.4 add_convert_fusion
  1084.0 4.4 fusion.81
  1091.0 6.3 add_convert_fusion.1
  1097.4 4.4 fusion.80
  1101.9 23.2 %fusion.74 = f32[512,2048]{1,0:T(8,128)} fusion(bf16[6144,2048]{1,0:T(8,128)(2,1)} %fusion.52, f32[6144,512]{1,0:T(8,128)} %get-tuple-element.331, f32[512]{0:T(512)S(1)} %convert_element_type.181, f32[6144]{0:T(1024)S(1)} %fusion.73), kind=kOutput, calls=%fused_computation.161 | convolution fusion | flops 12894339072 | bytes 41969664 | tf_op jit(solution)/shard_map/nd,nf->df/dot_general | solution.py:189
  1125.4 21.2 %fusion.82 = f32[2048,512]{1,0:T(8,128)} fusion(bf16[6144,2048]{1,0:T(8,128)(2,1)} %get-tuple-element.332, bf16[6144,512]{1,0:T(8,128)(2,1)} %fusion.55), kind=kOutput, calls=%fused_computation.169 | convolution fusion | flops 12884901888 | bytes 35651584 | tf_op jit(solution)/shard_map/nf,nd->fd/dot_general | solution.py:186
  1146.7 21.6 %multiply_convert_fusion.3 = bf16[6144,512]{1,0:T(8,128)(2,1)} fusion(f32[6144,512]{1,0:T(8,128)} %get-tuple-element.331, bf16[6144,2048]{1,0:T(8,128)(2,1)} %get-tuple-element.332, bf16[2048,512]{1,0:T(8,128)(2,1)S(1)} %copy-done.32, f32[6144]{0:T(1024)S(1)} %bitcast.273), kind=kOutput, calls=%fused_computation.136 | convolution fusion | flops 12894339072 | bytes 46161920 | tf_op jit(solution)/shard_map/dot_general | solution.py:171
  1168.3 9.6 fusion.77
  1177.9 9.1 fusion.57
  1187.0 9.2 fusion.56
  1196.1 9.4 fusion.78
  1205.5 20.2 %fusion.61 = (f32[512]{0:T(512)S(1)}, f32[6144]{0:T(1024)S(1)}, f32[6144,512]{1,0:T(8,128)}) fusion(bf16[24,256,512]{2,1,0:T(8,128)(2,1)} %param.15, f32[6144]{0:T(1024)S(1)} %copy-done.15, f32[512]{0:T(512)S(1)} %copy-done.26, bf16[6144,512]{1,0:T(8,128)(2,1)} %fusion.56, bf16[512,512]{1,0:T(8,128)(2,1)S(1)} %copy-done.9, f32[6144,512]{1,0:T(8,128)} %fusion.77, ...), kind=kOutput, calls=%fused_computation.126 | convolution fusion | flops 3249530368 | bytes 50909184 | tf_op jit(solution)/shard_map/ne,de->nd/dot_general | solution.py:231
  1225.8 37.0 %all-reduce.4 = (f32[512]{0:T(512)S(1)}, f32[512]{0:T(512)S(1)}) all-reduce(f32[512]{0:T(512)S(1)} %get-tuple-element.258, f32[512]{0:T(512)S(1)} %copy-done.30), channel_id=10, replica_groups=mesh['dp'=8,'seq'=4] {'dp','seq'}, use_global_device_ids=true, to_apply=%region_25.26.clone | all-reduce | flops 1024 | bytes 8192
  1263.9 16.3 fusion.54
  1280.2 76.8 %reduce-scatter.19.cloned.1.call-done = f32[16,512]{1,0:T(8,128)} async-done(((f32[512,512]{1,0:T(8,128)}), f32[16,512]{1,0:T(8,128)}) %reduce-scatter.19.cloned.1.call-update) | async-done | bytes 32784 | tf_op jit(solution)/shard_map/reduce_scatter | solution.py:240
  1357.0 133.7 %reduce-scatter.17.cloned.1.call-done = f32[16,512]{1,0:T(8,128)} async-done(((f32[512,512]{1,0:T(8,128)}), f32[16,512]{1,0:T(8,128)}) %reduce-scatter.17.cloned.1.call-update) | async-done | bytes 32784 | tf_op jit(solution)/shard_map/reduce_scatter | solution.py:239
  1490.7 133.6 %reduce-scatter.15.cloned.1.call-done = f32[16,512]{1,0:T(8,128)} async-done(((f32[512,512]{1,0:T(8,128)}), f32[16,512]{1,0:T(8,128)}) %reduce-scatter.15.cloned.1.call-update) | async-done | bytes 32784 | tf_op jit(solution)/shard_map/reduce_scatter | solution.py:238
  1624.3 139.6 %reduce-scatter.21.cloned.1.call-done = f32[16,2048]{1,0:T(8,128)} async-done(((f32[512,2048]{1,0:T(8,128)}), f32[16,2048]{1,0:T(8,128)}) %reduce-scatter.21.cloned.1.call-update) | async-done | bytes 131088 | tf_op jit(solution)/shard_map/reduce_scatter | solution.py:241
  1763.9 139.5 %reduce-scatter.23.cloned.1.call-done = f32[64,512]{1,0:T(8,128)} async-done(((f32[2048,512]{1,0:T(8,128)}), f32[64,512]{1,0:T(8,128)}) %reduce-scatter.23.cloned.1.call-update) | async-done | bytes 131088 | tf_op jit(solution)/shard_map/reduce_scatter | solution.py:242
  (1060 shorter events, 629.8 us)
Async XLA Ops:
  7.2 432.7 %all-gather.3.cloned.1.call-start = ((), (), s32[]{:S(2)}) async-start(), calls=%async_computation.8 | async-start | bytes 2162688 | tf_op jit(solution)/shard_map/all_gather | solution.py:132
  7.9 466.1 %all-gather.5.cloned.1.call-start = ((), (), s32[]{:S(2)}) async-start(), calls=%async_computation.9 | async-start | bytes 2162688 | tf_op jit(solution)/shard_map/all_gather | solution.py:133
  8.7 1066.4 %reduce-scatter.11.cloned.1.call-start = ((), (), s32[]{:S(2)}) async-start(), calls=%async_computation.11 | async-start | bytes 245760 | tf_op jit(solution)/shard_map/reduce_scatter | solution.py:209
  52.5 60.4 %copy-start.25 = (f32[512]{0:T(512)}, f32[512]{0:T(512)S(1)}, u32[]{:S(2)}) copy-start(f32[512]{0:T(512)S(1)} %convert_element_type.170) | copy-start | bytes 6148
  58.1 42.3 %copy-start.14 = (f32[6144]{0:T(1024)}, f32[6144]{0:T(1024)S(1)}, u32[]{:S(2)}) copy-start(f32[6144]{0:T(1024)S(1)} %rsqrt.23) | copy-start | bytes 73732
  100.4 12.5 copy-start.8
  107.6 14.0 copy-start.27
  167.9 30.1 %copy-start.28 = (bf16[16,512]{1,0:T(8,128)(2,1)S(1)}, bf16[16,512]{1,0:T(8,128)(2,1)}, u32[]{:S(2)}) copy-start(bf16[16,512]{1,0:T(8,128)(2,1)} %param.18) | copy-start | bytes 49156
  167.9 69.7 %slice-start.4 = ((s8[6291456]{0:T(1024)(128)(4,1)}), s8[2097152]{0:T(1024)(128)(4,1)S(1)}, s32[]{:S(2)}) async-start(s8[6291456]{0:T(1024)(128)(4,1)} %bitcast.259), calls=%async_computation.22 | async-start | bytes 4194304
  176.8 60.8 %slice-start.5 = ((s8[6291456]{0:T(1024)(128)(4,1)}), s8[4194304]{0:T(1024)(128)(4,1)S(1)}, s32[]{:S(2)}) async-start(s8[6291456]{0:T(1024)(128)(4,1)} %bitcast.259), calls=%async_computation.23 | async-start | bytes 8388608
  251.6 131.3 %copy-start.29 = (bf16[16,512]{1,0:T(8,128)(2,1)S(1)}, bf16[16,512]{1,0:T(8,128)(2,1)}, u32[]{:S(2)}) copy-start(bf16[16,512]{1,0:T(8,128)(2,1)} %param.21) | copy-start | bytes 49156
  474.1 46.7 %copy-start.33 = (bf16[512,2048]{1,0:T(8,128)(2,1)S(1)}, bf16[512,2048]{1,0:T(8,128)(2,1)}, u32[]{:S(2)}) copy-start(bf16[512,2048]{1,0:T(8,128)(2,1)} %all-gather.3.cloned.1.call-done) | copy-start | bytes 6291460
  520.7 24.2 %copy-start.17 = (f32[6144]{0:T(1024)S(1)}, f32[6144]{0:T(1024)}, u32[]{:S(2)}) copy-start(f32[6144]{0:T(1024)} %copy-done.16) | copy-start | bytes 73732
  520.7 24.2 %copy-start.21 = (f32[3,2,8,128]{3,1,2,0:T(2,128)S(1)}, f32[3,2,8,128]{3,1,2,0:T(2,128)}, u32[]{:S(2)}) copy-start(f32[3,2,8,128]{3,1,2,0:T(2,128)} %copy-done.20) | copy-start | bytes 73732
  563.3 483.3 %copy-start.24 = (f32[24,256]{1,0:T(8,128)S(1)}, f32[24,256]{1,0:T(8,128)}, u32[]{:S(2)}) copy-start(f32[24,256]{1,0:T(8,128)} %get-tuple-element.328) | copy-start | bytes 73732
  563.3 483.3 %copy-start.26 = (f32[512]{0:T(512)S(1)}, f32[512]{0:T(512)}, u32[]{:S(2)}) copy-start(f32[512]{0:T(512)} %copy-done.25) | copy-start | bytes 6148
  564.7 13.7 copy-start.3
  590.4 12.3 copy-start.1
  604.9 13.7 copy-start.3
  630.6 12.2 copy-start.1
  645.0 13.7 copy-start.3
  670.7 12.2 copy-start.1
  685.1 13.7 copy-start.3
  725.2 13.7 copy-start.3
  765.3 13.7 copy-start.3
  805.4 13.7 copy-start.3
  845.4 13.7 copy-start.3
  871.1 12.2 copy-start.1
  885.5 13.7 copy-start.3
  911.2 12.3 copy-start.1
  925.7 13.7 copy-start.3
  951.4 12.2 copy-start.1
  965.8 13.7 copy-start.3
  991.5 12.2 copy-start.1
  1005.9 13.7 copy-start.3
  1031.7 12.2 copy-start.1
  1046.6 41.9 %reduce-scatter.9.cloned.1.call-start = ((), (), s32[]{:S(2)}) async-start(), calls=%async_computation.10 | async-start | bytes 245760 | tf_op jit(solution)/shard_map/reduce_scatter | solution.py:206
  1054.6 225.6 %reduce-scatter.13.cloned.1.call-start = ((), (), s32[]{:S(2)}) async-start(), calls=%async_computation.12 | async-start | bytes 1081344 | tf_op jit(solution)/shard_map/reduce_scatter | solution.py:237
  1063.7 293.3 %reduce-scatter.19.cloned.1.call-start = ((), (), s32[]{:S(2)}) async-start(), calls=%async_computation.15 | async-start | bytes 1081344 | tf_op jit(solution)/shard_map/reduce_scatter | solution.py:240
  1075.0 415.7 %reduce-scatter.17.cloned.1.call-start = ((), (), s32[]{:S(2)}) async-start(), calls=%async_computation.14 | async-start | bytes 1081344 | tf_op jit(solution)/shard_map/reduce_scatter | solution.py:239
  1088.4 535.8 %reduce-scatter.15.cloned.1.call-start = ((), (), s32[]{:S(2)}) async-start(), calls=%async_computation.13 | async-start | bytes 1081344 | tf_op jit(solution)/shard_map/reduce_scatter | solution.py:238
  1101.8 662.0 %reduce-scatter.21.cloned.1.call-start = ((), (), s32[]{:S(2)}) async-start(), calls=%async_computation.16 | async-start | bytes 4325376 | tf_op jit(solution)/shard_map/reduce_scatter | solution.py:241
  1125.1 778.2 %reduce-scatter.23.cloned.1.call-start = ((), (), s32[]{:S(2)}) async-start(), calls=%async_computation.17 | async-start | bytes 4325376 | tf_op jit(solution)/shard_map/reduce_scatter | solution.py:242
  1125.4 21.3 %copy-start.22 = (f32[3,2,8,128]{3,1,2,0:T(2,128)S(1)}, f32[3,2,8,128]{3,1,2,0:T(2,128)}, u32[]{:S(2)}) copy-start(f32[3,2,8,128]{3,1,2,0:T(2,128)} %copy-done.20) | copy-start | bytes 73732
  1125.4 21.3 %copy-start.32 = (bf16[2048,512]{1,0:T(8,128)(2,1)S(1)}, bf16[2048,512]{1,0:T(8,128)(2,1)}, u32[]{:S(2)}) copy-start(bf16[2048,512]{1,0:T(8,128)(2,1)} %all-gather.5.cloned.1.call-done) | copy-start | bytes 6291460
  1146.7 21.6 %copy-start.13 = (bf16[512,512]{1,0:T(8,128)(2,1)S(1)}, bf16[512,512]{1,0:T(8,128)(2,1)}, u32[]{:S(2)}) copy-start(bf16[512,512]{1,0:T(8,128)(2,1)} %copy-done.12) | copy-start | bytes 1572868
  1205.5 20.3 %copy-start.30 = (f32[512]{0:T(512)S(1)}, f32[512]{0:T(512)}, u32[]{:S(2)}) copy-start(f32[512]{0:T(512)} %get-tuple-element.256) | copy-start | bytes 6148
  1205.5 58.4 %copy-start.19 = (f32[3,2,8,128]{3,1,2,0:T(2,128)S(1)}, f32[3,2,8,128]{3,1,2,0:T(2,128)}, u32[]{:S(2)}) copy-start(f32[3,2,8,128]{3,1,2,0:T(2,128)} %copy-done.18) | copy-start | bytes 73732
  (46 other events, 438.7 us)
Sparse Core Ops, SparseCore 0:
  10.9 59.1 all-gather.2
  72.9 55.7 all-gather.4
  1046.7 17.1 reduce-scatter.10
  1066.2 19.7 reduce-scatter.8
  1088.6 134.7 reduce-scatter.12
  1226.2 130.7 reduce-scatter.18
  1359.8 130.8 reduce-scatter.16
  1493.6 130.6 reduce-scatter.14
  1627.1 136.7 reduce-scatter.20
  1766.6 136.7 reduce-scatter.22
where the time goes:
time: 1930 us; the launch traced here: 1910 us
  waiting for transfers between devices  625 us (32%)
  matrix products  462 us (24%)
  local copies, waits for them, and re-layouts  441 us (23%)
  blocking collectives  248 us (13%)
  other arithmetic  115 us (6%)
    dynamic_update_slice x108, local copies, waits for them, and re-layouts, body(): lax.map(partial(attend_backward, first_span), (query_b, key_b, value_b, k...  197 us
    reduce_scatter x1, waiting for transfers between devices, body(): lax.psum_scatter(d_up, ('dp', 'seq'), scatter_dimension=0, tiled=True)  140 us
    reduce_scatter x1, waiting for transfers between devices, body(): lax.psum_scatter(d_down, ('dp', 'seq'), scatter_dimension=0, tiled=True)  139 us
    reduce_scatter x1, waiting for transfers between devices, body(): lax.psum_scatter(d_wvalue, ('dp', 'seq'), scatter_dimension=0, tiled=True)  134 us
    reduce_scatter x1, waiting for transfers between devices, body(): lax.psum_scatter(d_wkey, ('dp', 'seq'), scatter_dimension=0, tiled=True)  134 us
    dynamic_slice x120, local copies, waits for them, and re-layouts, body(): lax.map(partial(attend_forward, first_span), (query_b, key_b, value_b, ke...  120 us
    unnamed x2, blocking collectives  79 us
    reduce_scatter x1, waiting for transfers between devices, body(): lax.psum_scatter(d_out, ('dp', 'seq'), scatter_dimension=0, tiled=True)  76.8 us
  transfers between devices with their start and end apart: 10, of which 5 were waited for; matrix products, arithmetic and copies ran while one was open for 23% of the time, Pallas kernels for 0%

commit v1 on v0

v1 whole, which is shorter than its diff:
```python
from functools import partial

import jax
import jax.numpy as jnp
from jax import lax
from jax.experimental import pallas as pl
from jax.experimental.pallas import tpu as pltpu
from jax.sharding import PartitionSpec as P

H = 8
HD = 64
SPAN = 128
EPS = 1e-06
K0 = 0.7978845608028654
K1 = 0.044715
FARP = 16
f32 = jnp.float32
bf = jnp.bfloat16
MESH = pl.DeviceIdType.MESH
VMEM_LIMIT = 62 << 20


def dot(a, b, ca=1, cb=0):
    return lax.dot_general(a, b, (((ca,), (cb,)), ((), ())), preferred_element_type=f32)


def sds(shape, dtype):
    return jax.ShapeDtypeStruct(shape, dtype)


def full(shape):
    return pl.BlockSpec(shape, lambda i: (0,) * len(shape), pipeline_mode=pl.Buffered(1))


def pair_diag(a):
    lane = lax.broadcasted_iota(jnp.int32, a.shape, 1)
    zero = jnp.zeros_like(a)
    return jnp.concatenate([jnp.where(lane < HD, a, zero), jnp.where(lane >= HD, a, zero)], axis=0)


def causal_mask():
    j = lax.broadcasted_iota(jnp.int32, (SPAN, 2 * SPAN), 0)
    i = lax.broadcasted_iota(jnp.int32, (SPAN, 2 * SPAN), 1)
    return j <= jnp.where(i >= SPAN, i - SPAN, i)


def gain_row(tiles, which, ndev, rows):
    width = ndev * rows
    r = lax.broadcasted_iota(jnp.int32, (ndev * 8, 128), 0)
    l = lax.broadcasted_iota(jnp.int32, (ndev * 8, 128), 1)
    keep = jnp.where((r % 8 == which) & (l < rows), tiles, 0.0).astype(bf)
    a = lax.broadcasted_iota(jnp.int32, (128, width), 0)
    b = lax.broadcasted_iota(jnp.int32, (128, width), 1)
    spread = dot(keep, jnp.where(b % rows == a, 1.0, 0.0).astype(bf))
    d = lax.broadcasted_iota(jnp.int32, (ndev * 8, width), 0)
    c = lax.broadcasted_iota(jnp.int32, (ndev * 8, width), 1)
    return jnp.sum(jnp.where(d // 8 == c // rows, spread, 0.0), axis=0, keepdims=True)


class Place:
    def __init__(self, dims):
        self.nz, self.nx, self.ny, self.nc = dims
        dp, seq = lax.axis_index("dp"), lax.axis_index("seq")
        self.z, self.x = dp // self.nx, dp % self.nx
        self.y, self.c = seq // self.nc, seq % self.nc

    def at(self, z=None, x=None, y=None, c=None):
        z = self.z if z is None else z
        x = self.x if x is None else x
        y = self.y if y is None else y
        c = self.c if c is None else c
        return (z * self.nx + x, y * self.nc + c)

    def line(self, axis):
        return getattr(self, axis), getattr(self, "n" + axis)

    def partners(self, axis):
        me, n = self.line(axis)
        return [(o, (me + o) % n, (me + n - o) % n) for o in range(1, n)]

    def greet(self, others):
        barrier = pltpu.get_barrier_semaphore()
        for other in others:
            pl.semaphore_signal(barrier, inc=1, device_id=other, device_id_type=MESH)
        pl.semaphore_wait(barrier, len(others))

    def others(self):
        return [self.at(**{a: to}) for a in ("z", "x", "y", "c") for _, to, _ in self.partners(a)]


class Copies:
    def __init__(self, send_sem, recv_sem):
        self.send_sem, self.recv_sem, self.used = send_sem, recv_sem, 0

    def make(self, src, dst, landed, device):
        k = self.used
        self.used += 1
        out = pltpu.make_async_remote_copy(
            src_ref=src, dst_ref=dst, send_sem=self.send_sem.at[k], recv_sem=self.recv_sem.at[k],
            device_id=device, device_id_type=MESH,
        )
        into = pltpu.make_async_remote_copy(
            src_ref=src, dst_ref=landed, send_sem=self.send_sem.at[k], recv_sem=self.recv_sem.at[k],
            device_id=device, device_id_type=MESH,
        )
        return out, into


def start(copies):
    for out, _ in copies:
        out.start()


def finish(copies):
    for out, into in copies:
        out.wait_send()
        into.wait_recv()


def halves(ref):
    n = ref.shape[-1] // 2
    return pl.ds(0, n), pl.ds(n, n)


def gather_phases(pc, cp, pieces, wholes):
    z, x, y, c = pc.z, pc.x, pc.y, pc.c
    first, second, third, last = [], [], [], []
    for piece, whole in zip(pieces, wholes):
        for _, to, fr in pc.partners("z"):
            first.append(cp.make(piece, whole.at[z, x, y, c], whole.at[fr, x, y, c], pc.at(z=to)))
    for whole in wholes:
        a, b = halves(whole)
        for _, to, fr in pc.partners("x"):
            v = whole.at[:, x, y, c, :, a]
            second.append(cp.make(v, v, whole.at[:, fr, y, c, :, a], pc.at(x=to)))
        for _, to, fr in pc.partners("y"):
            v = whole.at[:, x, y, c, :, b]
            second.append(cp.make(v, v, whole.at[:, x, fr, c, :, b], pc.at(y=to)))
    for whole in wholes:
        a, b = halves(whole)
        for _, to, fr in pc.partners("y"):
            v = whole.at[:, :, y, c, :, a]
            third.append(cp.make(v, v, whole.at[:, :, fr, c, :, a], pc.at(y=to)))
        for _, to, fr in pc.partners("x"):
            v = whole.at[:, x, :, c, :, b]
            third.append(cp.make(v, v, whole.at[:, fr, :, c, :, b], pc.at(x=to)))
    for whole in wholes:
        for _, to, fr in pc.partners("c"):
            v = whole.at[:, :, :, c]
            last.append(cp.make(v, v, whole.at[:, :, :, fr], pc.at(c=to)))
    return first, second, third, last


def gather_kernel(dims, spans_dev, n_w, *refs):
    x_ref = refs[0]
    pieces = refs[1 : 1 + n_w]
    wholes = refs[1 + n_w : 1 + 2 * n_w]
    mean_out = refs[1 + 2 * n_w]
    mean_ref, local_sem, send_sem, recv_sem = refs[2 + 2 * n_w :]
    pc = Place(dims)
    cp = Copies(send_sem, recv_sem)
    phases = gather_phases(pc, cp, pieces, wholes)
    seq = lax.axis_index("seq")
    seqn = pc.ny * pc.nc
    t0 = seq * spans_dev
    i, n = pl.program_id(0), pl.num_programs(0)
    means = []
    for o in range(1, seqn):
        to, fr = (seq + o) % seqn, (seq + seqn - o) % seqn
        v = mean_ref.at[pl.ds(t0, spans_dev)]
        means.append(
            cp.make(v, v, mean_ref.at[pl.ds(fr * spans_dev, spans_dev)], (lax.axis_index("dp"), to))
        )
    own = [
        pltpu.make_async_copy(piece, whole.at[pc.z, pc.x, pc.y, pc.c], local_sem.at[k])
        for k, (piece, whole) in enumerate(zip(pieces, wholes))
    ]

    @pl.when(i == 0)
    def _():
        seq_peers = [(lax.axis_index("dp"), (seq + o) % seqn) for o in range(1, seqn)]
        zx = [pc.at(**{a: to}) for a in ("z", "x") for _, to, _ in pc.partners(a)]
        pc.greet(zx + seq_peers)
        for copy in own:
            copy.start()
        start(phases[0])

    T = x_ref.shape[0]
    x = x_ref[...].astype(f32)
    r = lax.rsqrt(jnp.mean(x * x, axis=1, keepdims=True) + EPS)
    xr = x * r
    nseq = T // (SPAN * spans_dev)
    for s in range(T // SPAN):
        row = jnp.sum(xr[s * SPAN : (s + 1) * SPAN], axis=0, keepdims=True) * (1.0 / SPAN)
        mean_ref[t0 + s % spans_dev, pl.ds(i * nseq + s // spans_dev, 1), :] = row

    @pl.when(i == n - 1)
    def _():
        start(means)
        for copy in own:
            copy.wait()
        finish(phases[0])
        for k in range(1, 4):
            start(phases[k])
            finish(phases[k])
        finish(means)
        mean_out[...] = mean_ref[...]


def gather_call(dims, slots, block, x, pieces):
    n_tok, width = x.shape
    spans_dev = slots // SPAN
    seqs = n_tok // slots
    nz, nx, ny, nc = dims
    spans_all = spans_dev * ny * nc
    n_w = len(pieces)
    hbm = pl.BlockSpec(memory_space=pl.ANY)
    copies = n_w * ((nz - 1) + 2 * (nx - 1) + 2 * (ny - 1) + (nc - 1)) + ny * nc - 1
    return pl.pallas_call(
        partial(gather_kernel, dims, spans_dev, n_w),
        grid=(n_tok // block,),
        in_specs=[pl.BlockSpec((block, width), lambda i: (i, 0))] + [hbm] * n_w,
        out_specs=[hbm] * n_w + [full((spans_all, seqs, width))],
        out_shape=[sds(dims + p.shape, p.dtype) for p in pieces] + [sds((spans_all, seqs, width), f32)],
        scratch_shapes=[
            pltpu.VMEM((spans_all, seqs, width), f32),
            pltpu.SemaphoreType.DMA((n_w,)),
            pltpu.SemaphoreType.DMA((copies,)),
            pltpu.SemaphoreType.DMA((copies,)),
        ],
        compiler_params=pltpu.CompilerParams(
            vmem_limit_bytes=VMEM_LIMIT, collective_id=0, has_side_effects=True,
            dimension_semantics=("arbitrary",),
        ),
    )(x, *pieces)


def scatter_kernel(dims, spans_dev, g_ref, dks_ref, dvs_ref, sum_ref, own_k_ref, own_v_ref,
                   got1, held1, got2a, got2b, held2, got3a, got3b, held3, got4,
                   far_send, far_got, send_sem, recv_sem):
    pc = Place(dims)
    cp = Copies(send_sem, recv_sem)
    z, x, y, c = pc.z, pc.x, pc.y, pc.c
    seq, dp = lax.axis_index("seq"), lax.axis_index("dp")
    seqn = pc.ny * pc.nc
    seq_peers = [(dp, (seq + o) % seqn) for o in range(1, seqn)]
    zx = [pc.at(**{a: to}) for a in ("z", "x") for _, to, _ in pc.partners(a)]
    pc.greet(zx + seq_peers)
    a, b = halves(g_ref)
    one = [
        cp.make(g_ref.at[:, :, :, to], got1.at[o - 1], got1.at[o - 1], pc.at(c=to))
        for o, to, _ in pc.partners("c")
    ]
    start(one)
    far_send[0] = dks_ref[...].astype(bf)
    far_send[1] = dvs_ref[...].astype(bf)
    far = []
    for o in range(1, seqn):
        to = (seq + o) % seqn
        far.append(
            cp.make(
                far_send.at[:, pl.ds(to * spans_dev, spans_dev)], far_got.at[o - 1], far_got.at[o - 1], (dp, to)
            )
        )
    start(far)
    finish(one)
    acc = g_ref[:, :, :, c].astype(f32)
    for o in range(pc.nc - 1):
        acc = acc + got1[o].astype(f32)
    held1[...] = acc.astype(bf)
    two = [
        cp.make(held1.at[:, to, :, :, a], got2a.at[o - 1], got2a.at[o - 1], pc.at(x=to))
        for o, to, _ in pc.partners("x")
    ] + [
        cp.make(held1.at[:, :, to, :, b], got2b.at[o - 1], got2b.at[o - 1], pc.at(y=to))
        for o, to, _ in pc.partners("y")
    ]
    start(two)
    finish(far)
    own = pl.ds(seq * spans_dev, spans_dev)
    tot_k, tot_v = dks_ref[own], dvs_ref[own]
    for o in range(seqn - 1):
        tot_k = tot_k + far_got[o, 0].astype(f32)
        tot_v = tot_v + far_got[o, 1].astype(f32)
    own_k_ref[...] = tot_k.astype(bf)
    own_v_ref[...] = tot_v.astype(bf)
    finish(two)
    half = g_ref.shape[-1] // 2
    acc = held1[:, x, :, :, :half].astype(f32)
    for o in range(pc.nx - 1):
        acc = acc + got2a[o].astype(f32)
    held2[0, :, : pc.ny] = acc.astype(bf)
    acc = held1[:, :, y, :, half:].astype(f32)
    for o in range(pc.ny - 1):
        acc = acc + got2b[o].astype(f32)
    held2[1, :, : pc.nx] = acc.astype(bf)
    three = [
        cp.make(held2.at[0, :, to], got3a.at[o - 1], got3a.at[o - 1], pc.at(y=to))
        for o, to, _ in pc.partners("y")
    ] + [
        cp.make(held2.at[1, :, to], got3b.at[o - 1], got3b.at[o - 1], pc.at(x=to))
        for o, to, _ in pc.partners("x")
    ]
    start(three)
    finish(three)
    acc = held2[0, :, y].astype(f32)
    for o in range(pc.ny - 1):
        acc = acc + got3a[o].astype(f32)
    held3[:, :, :half] = acc.astype(bf)
    acc = held2[1, :, x].astype(f32)
    for o in range(pc.nx - 1):
        acc = acc + got3b[o].astype(f32)
    held3[:, :, half:] = acc.astype(bf)
    four = [
        cp.make(held3.at[to], got4.at[o - 1], got4.at[o - 1], pc.at(z=to)) for o, to, _ in pc.partners("z")
    ]
    start(four)
    finish(four)
    acc = held3[z].astype(f32)
    for o in range(pc.nz - 1):
        acc = acc + got4[o].astype(f32)
    sum_ref[...] = acc


def scatter_call(dims, slots, grads, dks, dvs):
    nz, nx, ny, nc = dims
    rows, width = grads.shape[1:]
    half = width // 2
    spans_dev = slots // SPAN
    spans_all, seqs, _ = dks.shape
    seqn = ny * nc
    most = max(nx, ny)
    copies = (nc - 1) + 2 * (nx - 1) + 2 * (ny - 1) + (nz - 1) + (seqn - 1)
    vm = pl.BlockSpec(memory_space=pltpu.VMEM)
    return pl.pallas_call(
        partial(scatter_kernel, dims, spans_dev),
        in_specs=[vm] * 3,
        out_specs=[vm] * 3,
        out_shape=[sds((rows, width), f32)] + [sds((spans_dev, seqs, dks.shape[2]), bf)] * 2,
        scratch_shapes=[
            pltpu.VMEM((nc - 1, nz, nx, ny, rows, width), bf),
            pltpu.VMEM((nz, nx, ny, rows, width), bf),
            pltpu.VMEM((nx - 1, nz, ny, rows, half), bf),
            pltpu.VMEM((ny - 1, nz, nx, rows, half), bf),
            pltpu.VMEM((2, nz, most, rows, half), bf),
            pltpu.VMEM((ny - 1, nz, rows, half), bf),
            pltpu.VMEM((nx - 1, nz, rows, half), bf),
            pltpu.VMEM((nz, rows, width), bf),
            pltpu.VMEM((nz - 1, rows, width), bf),
            pltpu.VMEM((2, spans_all, seqs, dks.shape[2]), bf),
            pltpu.VMEM((seqn - 1, 2, spans_dev, seqs, dks.shape[2]), bf),
            pltpu.SemaphoreType.DMA((copies,)),
            pltpu.SemaphoreType.DMA((copies,)),
        ],
        compiler_params=pltpu.CompilerParams(
            vmem_limit_bytes=VMEM_LIMIT, collective_id=1, has_side_effects=True
        ),
    )(grads.reshape(dims + (rows, width)), dks, dvs)


def attend_forward_kernel(slots, x_ref, mean_ref, wq_ref, wk_ref, wv_ref, ga_ref,
                          q_ref, k_ref, v_ref, att_ref, lse_ref, ks_ref, vs_ref, tmp_ref):
    T, D = x_ref.shape
    spans_all, seqs, _ = mean_ref.shape
    i = pl.program_id(0)
    spt, nseq = slots // SPAN, T // slots
    ga = ga_ref[...]

    @pl.when(i == 0)
    def _():
        mb = (mean_ref[...].reshape(spans_all * seqs, D) * ga).astype(bf)
        for w_ref, out in ((wk_ref, ks_ref), (wv_ref, vs_ref)):
            sums = dot(mb, w_ref[...])
            tmp_ref[...] = jnp.zeros_like(tmp_ref)
            for t in range(spans_all):
                tmp_ref[:, t, :] = sums[t * seqs : (t + 1) * seqs]
            out[...] = tmp_ref[...].astype(bf)

    x = x_ref[...].astype(f32)
    r = lax.rsqrt(jnp.mean(x * x, axis=1, keepdims=True) + EPS)
    xn = (x * r * ga).astype(bf)
    q_ref[...] = (dot(xn, wq_ref[...]).astype(bf) * (HD**-0.5)).astype(bf)
    k_ref[...] = dot(xn, wk_ref[...]).astype(bf)
    v_ref[...] = dot(xn, wv_ref[...]).astype(bf)
    causal = causal_mask()
    t_row = lax.broadcasted_iota(jnp.int32, (FARP, 2 * SPAN), 0)
    first = lax.axis_index("seq") * spt
    for s in range(T // SPAN):
        seq = i * nseq + s // spt
        far = t_row < (first + s % spt)
        rows = slice(s * SPAN, (s + 1) * SPAN)
        for p in range(D // 128):
            ln = slice(p * 128, (p + 1) * 128)
            ke = jnp.concatenate([k_ref[rows, ln], ks_ref[seq, :, ln]], axis=0)
            ve = jnp.concatenate([v_ref[rows, ln], vs_ref[seq, :, ln]], axis=0)
            sc = dot(ke, pair_diag(q_ref[rows, ln]), 1, 1)
            sn = jnp.where(causal, sc[:SPAN], -1e30)
            sf = jnp.where(far, sc[SPAN:], -1e30)
            m = jnp.maximum(jnp.max(sn, axis=0, keepdims=True), jnp.max(sf, axis=0, keepdims=True))
            en = jnp.exp(sn - m)
            ef = jnp.exp(sf - m)
            l = jnp.sum(en, axis=0, keepdims=True) + jnp.sum(ef, axis=0, keepdims=True)
            rl = 1.0 / l
            pb = jnp.concatenate([(en * rl).astype(bf), (ef * rl).astype(bf)], axis=0)
            at = dot(ve, pb, 0, 0)
            att_ref[rows, ln] = jnp.concatenate([at[:HD, :SPAN], at[HD:, SPAN:]], axis=0).astype(bf).T
            total = m + jnp.log(l)
            lse_ref[2 * p : 2 * p + 1, rows] = total[:, :SPAN]
            lse_ref[2 * p + 1 : 2 * p + 2, rows] = total[:, SPAN:]


def attend_forward_call(slots, block, x, mean, wq, wk, wv, ga):
    n_tok, D = x.shape
    seqs = n_tok // slots
    tok = pl.BlockSpec((block, D), lambda i: (i, 0))
    summ = (seqs, FARP, D)
    return pl.pallas_call(
        partial(attend_forward_kernel, slots),
        grid=(n_tok // block,),
        in_specs=[tok, full(mean.shape), full((D, D)), full((D, D)), full((D, D)), full((1, D))],
        out_specs=[tok] * 4 + [pl.BlockSpec((H, block), lambda i: (0, i)), full(summ), full(summ)],
        out_shape=[sds((n_tok, D), bf)] * 4 + [sds((H, n_tok), f32), sds(summ, bf), sds(summ, bf)],
        scratch_shapes=[pltpu.VMEM(summ, f32)],
        compiler_params=pltpu.CompilerParams(
            vmem_limit_bytes=VMEM_LIMIT, dimension_semantics=("arbitrary",)
        ),
    )(x, mean, wq, wk, wv, ga)


def mlp_kernel(chunk, slots, ndev, len_ref, x_ref, att_ref, cot_ref, wo_ref, wu_ref, wd_ref, gm_ref,
               out_ref, datt_ref, dmid_ref, gsum_ref, adown, aup, aout, agm):
    T, D = x_ref.shape
    FF = wu_ref.shape[1]
    i, n = pl.program_id(0), pl.num_programs(0)

    @pl.when(i == 0)
    def _():
        for acc in (adown, aup, aout, agm):
            acc[...] = jnp.zeros_like(acc)

    att = att_ref[...]
    mid = x_ref[...].astype(f32) + dot(att, wo_ref[...])
    r = lax.rsqrt(jnp.mean(mid * mid, axis=1, keepdims=True) + EPS)
    gm = gm_ref[...]
    hn = (mid * r * gm).astype(bf)
    nseq = T // slots
    row = lax.broadcasted_iota(jnp.int32, (slots, 1), 0) + lax.axis_index("seq") * slots
    valid = jnp.concatenate(
        [jnp.where(row < len_ref[i * nseq + s], 1.0, 0.0) for s in range(nseq)], axis=0
    )
    g = cot_ref[...].astype(f32) * valid
    gb = g.astype(bf)
    gbt = gb.T
    hnt = hn.T
    y = jnp.zeros((T, D), f32)
    dhn = jnp.zeros((T, D), f32)
    for j in range(FF // chunk):
        sl = slice(j * chunk, (j + 1) * chunk)
        u = dot(hn, wu_ref[:, sl])
        u2 = u * u
        h = 0.5 + 0.5 * jnp.tanh(u * (K0 + (K0 * K1) * u2))
        act = (u * h).astype(bf)
        da = dot(gb, wd_ref[sl, :], 1, 1)
        slope = h + (u * (K0 + (3 * K0 * K1) * u2)) * ((h + h) * (1.0 - h))
        du = (da * slope).astype(bf)
        y = y + dot(act, wd_ref[sl, :])
        dhn = dhn + dot(du, wu_ref[:, sl], 1, 1)
        adown[:, sl] += dot(gbt, act)
        aup[:, sl] += dot(hnt, du)
    out_ref[...] = ((mid + y) * valid).astype(bf)
    mr = mid * r
    dm = dhn * mr
    agm[...] += jnp.sum(dm.reshape(T // 8, 8, D), axis=0)
    coef = jnp.mean(dm * gm, axis=1, keepdims=True)
    db = (g + r * (dhn * gm - mr * coef)).astype(bf)
    dmid_ref[...] = db
    aout[...] += dot(att, db, 0, 0)
    datt_ref[...] = dot(db, wo_ref[...], 1, 1).astype(bf)

    @pl.when(i == n - 1)
    def _():
        rd, rf = D // ndev, FF // ndev
        gsum_ref[:, :rd, :] = aout[...].reshape(ndev, rd, D).astype(bf)
        for j in range(FF // D):
            gsum_ref[:, rd * (j + 1) : rd * (j + 2), :] = (
                aup[:, j * D : (j + 1) * D].reshape(ndev, rd, D).astype(bf)
            )
            part = adown[:, j * D : (j + 1) * D].T.astype(bf)
            nd = D // rf
            gsum_ref[j * nd : (j + 1) * nd, rd * (FF // D + 1) : rd * (FF // D + 1) + rf, :] = part.reshape(
                nd, rf, D
            )
        gsum_ref[:, rd * (FF // D + 1) + rf :, :] = spread_gain(agm[...], ndev, rd).astype(bf)


def spread_gain(parts, ndev, rd):
    D = parts.shape[1]
    total = jnp.sum(parts, axis=0, keepdims=True)
    d = lax.broadcasted_iota(jnp.int32, (ndev, 16, D), 0)
    s = lax.broadcasted_iota(jnp.int32, (ndev, 16, D), 1)
    l = lax.broadcasted_iota(jnp.int32, (ndev, 16, D), 2)
    return jnp.where((s == 0) & (l // rd == d), total.reshape(1, 1, D), 0.0)


def mlp_call(chunk, slots, block, ndev, lens, x, att, cot, wo, wu, wd, gm):
    n_tok, D = x.shape
    FF = wu.shape[1]
    tok = pl.BlockSpec((block, D), lambda i: (i, 0))
    rows = D // ndev * (FF // D + 1) + FF // ndev + 16
    return pl.pallas_call(
        partial(mlp_kernel, chunk, slots, ndev),
        grid=(n_tok // block,),
        in_specs=[pl.BlockSpec(memory_space=pltpu.SMEM), tok, tok, tok]
        + [full((D, D)), full((D, FF)), full((FF, D)), full((1, D))],
        out_specs=[tok, tok, tok, full((ndev, rows, D))],
        out_shape=[sds((n_tok, D), bf)] * 3 + [sds((ndev, rows, D), bf)],
        scratch_shapes=[pltpu.VMEM((D, FF), f32), pltpu.VMEM((D, FF), f32), pltpu.VMEM((D, D), f32),
                        pltpu.VMEM((8, D), f32)],
        compiler_params=pltpu.CompilerParams(
            vmem_limit_bytes=VMEM_LIMIT, dimension_semantics=("arbitrary",)
        ),
    )(lens, x, att, cot, wo, wu, wd, gm)


def attend_backward_kernel(slots, ndev, x_ref, q_ref, k_ref, v_ref, da_ref, lse_ref, mean_ref, ks_ref, vs_ref,
                           wq_ref, wk_ref, wv_ref, ga_ref, dxn_ref, gsum_ref, dks_ref, dvs_ref, aq, ak, av, aga):
    T, D = x_ref.shape
    spans_all, seqs, _ = mean_ref.shape
    i, n = pl.program_id(0), pl.num_programs(0)
    ga = ga_ref[...]

    @pl.when(i == 0)
    def _():
        for acc in (aq, ak, av, aga):
            acc[...] = jnp.zeros_like(acc)

    x = x_ref[...].astype(f32)
    r = lax.rsqrt(jnp.mean(x * x, axis=1, keepdims=True) + EPS)
    xr = x * r
    xn = (xr * ga).astype(bf)
    causal = causal_mask()
    spt, nseq = slots // SPAN, T // slots
    t_row = lax.broadcasted_iota(jnp.int32, (FARP, 2 * SPAN), 0)
    first = lax.axis_index("seq") * spt
    dqs, dks, dvs = [], [], []
    for s in range(T // SPAN):
        seq = i * nseq + s // spt
        far = t_row < (first + s % spt)
        rows = slice(s * SPAN, (s + 1) * SPAN)
        dq_p, dk_p, dv_p, fk, fv = [], [], [], [], []
        for p in range(D // 128):
            ln = slice(p * 128, (p + 1) * 128)
            qbd = pair_diag(q_ref[rows, ln])
            dbd = pair_diag(da_ref[rows, ln])
            ke = jnp.concatenate([k_ref[rows, ln], ks_ref[seq, :, ln]], axis=0)
            ve = jnp.concatenate([v_ref[rows, ln], vs_ref[seq, :, ln]], axis=0)
            sc = dot(ke, qbd, 1, 1)
            dp = dot(ve, dbd, 1, 1)
            lse = jnp.concatenate([lse_ref[2 * p : 2 * p + 1, rows], lse_ref[2 * p + 1 : 2 * p + 2, rows]], axis=1)
            pn = jnp.where(causal, jnp.exp(sc[:SPAN] - lse), 0.0)
            pf = jnp.where(far, jnp.exp(sc[SPAN:] - lse), 0.0)
            dpn, dpf = dp[:SPAN], dp[SPAN:]
            delta = jnp.sum(pn * dpn, axis=0, keepdims=True) + jnp.sum(pf * dpf, axis=0, keepdims=True)
            ds = jnp.concatenate([(pn * (dpn - delta)).astype(bf), (pf * (dpf - delta)).astype(bf)], axis=0)
            pb = jnp.concatenate([pn.astype(bf), pf.astype(bf)], axis=0)
            dv = dot(pb, dbd)
            dk = dot(ds, qbd)
            dq = dot(ke, ds, 0, 0)
            dq = jnp.concatenate([dq[:HD, :SPAN], dq[HD:, SPAN:]], axis=0) * (HD**-0.5)
            dq_p.append(dq.astype(bf).T)
            dk_p.append(dk[:SPAN].astype(bf))
            dv_p.append(dv[:SPAN].astype(bf))
            fk.append(dk[SPAN : SPAN + spans_all])
            fv.append(dv[SPAN : SPAN + spans_all])
        dqs.append(jnp.concatenate(dq_p, axis=1))
        dks.append(jnp.concatenate(dk_p, axis=1))
        dvs.append(jnp.concatenate(dv_p, axis=1))
        fk, fv = jnp.concatenate(fk, axis=1), jnp.concatenate(fv, axis=1)
        if s % spt == 0:
            sum_k, sum_v = fk, fv
        else:
            sum_k, sum_v = sum_k + fk, sum_v + fv
        if s % spt == spt - 1:
            for t in range(spans_all):
                dks_ref[t, pl.ds(seq, 1), :] = sum_k[t : t + 1]
                dvs_ref[t, pl.ds(seq, 1), :] = sum_v[t : t + 1]
    dq, dk, dv = (jnp.concatenate(parts, axis=0) for parts in (dqs, dks, dvs))
    xt = xn.T
    aq[...] += dot(xt, dq)
    ak[...] += dot(xt, dk)
    av[...] += dot(xt, dv)
    dxn = dot(dq, wq_ref[...], 1, 1) + dot(dk, wk_ref[...], 1, 1) + dot(dv, wv_ref[...], 1, 1)
    dxn_ref[...] = dxn.astype(bf)
    aga[...] += jnp.sum((dxn * xr).reshape(T // 8, 8, D), axis=0)

    @pl.when(i == n - 1)
    def _():
        rd = D // ndev
        mean = mean_ref[...].reshape(spans_all * seqs, D)
        mb = (mean * ga).astype(bf)
        fk = dks_ref[...].reshape(spans_all * seqs, D).astype(bf)
        fv = dvs_ref[...].reshape(spans_all * seqs, D).astype(bf)
        far = dot(fk, wk_ref[...], 1, 1) + dot(fv, wv_ref[...], 1, 1)
        gain = aga[...] + jnp.sum((far * mean).reshape(spans_all * seqs // 8, 8, D), axis=0)
        gsum_ref[:, :rd, :] = aq[...].reshape(ndev, rd, D).astype(bf)
        gsum_ref[:, rd : 2 * rd, :] = (ak[...] + dot(mb, fk, 0, 0)).reshape(ndev, rd, D).astype(bf)
        gsum_ref[:, 2 * rd : 3 * rd, :] = (av[...] + dot(mb, fv, 0, 0)).reshape(ndev, rd, D).astype(bf)
        gsum_ref[:, 3 * rd :, :] = spread_gain(gain, ndev, rd).astype(bf)


def attend_backward_call(slots, block, ndev, x, q, k, v, da, lse, mean, ks, vs, wq, wk, wv, ga):
    n_tok, D = x.shape
    tok = pl.BlockSpec((block, D), lambda i: (i, 0))
    rows = D // ndev * 3 + 16
    return pl.pallas_call(
        partial(attend_backward_kernel, slots, ndev),
        grid=(n_tok // block,),
        in_specs=[tok] * 5
        + [pl.BlockSpec((H, block), lambda i: (0, i)), full(mean.shape), full(ks.shape), full(vs.shape)]
        + [full((D, D))] * 3
        + [full((1, D))],
        out_specs=[tok, full((ndev, rows, D)), full(mean.shape), full(mean.shape)],
        out_shape=[sds((n_tok, D), bf), sds((ndev, rows, D), bf), sds(mean.shape, f32), sds(mean.shape, f32)],
        scratch_shapes=[pltpu.VMEM((D, D), f32)] * 3 + [pltpu.VMEM((8, D), f32)],
        compiler_params=pltpu.CompilerParams(
            vmem_limit_bytes=VMEM_LIMIT, dimension_semantics=("arbitrary",)
        ),
    )(x, q, k, v, da, lse, mean, ks, vs, wq, wk, wv, ga)


def grad_input_kernel(slots, x_ref, dxn_ref, dmid_ref, own_k_ref, own_v_ref, wk_ref, wv_ref, ga_ref, out_ref, far_ref):
    T, D = x_ref.shape
    spt, seqs, _ = own_k_ref.shape
    i = pl.program_id(0)
    nseq = T // slots

    @pl.when(i == 0)
    def _():
        fk = own_k_ref[...].reshape(spt * seqs, D)
        fv = own_v_ref[...].reshape(spt * seqs, D)
        far = (dot(fk, wk_ref[...], 1, 1) + dot(fv, wv_ref[...], 1, 1)) * (1.0 / SPAN)
        far_ref[...] = far.reshape(spt, seqs, D)

    ga = ga_ref[...]
    x = x_ref[...].astype(f32)
    r = lax.rsqrt(jnp.mean(x * x, axis=1, keepdims=True) + EPS)
    xr = x * r
    dxn = dxn_ref[...].astype(f32)
    parts = []
    for s in range(T // SPAN):
        far = far_ref[s % spt, pl.ds(i * nseq + s // spt, 1), :]
        parts.append(dxn[s * SPAN : (s + 1) * SPAN] + far)
    gd = jnp.concatenate(parts, axis=0) * ga
    coef = jnp.mean(gd * xr, axis=1, keepdims=True)
    out_ref[...] = dmid_ref[...].astype(f32) + r * (gd - xr * coef)


def grad_input_call(slots, block, x, dxn, dmid, own_k, own_v, wk, wv, ga):
    n_tok, D = x.shape
    tok = pl.BlockSpec((block, D), lambda i: (i, 0))
    return pl.pallas_call(
        partial(grad_input_kernel, slots),
        grid=(n_tok // block,),
        in_specs=[tok] * 3 + [full(own_k.shape)] * 2 + [full((D, D))] * 2 + [full((1, D))],
        out_specs=tok,
        out_shape=sds((n_tok, D), f32),
        scratch_shapes=[pltpu.VMEM(own_k.shape, f32)],
        compiler_params=pltpu.CompilerParams(
            vmem_limit_bytes=VMEM_LIMIT, dimension_semantics=("arbitrary",)
        ),
    )(x, dxn, dmid, own_k, own_v, wk, wv, ga)


def gains_kernel(rows, ndev, tiles_ref, ga_ref, gm_ref):
    tiles = tiles_ref[:, :128]
    ga_ref[...] = gain_row(tiles, 0, ndev, rows)
    gm_ref[...] = gain_row(tiles, 1, ndev, rows)


def body(dims, inputs, lengths, cotangent, w_query, w_key, w_value, w_out, w_up, w_down, gain_attn, gain_mlp):
    seqs, slots, D = inputs.shape
    nz, nx, ny, nc = dims
    ndev = nz * nx * ny * nc
    FF = w_up.shape[1]
    rd, rf = w_query.shape[0], w_down.shape[0]
    n_tok = seqs * slots
    block = 512
    x = inputs.reshape(n_tok, D)
    cot = cotangent.reshape(n_tok, D)
    weights = (w_query, w_key, w_value, w_out, w_up, w_down)
    gains = jnp.zeros((8, 256), f32)
    gains = gains.at[0, :rd].set(gain_attn.astype(f32)).at[1, :rd].set(gain_mlp.astype(f32))
    everyone = ("dp", "seq")
    near = rd % 16 == 0
    if near:
        *wholes, tiles, mean = gather_call(dims, slots, block, x, weights + (gains,))
    else:
        *wholes, tiles, mean = gather_call(dims, slots, block, x, (gains,))
        wholes = [lax.all_gather(w, everyone, axis=0, tiled=True) for w in weights]
    wq, wk, wv, wo, wu, wd = (w.reshape(-1, w.shape[-1]) for w in wholes)
    ga, gm = pl.pallas_call(
        partial(gains_kernel, rd, ndev), out_shape=[sds((1, D), f32)] * 2
    )(tiles.reshape(ndev * 8, 256))
    q, k, v, att, lse, ks, vs = attend_forward_call(slots, block, x, mean, wq, wk, wv, ga)
    pack = ndev if near else 32
    output, datt, dmid, sums_m = mlp_call(512, slots, block, pack, lengths, x, att, cot, wo, wu, wd, gm)
    dxn, sums_a, dks, dvs = attend_backward_call(slots, block, pack, x, q, k, v, datt, lse, mean, ks, vs, wq, wk, wv, ga)
    device = lax.axis_index("dp") * (ny * nc) + lax.axis_index("seq")
    if near:
        sums, own_k, own_v = scatter_call(dims, slots, jnp.concatenate([sums_m, sums_a], axis=1), dks, dvs)
        last = rd * (FF // D + 1) + rf
        g_out = sums[:rd]
        g_up = jnp.concatenate([sums[rd * (j + 1) : rd * (j + 2)] for j in range(FF // D)], axis=1)
        g_down = sums[rd * (FF // D + 1) : last]
        g_gm = lax.dynamic_slice(sums[last], (device * rd,), (rd,))
        rest = sums[last + 16 :]
        g_q, g_k, g_v = rest[:rd], rest[rd : 2 * rd], rest[2 * rd : 3 * rd]
        g_ga = lax.dynamic_slice(rest[3 * rd], (device * rd,), (rd,))
    else:
        pd, pf = D // pack, FF // pack
        last = pd * (FF // D + 1) + pf

        def scattered(a):
            return lax.psum_scatter(a.astype(f32), everyone, scatter_dimension=0, tiled=True)

        g_out = scattered(sums_m[:, :pd].reshape(D, D))
        g_up = scattered(
            jnp.concatenate([sums_m[:, pd * (j + 1) : pd * (j + 2)].reshape(D, D) for j in range(FF // D)], axis=1)
        )
        g_down = scattered(sums_m[:, pd * (FF // D + 1) : last].reshape(FF, D))
        g_gm = scattered(jnp.sum(sums_m[:, last].astype(f32), axis=0))
        g_q, g_k, g_v = (scattered(sums_a[:, j * pd : (j + 1) * pd].reshape(D, D)) for j in range(3))
        g_ga = scattered(jnp.sum(sums_a[:, 3 * pd].astype(f32), axis=0))
        own_k, own_v = (
            lax.psum_scatter(d.astype(bf), "seq", scatter_dimension=0, tiled=True) for d in (dks, dvs)
        )
    grad_input = grad_input_call(slots, block, x, dxn, dmid, own_k, own_v, wk, wv, ga)
    return (
        output.reshape(inputs.shape), grad_input.reshape(inputs.shape),
        g_q, g_k, g_v, g_out, g_up, g_down, g_ga, g_gm,
    )


def solution(mesh):
    dp, seq = mesh.shape["dp"], mesh.shape["seq"]
    nx = max(d for d in range(1, dp + 1) if dp % d == 0 and d * d <= dp)
    nc = 2 if seq % 2 == 0 else 1
    dims = (dp // nx, nx, seq // nc, nc)
    rows, vec = P(("dp", "seq"), None), P(("dp", "seq"))
    tokens = P("dp", "seq", None)
    return jax.shard_map(
        partial(body, dims),
        mesh=mesh,
        in_specs=(tokens, P("dp"), tokens) + (rows,) * 6 + (vec,) * 2,
        out_specs=(tokens, tokens) + (rows,) * 6 + (vec,) * 2,
        check_vma=False,
    )
```

time: 1930 us -> 417 us (0.22)
  waiting for transfers between devices: 625 us -> 0 us
  matrix products: 462 us -> 0 us
  local copies, waits for them, and re-layouts: 441 us -> 5.12 us
  Pallas kernels: 0 us -> 400 us
  blocking collectives: 248 us -> 0 us
  other arithmetic: 115 us -> 8.93 us
    reduce_scatter x8 -> x0, waiting for transfers between devices: 623 us -> none  [the longest x1 140 us: body(): lax.psum_scatter(d_up, ('dp', 'seq'), scatter_dimension=0, tiled=True)]
    dot_general x186 -> x0, matrix products: 462 us -> none  [the longest x1 46.7 us: body(): jnp.einsum('nd,fd->nf', grad_branch, full_down, preferred_element_type=jn...]
    pallas_call x0 -> x7, Pallas kernels: none -> 400 us  [the longest x1 114 us: mlp_call(): pl.pallas_call(partial(mlp_kernel, chunk, slots, ndev), grid=(n_tok // bl...]
    dynamic_update_slice x144 -> x0, local copies, waits for them, and re-layouts: 221 us -> none  [the longest x108 197 us: body(): lax.map(partial(attend_backward, first_span), (query_b, key_b, value_b, k...]
    all_gather x6 -> x0, blocking collectives: 169 us -> none  [the longest x1 42.3 us: body(): lax.all_gather(w_value, ('dp', 'seq'), axis=0, tiled=True)]
    dynamic_slice x120 -> x1, local copies, waits for them, and re-layouts: 120 us -> 0.58 us  [body(): g_gm = lax.dynamic_slice(sums[last], (device * rd,), (rd,))]
    unnamed x2 -> x0, blocking collectives: 79 us -> none
    convert_element_type x35 -> x0, other arithmetic: 55.5 us -> none  [the longest x2 15.5 us: body(): d_value = (d_value.reshape(seq_count, spans_dev, SPAN, model_width) + own...]
  transfers between devices with their start and end apart: 10 -> 0, of which waited for: 5 -> 0; matrix products, arithmetic and copies ran while one was open for 23% -> 0% of each run, Pallas kernels for 0% -> 0%
where the time goes in v1:
time: 417 us; the launch traced here: 414 us
  Pallas kernels  400 us (96%)
  other arithmetic  8.93 us (2%)
  local copies, waits for them, and re-layouts  5.12 us (1%)
    pallas_call x1, Pallas kernels, mlp_call(): pl.pallas_call(partial(mlp_kernel, chunk, slots, ndev), grid=(n_tok // bl...  114 us
    pallas_call x1, Pallas kernels, attend_backward_call(): pl.pallas_call(partial(attend_backward_kernel, slots, ndev), grid=(n_tok...  72.1 us
    pallas_call x1, Pallas kernels, attend_forward_call(): pl.pallas_call(partial(attend_forward_kernel, slots), grid=(n_tok // bloc...  68 us
    pallas_call x1, Pallas kernels, scatter_call(): pl.pallas_call(partial(scatter_kernel, dims, spans_dev), in_specs=[vm] *...  64.1 us
    pallas_call x1, Pallas kernels, gather_call(): pl.pallas_call(partial(gather_kernel, dims, spans_dev, n_w), grid=(n_tok...  62 us
    pallas_call x1, Pallas kernels, grad_input_call(): pl.pallas_call(partial(grad_input_kernel, slots), grid=(n_tok // block,),...  17.5 us

profile of v1, /device:TPU:0, one launch (start us, length us, event | category | flops | bytes accessed | tf_op | source)
XLA Modules:
  0.0 414.4 jit_solution(2138197418752897605)
XLA Ops:
  0.6 0.7 pad_convert_fusion
  1.3 0.7 bitcast_convert_fusion
  2.0 0.1 scatter.14.refs_7_
  2.1 0.0 copy-start
  2.1 0.6 copy-done
  2.7 62.0 %shard_map.186 = (bf16[4,2,2,2,16,512]{5,4,3,2,1,0:T(8,128)(2,1)}, bf16[4,2,2,2,16,512]{5,4,3,2,1,0:T(8,128)(2,1)}, bf16[4,2,2,2,16,512]{5,4,3,2,1,0:T(8,128)(2,...) custom-call(bf16[6144,512]{1,0:T(8,128)(2,1)} %bitcast.20, ...), custom_call_target="tpu_custom_call" | custom-call | tf_op jit(solution)/shard_map/pallas_call | solution.py:219
  64.7 1.8 shard_map.187
  66.5 68.0 %shard_map.188 = (bf16[6144,512]{1,0:T(8,128)(2,1)}, bf16[6144,512]{1,0:T(8,128)(2,1)}, bf16[6144,512]{1,0:T(8,128)(2,1)}, bf16[6144,512]{1,0:T(8,128)(2,1)}, f3...) custom-call(bf16[6144,512]{1,0:T(8,128)(2,1)} %bitcast.21, ...), custom_call_target="tpu_custom_call" | custom-call | tf_op jit(solution)/shard_map/pallas_call | solution.py:417
  134.5 114.3 %shard_map.189 = (bf16[6144,512]{1,0:T(8,128)(2,1)}, bf16[6144,512]{1,0:T(8,128)(2,1)}, bf16[6144,512]{1,0:T(8,128)(2,1)}, bf16[32,160,512]{2,1,0:T(8,128)(2,1)}) custom-call(s32[24]{0:T(128)} %len_ref.1, bf16[6144,512]{1,0:T(8,128)(2,1)} %bitcast.22, bf16[6144,512]{1,0:T(8,128)(2,1)} %get-tuple-element.68.att_ref, bf16[6144,512]{1,0:T(8,128)(2,1)} %bitcast.27, ...), custom_call_target="tpu_custom_call" | custom-call | tf_op jit(solution)/shard_map/pallas_call | solution.py:510
  248.8 72.1 %shard_map.190 = (bf16[6144,512]{1,0:T(8,128)(2,1)}, bf16[32,64,512]{2,1,0:T(8,128)(2,1)}, f32[8,24,512]{2,1,0:T(8,128)}, f32[8,24,512]{2,1,0:T(8,128)}) custom-call(bf16[6144,512]{1,0:T(8,128)(2,1)} %bitcast.23, bf16[6144,512]{1,0:T(8,128)(2,1)} %get-tuple-element.74.q_ref, bf16[6144,512]{1,0:T(8,128)(2,1)} %get-tuple-element.75.k_ref, ...), custom_call_target="tpu_custom_call" | custom-call | tf_op jit(solution)/shard_map/pallas_call | solution.py:615
  320.8 6.9 %pad_maximum_fusion = bf16[32,224,512]{2,1,0:T(8,128)(2,1)} fusion(bf16[32,64,512]{2,1,0:T(8,128)(2,1)} %get-tuple-element.84, bf16[32,160,512]{2,1,0:T(8,128)(2,1)} %get-tuple-element.83), kind=kLoop, calls=%fused_computation | loop fusion | flops 14680064 | bytes 14680064 | tf_op jit(solution)/shard_map/concatenate | solution.py:710
  327.8 64.1 %shard_map.191 = (f32[224,512]{1,0:T(8,128)}, bf16[2,24,512]{2,1,0:T(8,128)(2,1)}, bf16[2,24,512]{2,1,0:T(8,128)(2,1)}) custom-call(bf16[4,2,2,2,224,512]{5,4,3,2,1,0:T(8,128)(2,1)} %bitcast.25, f32[8,24,512]{2,1,0:T(8,128)} %get-tuple-element.85.dks_ref, f32[8,24,512]{2,1,0:T(8,128)} %get-tuple-element.86.dvs_ref), custom_call_target="tpu_custom_call" | custom-call | tf_op jit(solution)/shard_map/pallas_call | solution.py:335
  391.8 0.7 fusion
  392.6 0.6 dynamic-slice_bitcast_fusion
  393.2 1.5 fusion.1
  394.7 0.7 pad_maximum_fusion.1
  395.4 17.5 %shard_map.192 = f32[6144,512]{1,0:T(8,128)} custom-call(bf16[6144,512]{1,0:T(8,128)(2,1)} %bitcast.24, bf16[6144,512]{1,0:T(8,128)(2,1)} %get-tuple-element.81.dxn_ref, bf16[6144,512]{1,0:T(8,128)(2,1)} %get-tuple-element.82.dmid_ref, bf16[2,24,512]{2,1,0:T(8,128)(2,1)} %get-tuple-element.87.own_k_ref, bf16[2,24,512]{2,1,0:T(8,128)(2,1)} %get-tuple-element.88.own_v_ref, ...), custom_call_target="tpu_custom_call" | custom-call | tf_op jit(solution)/shard_map/pallas_call | solution.py:661
  412.8 1.6 slice.81
Async XLA Ops:
  2.1 0.6 copy-start

commit v2 on v1

v2 whole, which is shorter than its diff:
```python
from functools import partial

import jax
import jax.numpy as jnp
from jax import lax
from jax.experimental import pallas as pl
from jax.experimental.pallas import tpu as pltpu
from jax.sharding import PartitionSpec as P

H = 8
HD = 64
SPAN = 128
EPS = 1e-06
K0 = 0.7978845608028654
K1 = 0.044715
FARP = 16
f32 = jnp.float32
bf = jnp.bfloat16
MESH = pl.DeviceIdType.MESH
VMEM_LIMIT = 62 << 20


def dot(a, b, ca=1, cb=0):
    return lax.dot_general(a, b, (((ca,), (cb,)), ((), ())), preferred_element_type=f32)


def sds(shape, dtype):
    return jax.ShapeDtypeStruct(shape, dtype)


def full(shape):
    return pl.BlockSpec(shape, lambda i: (0,) * len(shape), pipeline_mode=pl.Buffered(1))


def pair_diag(a):
    lane = lax.broadcasted_iota(jnp.int32, a.shape, 1)
    zero = jnp.zeros_like(a)
    return jnp.concatenate([jnp.where(lane < HD, a, zero), jnp.where(lane >= HD, a, zero)], axis=0)


def causal_mask():
    j = lax.broadcasted_iota(jnp.int32, (SPAN, 2 * SPAN), 0)
    i = lax.broadcasted_iota(jnp.int32, (SPAN, 2 * SPAN), 1)
    return j <= jnp.where(i >= SPAN, i - SPAN, i)


def gain_row(tiles, which, ndev, rows):
    width = ndev * rows
    r = lax.broadcasted_iota(jnp.int32, (ndev * 8, 128), 0)
    l = lax.broadcasted_iota(jnp.int32, (ndev * 8, 128), 1)
    keep = jnp.where((r % 8 == which) & (l < rows), tiles, 0.0).astype(bf)
    a = lax.broadcasted_iota(jnp.int32, (128, width), 0)
    b = lax.broadcasted_iota(jnp.int32, (128, width), 1)
    spread = dot(keep, jnp.where(b % rows == a, 1.0, 0.0).astype(bf))
    d = lax.broadcasted_iota(jnp.int32, (ndev * 8, width), 0)
    c = lax.broadcasted_iota(jnp.int32, (ndev * 8, width), 1)
    return jnp.sum(jnp.where(d // 8 == c // rows, spread, 0.0), axis=0, keepdims=True)


class Place:
    def __init__(self, dims):
        self.nz, self.nx, self.ny, self.nc = dims
        dp, seq = lax.axis_index("dp"), lax.axis_index("seq")
        self.z, self.x = dp // self.nx, dp % self.nx
        self.y, self.c = seq // self.nc, seq % self.nc

    def at(self, z=None, x=None, y=None, c=None):
        z = self.z if z is None else z
        x = self.x if x is None else x
        y = self.y if y is None else y
        c = self.c if c is None else c
        return (z * self.nx + x, y * self.nc + c)

    def line(self, axis):
        return getattr(self, axis), getattr(self, "n" + axis)

    def partners(self, axis):
        me, n = self.line(axis)
        return [(o, (me + o) % n, (me + n - o) % n) for o in range(1, n)]

    def greet(self, others):
        barrier = pltpu.get_barrier_semaphore()
        for other in others:
            pl.semaphore_signal(barrier, inc=1, device_id=other, device_id_type=MESH)
        pl.semaphore_wait(barrier, len(others))

    def others(self):
        return [self.at(**{a: to}) for a in ("z", "x", "y", "c") for _, to, _ in self.partners(a)]


class Copies:
    def __init__(self, send_sem, recv_sem):
        self.send_sem, self.recv_sem, self.used = send_sem, recv_sem, 0

    def make(self, src, dst, landed, device):
        k = self.used
        self.used += 1
        out = pltpu.make_async_remote_copy(
            src_ref=src, dst_ref=dst, send_sem=self.send_sem.at[k], recv_sem=self.recv_sem.at[k],
            device_id=device, device_id_type=MESH,
        )
        into = pltpu.make_async_remote_copy(
            src_ref=src, dst_ref=landed, send_sem=self.send_sem.at[k], recv_sem=self.recv_sem.at[k],
            device_id=device, device_id_type=MESH,
        )
        return out, into


def start(copies):
    for out, _ in copies:
        out.start()


def finish(copies):
    for out, into in copies:
        out.wait_send()
        into.wait_recv()


def halves(ref):
    n = ref.shape[-1] // 2
    return pl.ds(0, n), pl.ds(n, n)


def gather_phases(pc, cp, pieces, wholes):
    z, x, y, c = pc.z, pc.x, pc.y, pc.c
    first, second, third, last = [], [], [], []
    for piece, whole in zip(pieces, wholes):
        for _, to, fr in pc.partners("z"):
            first.append(cp.make(piece, whole.at[z, x, y, c], whole.at[fr, x, y, c], pc.at(z=to)))
    for whole in wholes:
        a, b = halves(whole)
        for _, to, fr in pc.partners("x"):
            v = whole.at[:, x, y, c, :, a]
            second.append(cp.make(v, v, whole.at[:, fr, y, c, :, a], pc.at(x=to)))
        for _, to, fr in pc.partners("y"):
            v = whole.at[:, x, y, c, :, b]
            second.append(cp.make(v, v, whole.at[:, x, fr, c, :, b], pc.at(y=to)))
    for whole in wholes:
        a, b = halves(whole)
        for _, to, fr in pc.partners("y"):
            v = whole.at[:, :, y, c, :, a]
            third.append(cp.make(v, v, whole.at[:, :, fr, c, :, a], pc.at(y=to)))
        for _, to, fr in pc.partners("x"):
            v = whole.at[:, x, :, c, :, b]
            third.append(cp.make(v, v, whole.at[:, fr, :, c, :, b], pc.at(x=to)))
    for whole in wholes:
        for _, to, fr in pc.partners("c"):
            v = whole.at[:, :, :, c]
            last.append(cp.make(v, v, whole.at[:, :, :, fr], pc.at(c=to)))
    return first, second, third, last


def front_kernel(dims, slots, n_first, n_later, *refs):
    near = n_first > 0
    refs = list(refs)

    def take(n):
        out = refs[:n]
        del refs[:n]
        return out

    (x_ref,) = take(1)
    pieces = take(n_first + n_later + 1 if near else 1)
    w_in = [] if near else take(3)
    q_ref, k_ref, v_ref, att_ref, lse_ref, ks_ref, vs_ref, mean_ref, ga_ref, gm_ref = take(10)
    first_out = take(n_first)
    later = take(n_later)
    w_refs = take(3) if near else w_in
    tiles_ref, own_mean, all_mean, tmp_ref, local_sem, send_sem, recv_sem = take(7)
    T, D = x_ref.shape
    spt, nseq = slots // SPAN, T // slots
    pc = Place(dims)
    cp = Copies(send_sem, recv_sem)
    seq, dp = lax.axis_index("seq"), lax.axis_index("dp")
    seqn = pc.ny * pc.nc
    spans_all, seqs = spt * seqn, all_mean.shape[1]
    ndev = pc.nz * pc.nx * seqn
    rd = D // ndev
    chunks = []
    own = []
    if near:
        wholes = w_refs + [tiles_ref]
        firsts = pieces[:n_first] + pieces[-1:]
        groups = [(firsts, wholes)] + [([p], [w]) for p, w in zip(pieces[n_first:-1], later)]
    else:
        groups = [(pieces, [tiles_ref])]
    for sources, targets in groups:
        chunks.append(gather_phases(pc, cp, sources, targets))
        mine = []
        for source, target in zip(sources, targets):
            mine.append(
                pltpu.make_async_copy(
                    source, target.at[pc.z, pc.x, pc.y, pc.c], local_sem.at[sum(map(len, own)) + len(mine)]
                )
            )
        own.append(mine)
    means = []
    for o in range(1, seqn):
        to, fr = (seq + o) % seqn, (seq + seqn - o) % seqn
        v = all_mean.at[pl.ds(seq * spt, spt)]
        means.append(cp.make(v, v, all_mean.at[pl.ds(fr * spt, spt)], (dp, to)))
    i, n = pl.program_id(0), pl.num_programs(0) // 2

    @pl.when(i == 0)
    def _():
        seq_peers = [(dp, (seq + o) % seqn) for o in range(1, seqn)]
        zx = [pc.at(**{a: to}) for a in ("z", "x") for _, to, _ in pc.partners(a)]
        pc.greet(zx + seq_peers)
        start(chunks[0][0])
        for mine in own:
            for copy in mine:
                copy.start()

    x = x_ref[...].astype(f32)
    r = lax.rsqrt(jnp.mean(x * x, axis=1, keepdims=True) + EPS)
    xr = x * r

    @pl.when(i < n)
    def _():
        for s in range(T // SPAN):
            row = jnp.sum(xr[s * SPAN : (s + 1) * SPAN], axis=0, keepdims=True) * (1.0 / SPAN)
            own_mean[s % spt, pl.ds(i * nseq + s // spt, 1), :] = row

    @pl.when(i == n - 1)
    def _():
        for mine in own:
            for copy in mine:
                copy.wait()
        c0 = chunks[0]
        finish(c0[0])
        start(c0[1])
        all_mean[pl.ds(seq * spt, spt)] = own_mean[...].astype(bf)
        start(means)
        if near:
            start(chunks[1][0])
        finish(c0[1])
        start(c0[2])
        finish(means)
        mean_ref[...] = all_mean[...]
        finish(c0[2])
        start(c0[3])
        finish(c0[3])
        for w_ref, out in zip(w_refs, first_out):
            out[...] = w_ref[...]
        tiles = tiles_ref[...].reshape(ndev * 8, tiles_ref.shape[-1])[:, :128]
        ga_ref[...] = gain_row(tiles, 0, ndev, rd)
        gm_ref[...] = gain_row(tiles, 1, ndev, rd)
        mb = (all_mean[...].astype(f32).reshape(spans_all * seqs, D) * ga_ref[...]).astype(bf)
        for w_ref, out in ((w_refs[1], ks_ref), (w_refs[2], vs_ref)):
            sums = dot(mb, w_ref[...].reshape(D, D))
            tmp_ref[...] = jnp.zeros_like(tmp_ref)
            for t in range(spans_all):
                tmp_ref[:, t, :] = sums[t * seqs : (t + 1) * seqs]
            out[...] = tmp_ref[...].astype(bf)

    if near:
        up, down, last = chunks[1], chunks[2], chunks[3]
        plan = [
            (0, [up[0]], [up[1], down[0], last[0]]),
            (2, [up[1]], [up[2]]),
            (4, [up[2], down[0], last[0]], [up[3], down[1]]),
            (6, [up[3], down[1]], [down[2]]),
            (8, [down[2]], [down[3], last[1]]),
            (9, [last[1]], [last[2]]),
            (10, [last[2]], [last[3]]),
        ]
        for at, ends, begins in plan:

            @pl.when(i == n + at)
            def _(ends=ends, begins=begins):
                for c in ends:
                    finish(c)
                for c in begins:
                    start(c)

    @pl.when(i >= n)
    def _():
        j = i - n
        xn = (xr * ga_ref[...]).astype(bf)
        q_ref[...] = (dot(xn, w_refs[0][...].reshape(D, D)).astype(bf) * (HD**-0.5)).astype(bf)
        k_ref[...] = dot(xn, w_refs[1][...].reshape(D, D)).astype(bf)
        v_ref[...] = dot(xn, w_refs[2][...].reshape(D, D)).astype(bf)
        attend_forward(slots, j, seq, q_ref, k_ref, v_ref, ks_ref, vs_ref, att_ref, lse_ref)

    if near:

        @pl.when(i == 2 * n - 1)
        def _():
            finish(chunks[2][3])
            finish(chunks[3][3])


def attend_forward(slots, j, seq, q_ref, k_ref, v_ref, ks_ref, vs_ref, att_ref, lse_ref):
    T, D = q_ref.shape
    spt, nseq = slots // SPAN, T // slots
    causal = causal_mask()
    t_row = lax.broadcasted_iota(jnp.int32, (FARP, 2 * SPAN), 0)

    def where(u):
        s, p = u
        return slice(s * SPAN, (s + 1) * SPAN), slice(p * 128, (p + 1) * 128), j * nseq + s // spt

    def scores(u):
        rows, ln, sq = where(u)
        ke = jnp.concatenate([k_ref[rows, ln], ks_ref[sq, :, ln]], axis=0)
        return dot(ke, pair_diag(q_ref[rows, ln]), 1, 1)

    def weigh(u, sc):
        far = t_row < (seq * spt + u[0] % spt)
        sn = jnp.where(causal, sc[:SPAN], -1e30)
        sf = jnp.where(far, sc[SPAN:], -1e30)
        m = jnp.maximum(jnp.max(sn, axis=0, keepdims=True), jnp.max(sf, axis=0, keepdims=True))
        en = jnp.exp(sn - m)
        ef = jnp.exp(sf - m)
        l = jnp.sum(en, axis=0, keepdims=True) + jnp.sum(ef, axis=0, keepdims=True)
        return en.astype(bf), ef.astype(bf), m, l

    def combine(u, en, ef, m, l):
        rows, ln, sq = where(u)
        p = u[1]
        at = (dot(v_ref[rows, ln], en, 0, 0) + dot(vs_ref[sq, :, ln], ef, 0, 0)) * (1.0 / l)
        att_ref[rows, ln] = jnp.concatenate([at[:HD, :SPAN], at[HD:, SPAN:]], axis=0).astype(bf).T
        total = m + jnp.log(l)
        lse_ref[2 * p : 2 * p + 1, rows] = total[:, :SPAN]
        lse_ref[2 * p + 1 : 2 * p + 2, rows] = total[:, SPAN:]

    units = [(s, p) for s in range(T // SPAN) for p in range(D // 128)]
    staged(units, scores, weigh, combine)


def staged(units, first, second, third):
    a, b = {}, {}
    for t in range(len(units) + 2):
        if t < len(units):
            a[t] = first(units[t])
        if 0 <= t - 1 < len(units):
            b[t - 1] = second(units[t - 1], a.pop(t - 1))
        if 0 <= t - 2:
            third(units[t - 2], *b.pop(t - 2))


def front_call(dims, slots, block, x, w_first, w_later, gains, near):
    n_tok, D = x.shape
    seqs, spt = n_tok // slots, slots // SPAN
    nz, nx, ny, nc = dims
    n = n_tok // block
    spans_all = spt * ny * nc
    hbm = pl.BlockSpec(memory_space=pl.ANY)
    summ = (seqs, FARP, D)
    per_piece = (nz - 1) + 2 * (nx - 1) + 2 * (ny - 1) + (nc - 1)
    n_pieces = len(w_first) + len(w_later) + 1 if near else 1
    copies = n_pieces * per_piece + ny * nc - 1
    tok = pl.BlockSpec((block, D), lambda i: (jnp.maximum(i - n, 0), 0))
    args = [x] + (list(w_first) + list(w_later) if near else []) + [gains] + ([] if near else list(w_first))
    in_specs = [pl.BlockSpec((block, D), lambda i: (i % n, 0))] + [hbm] * n_pieces
    if not near:
        in_specs += [full(w.shape) for w in w_first]
    row = sds((1, D), f32)
    return pl.pallas_call(
        partial(front_kernel, dims, slots, len(w_first) if near else 0, len(w_later) if near else 0),
        grid=(2 * n,),
        in_specs=in_specs,
        out_specs=[tok] * 4
        + [pl.BlockSpec((H, block), lambda i: (0, jnp.maximum(i - n, 0))), full(summ), full(summ)]
        + [full((spans_all, seqs, D)), full((1, D)), full((1, D))]
        + ([full(dims + w.shape) for w in w_first] + [hbm] * len(w_later) if near else []),
        out_shape=[sds((n_tok, D), bf)] * 4
        + [sds((H, n_tok), f32), sds(summ, bf), sds(summ, bf), sds((spans_all, seqs, D), bf), row, row]
        + ([sds(dims + w.shape, w.dtype) for w in (*w_first, *w_later)] if near else []),
        scratch_shapes=([pltpu.VMEM(dims + w.shape, w.dtype) for w in w_first] if near else [])
        + [
            pltpu.VMEM(dims + gains.shape, f32),
            pltpu.VMEM((spt, seqs, D), f32),
            pltpu.VMEM((spans_all, seqs, D), bf),
            pltpu.VMEM(summ, f32),
            pltpu.SemaphoreType.DMA((n_pieces,)),
            pltpu.SemaphoreType.DMA((copies,)),
            pltpu.SemaphoreType.DMA((copies,)),
        ],
        compiler_params=pltpu.CompilerParams(
            vmem_limit_bytes=VMEM_LIMIT, collective_id=0, has_side_effects=True,
            dimension_semantics=("arbitrary",),
        ),
    )(*args)


def mlp_kernel(chunk, slots, ndev, len_ref, x_ref, att_ref, cot_ref, wo_ref, wu_ref, wd_ref, gm_ref,
               out_ref, datt_ref, dmid_ref, gsum_ref, adown, aup, aout):
    T, D = x_ref.shape
    FF = wu_ref.shape[1]
    i, n = pl.program_id(0), pl.num_programs(0)

    @pl.when(i == 0)
    def _():
        for acc in (adown, aup, aout):
            acc[...] = jnp.zeros_like(acc)

    att = att_ref[...]
    mid = x_ref[...].astype(f32) + dot(att, wo_ref[...])
    r = lax.rsqrt(jnp.mean(mid * mid, axis=1, keepdims=True) + EPS)
    gm = gm_ref[...]
    hn = (mid * r * gm).astype(bf)
    nseq = T // slots
    row = lax.broadcasted_iota(jnp.int32, (slots, 1), 0) + lax.axis_index("seq") * slots
    valid = jnp.concatenate(
        [jnp.where(row < len_ref[i * nseq + s], 1.0, 0.0) for s in range(nseq)], axis=0
    )
    g = cot_ref[...].astype(f32) * valid
    gb = g.astype(bf)
    gbt = gb.T
    hnt = hn.T
    y = jnp.zeros((T, D), f32)
    dhn = jnp.zeros((T, D), f32)
    cols = [slice(j * chunk, (j + 1) * chunk) for j in range(FF // chunk)]

    def products(sl):
        return dot(hn, wu_ref[:, sl]), dot(gb, wd_ref[sl, :], 1, 1)

    ready = products(cols[0])
    for j, sl in enumerate(cols):
        u, da = ready
        if j + 1 < len(cols):
            ready = products(cols[j + 1])
        h = 0.5 + 0.5 * jnp.tanh(u * (K0 + (K0 * K1) * (u * u)))
        act = (u * h).astype(bf)
        ub, hb = u.astype(bf), h.astype(bf)
        slope = hb + (ub * (bf(K0) + bf(3 * K0 * K1) * (ub * ub))) * ((hb + hb) * (bf(1.0) - hb))
        du = da.astype(bf) * slope
        y = y + dot(act, wd_ref[sl, :])
        dhn = dhn + dot(du, wu_ref[:, sl], 1, 1)
        adown[:, sl] += dot(gbt, act)
        aup[:, sl] += dot(hnt, du)
    out_ref[...] = ((mid + y) * valid).astype(bf)
    mr = mid * r
    gd = dhn * gm
    coef = jnp.mean(gd * mr, axis=1, keepdims=True)
    db = (g + r * (gd - mr * coef)).astype(bf)
    dmid_ref[...] = db
    aout[...] += dot(att, db, 0, 0)
    datt_ref[...] = dot(db, wo_ref[...], 1, 1).astype(bf)

    @pl.when(i == n - 1)
    def _():
        rd, rf = D // ndev, FF // ndev
        gsum_ref[:, :rd, :] = aout[...].reshape(ndev, rd, D).astype(bf)
        for j in range(FF // D):
            gsum_ref[:, rd * (j + 1) : rd * (j + 2), :] = (
                aup[:, j * D : (j + 1) * D].reshape(ndev, rd, D).astype(bf)
            )
            part = adown[:, j * D : (j + 1) * D].T.astype(bf)
            nd = D // rf
            gsum_ref[j * nd : (j + 1) * nd, rd * (FF // D + 1) : rd * (FF // D + 1) + rf, :] = part.reshape(
                nd, rf, D
            )


def mlp_call(chunk, slots, block, ndev, lens, x, att, cot, wo, wu, wd, gm):
    n_tok, D = x.shape
    FF = wu.shape[1]
    tok = pl.BlockSpec((block, D), lambda i: (i, 0))
    rows = D // ndev * (FF // D + 1) + FF // ndev
    return pl.pallas_call(
        partial(mlp_kernel, chunk, slots, ndev),
        grid=(n_tok // block,),
        in_specs=[pl.BlockSpec(memory_space=pltpu.SMEM), tok, tok, tok]
        + [full((D, D)), full((D, FF)), full((FF, D)), full((1, D))],
        out_specs=[tok, tok, tok, full((ndev, rows, D))],
        out_shape=[sds((n_tok, D), bf)] * 3 + [sds((ndev, rows, D), bf)],
        scratch_shapes=[pltpu.VMEM((D, FF), f32), pltpu.VMEM((D, FF), f32), pltpu.VMEM((D, D), f32)],
        compiler_params=pltpu.CompilerParams(
            vmem_limit_bytes=VMEM_LIMIT, dimension_semantics=("arbitrary",)
        ),
    )(lens, x, att, cot, wo, wu, wd, gm)


class Scatter:
    @staticmethod
    def scratch(dims, rows, width):
        nz, nx, ny, nc = dims
        half, most = width // 2, max(nx, ny)
        return [
            pltpu.VMEM((nc - 1, nz, nx, ny, rows, width), bf),
            pltpu.VMEM((nz, nx, ny, rows, width), bf),
            pltpu.VMEM((nx - 1, nz, ny, rows, half), bf),
            pltpu.VMEM((ny - 1, nz, nx, rows, half), bf),
            pltpu.VMEM((2, nz, most, rows, half), bf),
            pltpu.VMEM((ny - 1, nz, rows, half), bf),
            pltpu.VMEM((nx - 1, nz, rows, half), bf),
            pltpu.VMEM((nz, rows, width), bf),
            pltpu.VMEM((nz - 1, rows, width), bf),
        ]

    @staticmethod
    def copies(dims):
        nz, nx, ny, nc = dims
        return (nc - 1) + 2 * (nx - 1) + 2 * (ny - 1) + (nz - 1)

    def __init__(self, pc, cp, g, mine, out, scratch):
        self.pc, self.mine, self.out, self.bufs = pc, mine, out, scratch
        got1, held1, got2a, got2b, held2, got3a, got3b, held3, got4 = scratch
        a, b = halves(g)
        self.one = [
            cp.make(g.at[:, :, :, to], got1.at[o - 1], got1.at[o - 1], pc.at(c=to))
            for o, to, _ in pc.partners("c")
        ]
        self.two = [
            cp.make(held1.at[:, to, :, :, a], got2a.at[o - 1], got2a.at[o - 1], pc.at(x=to))
            for o, to, _ in pc.partners("x")
        ] + [
            cp.make(held1.at[:, :, to, :, b], got2b.at[o - 1], got2b.at[o - 1], pc.at(y=to))
            for o, to, _ in pc.partners("y")
        ]
        self.three = [
            cp.make(held2.at[0, :, to], got3a.at[o - 1], got3a.at[o - 1], pc.at(y=to))
            for o, to, _ in pc.partners("y")
        ] + [
            cp.make(held2.at[1, :, to], got3b.at[o - 1], got3b.at[o - 1], pc.at(x=to))
            for o, to, _ in pc.partners("x")
        ]
        self.four = [
            cp.make(held3.at[to], got4.at[o - 1], got4.at[o - 1], pc.at(z=to)) for o, to, _ in pc.partners("z")
        ]

    @staticmethod
    def total(acc, got, n):
        acc = acc.astype(f32)
        for o in range(n - 1):
            acc = acc + got[o].astype(f32)
        return acc

    def step(self, k):
        pc = self.pc
        got1, held1, got2a, got2b, held2, got3a, got3b, held3, got4 = self.bufs
        half = held1.shape[-1] // 2
        if k == 0:
            start(self.one)
        elif k == 1:
            finish(self.one)
            for z in range(pc.nz):
                for x in range(pc.nx):
                    acc = self.mine(z, x).astype(f32)
                    for o in range(pc.nc - 1):
                        acc = acc + got1[o, z, x].astype(f32)
                    held1[z, x] = acc.astype(bf)
            start(self.two)
        elif k == 2:
            finish(self.two)
            held2[0, :, : pc.ny] = self.total(held1[:, pc.x, :, :, :half], got2a, pc.nx).astype(bf)
            held2[1, :, : pc.nx] = self.total(held1[:, :, pc.y, :, half:], got2b, pc.ny).astype(bf)
            start(self.three)
        elif k == 3:
            finish(self.three)
            held3[:, :, :half] = self.total(held2[0, :, pc.y], got3a, pc.ny).astype(bf)
            held3[:, :, half:] = self.total(held2[1, :, pc.x], got3b, pc.nx).astype(bf)
            start(self.four)
        else:
            finish(self.four)
            self.out[...] = self.total(held3[pc.z], got4, pc.nz)


def back_kernel(dims, slots, pack, near, *refs):
    refs = list(refs)

    def take(n):
        out = refs[:n]
        del refs[:n]
        return out

    x_ref, q_ref, k_ref, v_ref, da_ref, lse_ref, dmid_ref, mean_ref, ks_ref, vs_ref = take(10)
    wq_ref, wk_ref, wv_ref, ga_ref = take(4)
    (g1_ref,) = take(1) if near else (None,)
    (din_ref,) = take(1)
    outs = take(2 if near else 1)
    aq, ak, av, dq_ref, dk_ref, dv_ref, dks_ref, dvs_ref, far_send, far_got, far_ref = take(11)
    if near:
        (g2_ref, own1) = take(2)
        bufs1, bufs2 = take(9), take(9)
        (own_sem,) = take(1)
    send_sem, recv_sem = take(2)
    T, D = x_ref.shape
    spt, nseq = slots // SPAN, T // slots
    pc = Place(dims)
    cp = Copies(send_sem, recv_sem)
    seq, dp = lax.axis_index("seq"), lax.axis_index("dp")
    seqn = pc.ny * pc.nc
    spans_all, seqs, _ = mean_ref.shape
    i, n = pl.program_id(0), pl.num_programs(0) // 2
    far = []
    for o in range(1, seqn):
        to = (seq + o) % seqn
        far.append(
            cp.make(far_send.at[:, pl.ds(to * spt, spt)], far_got.at[o - 1], far_got.at[o - 1], (dp, to))
        )
    if near:
        own_copy = pltpu.make_async_copy(g1_ref.at[:, :, :, pc.c], own1, own_sem.at[0])
        big = Scatter(pc, cp, g1_ref, lambda z, x: own1[z, x], outs[0], bufs1)
        small = Scatter(pc, cp, g2_ref, lambda z, x: g2_ref[z, x, :, pc.c], outs[1], bufs2)

    @pl.when(i == 0)
    def _():
        seq_peers = [(dp, (seq + o) % seqn) for o in range(1, seqn)]
        zx = [pc.at(**{a: to}) for a in ("z", "x") for _, to, _ in pc.partners(a)]
        pc.greet(zx + seq_peers)
        if near:
            own_copy.start()
            big.step(0)
        for acc in (aq, ak, av):
            acc[...] = jnp.zeros_like(acc)

    if near:

        @pl.when(i == 2)
        def _():
            own_copy.wait()
            big.step(1)

        for k, at in ((2, 6), (3, 8), (4, 11)):

            @pl.when(i == at)
            def _(k=k):
                big.step(k)

    x = x_ref[...].astype(f32)
    r = lax.rsqrt(jnp.mean(x * x, axis=1, keepdims=True) + EPS)
    xr = x * r
    ga = ga_ref[...]

    @pl.when(i < n)
    def _():
        tok = pl.ds(pl.multiple_of(i * T, T), T)
        attend_backward(slots, i, seq, spans_all, q_ref, k_ref, v_ref, da_ref, ks_ref, vs_ref, lse_ref,
                        dq_ref.at[tok], dk_ref.at[tok], dv_ref.at[tok], dks_ref, dvs_ref)
        xt = (xr * ga).astype(bf).T
        aq[...] += dot(xt, dq_ref[tok, :])
        ak[...] += dot(xt, dk_ref[tok, :])
        av[...] += dot(xt, dv_ref[tok, :])

    @pl.when(i == n - 1)
    def _():
        for t in range(spans_all):
            far_send[0, t] = dks_ref[:, t, :].astype(bf)
            far_send[1, t] = dvs_ref[:, t, :].astype(bf)
        start(far)
        mb = (mean_ref[...].astype(f32).reshape(spans_all * seqs, D) * ga).astype(bf)
        fk = far_send[0].reshape(spans_all * seqs, D)
        fv = far_send[1].reshape(spans_all * seqs, D)
        rows = D // pack
        parts = (aq[...], ak[...] + dot(mb, fk, 0, 0), av[...] + dot(mb, fv, 0, 0))
        for j, part in enumerate(parts):
            if near:
                g2_ref[:, :, :, :, j * rows : (j + 1) * rows, :] = part.astype(bf).reshape(dims + (rows, D))
            else:
                outs[0][j] = part
        if near:
            small.step(0)

    @pl.when(i == n)
    def _():
        finish(far)
        tot = []
        for h in range(2):
            acc = far_send[h, pl.ds(seq * spt, spt)].astype(f32)
            for o in range(seqn - 1):
                acc = acc + far_got[o, h].astype(f32)
            tot.append(acc.astype(bf).reshape(spt * seqs, D))
        rows = dot(tot[0], wk_ref[...], 1, 1) + dot(tot[1], wv_ref[...], 1, 1)
        far_ref[...] = (rows * (1.0 / SPAN)).reshape(spt, seqs, D)

    if near:
        for k, at in ((1, 1), (2, 5), (3, 8)):

            @pl.when(i == n + at)
            def _(k=k):
                small.step(k)

    @pl.when(i >= n)
    def _():
        j = i - n
        tok = pl.ds(pl.multiple_of(j * T, T), T)
        dxn = dot(dq_ref[tok, :], wq_ref[...], 1, 1)
        dxn = dxn + dot(dk_ref[tok, :], wk_ref[...], 1, 1)
        dxn = dxn + dot(dv_ref[tok, :], wv_ref[...], 1, 1)
        parts = []
        for s in range(T // SPAN):
            row = far_ref[s % spt, pl.ds(j * nseq + s // spt, 1), :]
            parts.append(dxn[s * SPAN : (s + 1) * SPAN] + row)
        gd = jnp.concatenate(parts, axis=0) * ga
        coef = jnp.mean(gd * xr, axis=1, keepdims=True)
        din_ref[...] = (dmid_ref[...].astype(f32) + r * (gd - xr * coef)).astype(bf)

    if near:

        @pl.when(i == 2 * n - 1)
        def _():
            small.step(4)


def attend_backward(slots, i, seq, spans_all, q_ref, k_ref, v_ref, da_ref, ks_ref, vs_ref, lse_ref,
                    dq_ref, dk_ref, dv_ref, dks_ref, dvs_ref):
    T, D = q_ref.shape
    spt, nseq = slots // SPAN, T // slots
    causal = causal_mask()
    t_row = lax.broadcasted_iota(jnp.int32, (FARP, 2 * SPAN), 0)

    def where(u):
        s, p = u
        return slice(s * SPAN, (s + 1) * SPAN), slice(p * 128, (p + 1) * 128), i * nseq + s // spt

    def scores(u):
        rows, ln, sq = where(u)
        ke = jnp.concatenate([k_ref[rows, ln], ks_ref[sq, :, ln]], axis=0)
        ve = jnp.concatenate([v_ref[rows, ln], vs_ref[sq, :, ln]], axis=0)
        qbd, dbd = pair_diag(q_ref[rows, ln]), pair_diag(da_ref[rows, ln])
        return dot(ke, qbd, 1, 1), dot(ve, dbd, 1, 1)

    def weigh(u, got):
        sc, dp = got
        rows, p = where(u)[0], u[1]
        far = t_row < (seq * spt + u[0] % spt)
        lse = jnp.concatenate([lse_ref[2 * p : 2 * p + 1, rows], lse_ref[2 * p + 1 : 2 * p + 2, rows]], axis=1)
        pn = jnp.where(causal, jnp.exp(sc[:SPAN] - lse), 0.0)
        pf = jnp.where(far, jnp.exp(sc[SPAN:] - lse), 0.0)
        dpn, dpf = dp[:SPAN], dp[SPAN:]
        delta = jnp.sum(pn * dpn, axis=0, keepdims=True) + jnp.sum(pf * dpf, axis=0, keepdims=True)
        dsn, dsf = (pn * (dpn - delta)).astype(bf), (pf * (dpf - delta)).astype(bf)
        return pn.astype(bf), pf.astype(bf), dsn, dsf

    def combine(u, pn, pf, dsn, dsf):
        rows, ln, sq = where(u)
        qbd, dbd = pair_diag(q_ref[rows, ln]), pair_diag(da_ref[rows, ln])
        dv = dot(jnp.concatenate([pn, pf], axis=0), dbd)
        dk = dot(jnp.concatenate([dsn, dsf], axis=0), qbd)
        dq = dot(k_ref[rows, ln], dsn, 0, 0) + dot(ks_ref[sq, :, ln], dsf, 0, 0)
        dq = jnp.concatenate([dq[:HD, :SPAN], dq[HD:, SPAN:]], axis=0) * (HD**-0.5)
        dq_ref[rows, ln] = dq.astype(bf).T
        dk_ref[rows, ln] = dk[:SPAN].astype(bf)
        dv_ref[rows, ln] = dv[:SPAN].astype(bf)
        fk, fv = dk[SPAN : SPAN + spans_all], dv[SPAN : SPAN + spans_all]
        if u[0] % spt == 0:
            dks_ref[sq, :, ln] = fk
            dvs_ref[sq, :, ln] = fv
        else:
            dks_ref[sq, :, ln] += fk
            dvs_ref[sq, :, ln] += fv

    units = [(s, p) for s in range(T // SPAN) for p in range(D // 128)]
    staged(units, scores, weigh, combine)


def back_call(dims, slots, block, pack, near, x, q, k, v, da, lse, dmid, mean, ks, vs, wq, wk, wv, ga, g1):
    n_tok, D = x.shape
    nz, nx, ny, nc = dims
    n = n_tok // block
    spt = slots // SPAN
    spans_all, seqs, _ = mean.shape
    seqn = ny * nc
    vm = pltpu.VMEM
    early = pl.BlockSpec((block, D), lambda i: (jnp.minimum(i, n - 1), 0))
    late = pl.BlockSpec((block, D), lambda i: (jnp.maximum(i - n, 0), 0))
    rows2 = D // pack * 3
    in_specs = (
        [pl.BlockSpec((block, D), lambda i: (i % n, 0))]
        + [early] * 4
        + [pl.BlockSpec((H, block), lambda i: (0, jnp.minimum(i, n - 1))), late]
        + [full(mean.shape), full(ks.shape), full(vs.shape)]
        + [full((D, D))] * 3
        + [full((1, D))]
    )
    args = [x, q, k, v, da, lse, dmid, mean, ks, vs, wq, wk, wv, ga]
    out_specs, out_shape = [late], [sds((n_tok, D), bf)]
    scratch = [vm((D, D), f32)] * 3 + [vm((n_tok, D), bf)] * 3 + [vm((seqs, spans_all, D), f32)] * 2
    scratch += [
        vm((2, spans_all, seqs, D), bf),
        vm((seqn - 1, 2, spt, seqs, D), bf),
        vm((spt, seqs, D), f32),
    ]
    copies = seqn - 1
    if near:
        rows1 = g1.shape[1]
        args.append(g1.reshape(dims + g1.shape[1:]))
        in_specs.append(pl.BlockSpec(memory_space=pl.ANY))
        out_specs += [full((rows1, D)), full((rows2, D))]
        out_shape += [sds((rows1, D), f32), sds((rows2, D), f32)]
        scratch += [vm(dims + (rows2, D), bf), vm((nz, nx, ny, rows1, D), bf)]
        scratch += Scatter.scratch(dims, rows1, D) + Scatter.scratch(dims, rows2, D)
        scratch.append(pltpu.SemaphoreType.DMA((1,)))
        copies += 2 * Scatter.copies(dims)
    else:
        out_specs.append(full((3, D, D)))
        out_shape.append(sds((3, D, D), f32))
    scratch += [pltpu.SemaphoreType.DMA((copies,))] * 2
    return pl.pallas_call(
        partial(back_kernel, dims, slots, pack, near),
        grid=(2 * n,),
        in_specs=in_specs,
        out_specs=out_specs,
        out_shape=out_shape,
        scratch_shapes=scratch,
        compiler_params=pltpu.CompilerParams(
            vmem_limit_bytes=VMEM_LIMIT, collective_id=1, has_side_effects=True,
            dimension_semantics=("arbitrary",),
        ),
    )(*args)


def body(dims, inputs, lengths, cotangent, w_query, w_key, w_value, w_out, w_up, w_down, gain_attn, gain_mlp):
    seqs, slots, D = inputs.shape
    nz, nx, ny, nc = dims
    ndev = nz * nx * ny * nc
    FF = w_up.shape[1]
    rd, rf = w_query.shape[0], w_down.shape[0]
    n_tok = seqs * slots
    block = 512
    x = inputs.reshape(n_tok, D)
    cot = cotangent.reshape(n_tok, D)
    gains = jnp.zeros((8, 256), f32)
    gains = gains.at[0, :rd].set(gain_attn.astype(f32)).at[1, :rd].set(gain_mlp.astype(f32))
    everyone = ("dp", "seq")
    near = rd % 16 == 0 and n_tok // block >= 12
    if near:
        w_first, w_later = (w_query, w_key, w_value), (w_up, w_down, w_out)
    else:
        wq, wk, wv, wu, wd, wo = (
            lax.all_gather(w, everyone, axis=0, tiled=True)
            for w in (w_query, w_key, w_value, w_up, w_down, w_out)
        )
        w_first, w_later = (wq, wk, wv), ()
    q, k, v, att, lse, ks, vs, mean, ga, gm, *later = front_call(dims, slots, block, x, w_first, w_later, gains, near)
    if near:
        *firsts, wu, wd, wo = (w.reshape(-1, w.shape[-1]) for w in later)
        wq, wk, wv = firsts
    pack = ndev if near else 32
    output, datt, dmid, sums_m = mlp_call(512, slots, 2 * block, pack, lengths, x, att, cot, wo, wu, wd, gm)
    grad_in, *sums = back_call(
        dims, slots, block, pack, near, x, q, k, v, datt, lse, dmid, mean, ks, vs, wq, wk, wv, ga, sums_m
    )
    pd, pf = D // pack, FF // pack
    last = pd * (FF // D + 1) + pf
    if near:
        sums_m, sums_a = sums
        g_out = sums_m[:pd]
        g_up = jnp.concatenate([sums_m[pd * (j + 1) : pd * (j + 2)] for j in range(FF // D)], axis=1)
        g_down = sums_m[pd * (FF // D + 1) : last]
        g_q, g_k, g_v = (sums_a[j * pd : (j + 1) * pd] for j in range(3))
    else:

        def scattered(a):
            return lax.psum_scatter(a.astype(f32), everyone, scatter_dimension=0, tiled=True)

        g_out = scattered(sums_m[:, :pd].reshape(D, D))
        g_up = scattered(
            jnp.concatenate([sums_m[:, pd * (j + 1) : pd * (j + 2)].reshape(D, D) for j in range(FF // D)], axis=1)
        )
        g_down = scattered(sums_m[:, pd * (FF // D + 1) : last].reshape(FF, D))
        g_q, g_k, g_v = (scattered(sums[0][j]) for j in range(3))
    g_ga = jnp.sum(
        w_query.astype(f32) * g_q + w_key.astype(f32) * g_k + w_value.astype(f32) * g_v, axis=1
    ) / gain_attn.astype(f32)
    g_gm = jnp.sum(w_up.astype(f32) * g_up, axis=1) / gain_mlp.astype(f32)
    return (
        output.reshape(inputs.shape), grad_in.astype(f32).reshape(inputs.shape),
        g_q, g_k, g_v, g_out, g_up, g_down, g_ga, g_gm,
    )


def solution(mesh):
    dp, seq = mesh.shape["dp"], mesh.shape["seq"]
    nx = max(d for d in range(1, dp + 1) if dp % d == 0 and d * d <= dp)
    nc = 2 if seq % 2 == 0 else 1
    dims = (dp // nx, nx, seq // nc, nc)
    rows, vec = P(("dp", "seq"), None), P(("dp", "seq"))
    tokens = P("dp", "seq", None)
    return jax.shard_map(
        partial(body, dims),
        mesh=mesh,
        in_specs=(tokens, P("dp"), tokens) + (rows,) * 6 + (vec,) * 2,
        out_specs=(tokens, tokens) + (rows,) * 6 + (vec,) * 2,
        check_vma=False,
    )
```

time: 417 us -> 267 us (0.64)
  Pallas kernels: 400 us -> 249 us
  other arithmetic: 8.93 us -> 14.1 us
    pallas_call x6 -> x2, Pallas kernels: 285 us -> 147 us  [the longest x1 75.1 us: back_call(): pl.pallas_call(partial(back_kernel, dims, slots, pack, near), grid=(2 * n...]
    pallas_call x1, Pallas kernels: 114 us -> 102 us  [mlp_call(): pl.pallas_call(partial(mlp_kernel, chunk, slots, ndev), grid=(n_tok // bl...]
    reshape x0 -> x1, other arithmetic: none -> 9.28 us  [body(): grad_in.astype(f32).reshape(inputs.shape)]
    concatenate x2 -> x0, other arithmetic: 7.61 us -> none  [the longest x1 6.95 us: body(): jnp.concatenate([sums_m, sums_a], axis=1)]
where the time goes in v2:
time: 267 us; the launch traced here: 266 us
  Pallas kernels  249 us (93%)
  other arithmetic  14.1 us (5%)
    pallas_call x1, Pallas kernels, mlp_call(): pl.pallas_call(partial(mlp_kernel, chunk, slots, ndev), grid=(n_tok // bl...  102 us
    pallas_call x1, Pallas kernels, back_call(): pl.pallas_call(partial(back_kernel, dims, slots, pack, near), grid=(2 * n...  75.1 us
    pallas_call x1, Pallas kernels, front_call(): pl.pallas_call(partial(front_kernel, dims, slots, len(w_first) if near el...  71.8 us
    reshape x1, other arithmetic, body(): grad_in.astype(f32).reshape(inputs.shape)  9.28 us

profile of v2, /device:TPU:0, one launch (start us, length us, event | category | flops | bytes accessed | tf_op | source)
XLA Modules:
  0.0 266.1 jit_solution(666420851052550491)
XLA Ops:
  0.6 0.7 convert_bitcast_fusion.1
  1.3 0.7 convert_bitcast_fusion
  2.0 0.2 scatter.9.refs_7_
  2.1 0.0 copy-start.4
  2.2 0.6 copy-done.4
  2.8 71.8 %shard_map.186 = (bf16[6144,512]{1,0:T(8,128)(2,1)}, bf16[6144,512]{1,0:T(8,128)(2,1)}, bf16[6144,512]{1,0:T(8,128)(2,1)}, bf16[6144,512]{1,0:T(8,128)(2,1)}, f3...) custom-call(bf16[6144,512]{1,0:T(8,128)(2,1)} %bitcast.16, ...), custom_call_target="tpu_custom_call" | custom-call | tf_op jit(solution)/shard_map/pallas_call | solution.py:360
  74.5 102.1 %shard_map.187 = (bf16[6144,512]{1,0:T(8,128)(2,1)}, bf16[6144,512]{1,0:T(8,128)(2,1)}, bf16[6144,512]{1,0:T(8,128)(2,1)}, bf16[32,144,512]{2,1,0:T(8,128)(2,1)}) custom-call(s32[24]{0:T(128)} %len_ref.1, bf16[6144,512]{1,0:T(8,128)(2,1)} %bitcast.17, bf16[6144,512]{1,0:T(8,128)(2,1)} %get-tuple-element.57.att_ref, bf16[6144,512]{1,0:T(8,128)(2,1)} %bitcast.19, ...), custom_call_target="tpu_custom_call" | custom-call | tf_op jit(solution)/shard_map/pallas_call | solution.py:463
  176.6 0.0 copy-start.1
  176.6 0.0 copy-start.2
  176.6 0.0 copy-start.3
  176.6 0.0 copy-start.5
  176.6 0.0 copy-start
  176.7 0.0 copy-start.6
  176.7 75.1 %shard_map.188 = (bf16[6144,512]{1,0:T(8,128)(2,1)}, f32[144,512]{1,0:T(8,128)}, f32[48,512]{1,0:T(8,128)}) custom-call(bf16[6144,512]{1,0:T(8,128)(2,1)} %bitcast.18, bf16[6144,512]{1,0:T(8,128)(2,1)} %get-tuple-element.63.refs_1_, bf16[6144,512]{1,0:T(8,128)(2,1)} %get-tuple-element.64.refs_2_, bf16[6144,512]{1,0:T(8,128)(2,1)} %get-tuple-element.65.refs_3_, ...), custom_call_target="tpu_custom_call" | custom-call | tf_op jit(solution)/shard_map/pallas_call | solution.py:793
  251.8 1.6 slice.70
  253.4 0.0 copy-done.1
  253.4 0.0 copy-done.2
  253.4 0.0 copy-done.3
  253.4 1.6 add_reduce_fusion
  255.0 0.0 copy-done.5
  255.0 0.5 convert_divide_fusion.1
  255.5 0.0 copy-done
  255.6 0.8 multiply_reduce_fusion
  256.3 0.0 copy-done.6
  256.3 0.5 convert_divide_fusion
  256.9 9.3 %convert.1 = f32[24,256,512]{2,1,0:T(8,128)} convert(bf16[24,256,512]{2,1,0:T(8,128)(2,1)} %bitcast.20) | non-fusion elementwise | flops 3145728 | bytes 18874368 | tf_op jit(solution)/shard_map/reshape | solution.py:862
  (1 shorter events, 0.0 us)
Async XLA Ops:
  2.1 0.6 copy-start.4
  176.6 76.8 %copy-start.1 = (bf16[16,512]{1,0:T(8,128)(2,1)S(1)}, bf16[16,512]{1,0:T(8,128)(2,1)}, u32[]{:S(2)}) copy-start(bf16[16,512]{1,0:T(8,128)(2,1)} %refs_1_.1) | copy-start | bytes 49156
  176.6 76.8 %copy-start.2 = (bf16[16,512]{1,0:T(8,128)(2,1)S(1)}, bf16[16,512]{1,0:T(8,128)(2,1)}, u32[]{:S(2)}) copy-start(bf16[16,512]{1,0:T(8,128)(2,1)} %refs_2_.1) | copy-start | bytes 49156
  176.6 76.8 %copy-start.3 = (bf16[16,512]{1,0:T(8,128)(2,1)S(1)}, bf16[16,512]{1,0:T(8,128)(2,1)}, u32[]{:S(2)}) copy-start(bf16[16,512]{1,0:T(8,128)(2,1)} %refs_3_.1) | copy-start | bytes 49156
  176.6 78.4 %copy-start.5 = (bf16[16]{0:T(256)(128)(2,1)S(1)}, bf16[16]{0:T(256)(128)(2,1)}, u32[]{:S(2)}) copy-start(bf16[16]{0:T(256)(128)(2,1)} %param.24) | copy-start | bytes 100
  176.6 78.9 %copy-start = (bf16[16,2048]{1,0:T(8,128)(2,1)S(1)}, bf16[16,2048]{1,0:T(8,128)(2,1)}, u32[]{:S(2)}) copy-start(bf16[16,2048]{1,0:T(8,128)(2,1)} %refs_4_.1) | copy-start | bytes 196612
  176.7 79.7 %copy-start.6 = (bf16[16]{0:T(256)(128)(2,1)S(1)}, bf16[16]{0:T(256)(128)(2,1)}, u32[]{:S(2)}) copy-start(bf16[16]{0:T(256)(128)(2,1)} %param.25) | copy-start | bytes 100

commit v3 on v2

--- a/solution.py
+++ b/solution.py
@@ -44,17 +44,17 @@
     return j <= jnp.where(i >= SPAN, i - SPAN, i)
 
 
-def gain_row(tiles, which, ndev, rows):
+def gain_row(slabs, which, ndev, rows):
     width = ndev * rows
-    r = lax.broadcasted_iota(jnp.int32, (ndev * 8, 128), 0)
-    l = lax.broadcasted_iota(jnp.int32, (ndev * 8, 128), 1)
-    keep = jnp.where((r % 8 == which) & (l < rows), tiles, 0.0).astype(bf)
+    r = lax.broadcasted_iota(jnp.int32, slabs.shape, 0)
+    l = lax.broadcasted_iota(jnp.int32, slabs.shape, 1)
+    keep = jnp.where((r % 16 == which) & (l < rows), slabs.astype(f32), 0.0).astype(bf)
     a = lax.broadcasted_iota(jnp.int32, (128, width), 0)
     b = lax.broadcasted_iota(jnp.int32, (128, width), 1)
     spread = dot(keep, jnp.where(b % rows == a, 1.0, 0.0).astype(bf))
-    d = lax.broadcasted_iota(jnp.int32, (ndev * 8, width), 0)
-    c = lax.broadcasted_iota(jnp.int32, (ndev * 8, width), 1)
-    return jnp.sum(jnp.where(d // 8 == c // rows, spread, 0.0), axis=0, keepdims=True)
+    d = lax.broadcasted_iota(jnp.int32, spread.shape, 0)
+    c = lax.broadcasted_iota(jnp.int32, spread.shape, 1)
+    return jnp.sum(jnp.where(d // 16 == c // rows, spread, 0.0), axis=0, keepdims=True)
 
 
 class Place:
@@ -79,10 +79,11 @@
         return [(o, (me + o) % n, (me + n - o) % n) for o in range(1, n)]
 
     def greet(self, others):
-        barrier = pltpu.get_barrier_semaphore()
         for other in others:
-            pl.semaphore_signal(barrier, inc=1, device_id=other, device_id_type=MESH)
-        pl.semaphore_wait(barrier, len(others))
+            pl.semaphore_signal(pltpu.get_barrier_semaphore(), inc=1, device_id=other, device_id_type=MESH)
+
+    def meet(self, others):
+        pl.semaphore_wait(pltpu.get_barrier_semaphore(), len(others))
 
     def others(self):
         return [self.at(**{a: to}) for a in ("z", "x", "y", "c") for _, to, _ in self.partners(a)]
@@ -117,34 +118,35 @@
         into.wait_recv()
 
 
-def halves(ref):
-    n = ref.shape[-1] // 2
-    return pl.ds(0, n), pl.ds(n, n)
-
-
-def gather_phases(pc, cp, pieces, wholes):
+def shares(rows, width):
+    if rows % 32 == 0:
+        return (pl.ds(0, rows // 2), slice(None)), (pl.ds(rows // 2, rows // 2), slice(None))
+    return (slice(None), pl.ds(0, width // 2)), (slice(None), pl.ds(width // 2, width // 2))
+
+
+def gather_phases(pc, cp, pieces, wholes, routes):
     z, x, y, c = pc.z, pc.x, pc.y, pc.c
     first, second, third, last = [], [], [], []
-    for piece, whole in zip(pieces, wholes):
+    for piece, whole, route in zip(pieces, wholes, routes):
+        rows, width = whole.shape[-2:]
+        everything = (slice(None), slice(None))
+        one, two = shares(rows, width) if route == "both" else (everything, everything)
         for _, to, fr in pc.partners("z"):
             first.append(cp.make(piece, whole.at[z, x, y, c], whole.at[fr, x, y, c], pc.at(z=to)))
-    for whole in wholes:
-        a, b = halves(whole)
         for _, to, fr in pc.partners("x"):
-            v = whole.at[:, x, y, c, :, a]
-            second.append(cp.make(v, v, whole.at[:, fr, y, c, :, a], pc.at(x=to)))
+            if route != "yx":
+                v = whole.at[(slice(None), x, y, c) + one]
+                second.append(cp.make(v, v, whole.at[(slice(None), fr, y, c) + one], pc.at(x=to)))
+            if route != "xy":
+                v = whole.at[(slice(None), x, slice(None), c) + two]
+                third.append(cp.make(v, v, whole.at[(slice(None), fr, slice(None), c) + two], pc.at(x=to)))
         for _, to, fr in pc.partners("y"):
-            v = whole.at[:, x, y, c, :, b]
-            second.append(cp.make(v, v, whole.at[:, x, fr, c, :, b], pc.at(y=to)))
-    for whole in wholes:
-        a, b = halves(whole)
-        for _, to, fr in pc.partners("y"):
-            v = whole.at[:, :, y, c, :, a]
-            third.append(cp.make(v, v, whole.at[:, :, fr, c, :, a], pc.at(y=to)))
-        for _, to, fr in pc.partners("x"):
-            v = whole.at[:, x, :, c, :, b]
-            third.append(cp.make(v, v, whole.at[:, fr, :, c, :, b], pc.at(x=to)))
-    for whole in wholes:
+            if route != "xy":
+                v = whole.at[(slice(None), x, y, c) + two]
+                second.append(cp.make(v, v, whole.at[(slice(None), x, fr, c) + two], pc.at(y=to)))
+            if route != "yx":
+                v = whole.at[(slice(None), slice(None), y, c) + one]
+                third.append(cp.make(v, v, whole.at[(slice(None), slice(None), fr, c) + one], pc.at(y=to)))
         for _, to, fr in pc.partners("c"):
             v = whole.at[:, :, :, c]
             last.append(cp.make(v, v, whole.at[:, :, :, fr], pc.at(c=to)))
@@ -160,14 +162,13 @@
         del refs[:n]
         return out
 
-    (x_ref,) = take(1)
-    pieces = take(n_first + n_later + 1 if near else 1)
+    x_ref, ga_own, gm_own = take(3)
+    pieces = take(n_first + n_later)
     w_in = [] if near else take(3)
     q_ref, k_ref, v_ref, att_ref, lse_ref, ks_ref, vs_ref, mean_ref, ga_ref, gm_ref = take(10)
-    first_out = take(n_first)
+    w_out = take(n_first)
     later = take(n_later)
-    w_refs = take(3) if near else w_in
-    tiles_ref, own_mean, all_mean, tmp_ref, local_sem, send_sem, recv_sem = take(7)
+    pack_ref, gain_ref, own_mean, all_mean, local_sem, send_sem, recv_sem = take(7)
     T, D = x_ref.shape
     spt, nseq = slots // SPAN, T // slots
     pc = Place(dims)
@@ -177,40 +178,41 @@
     spans_all, seqs = spt * seqn, all_mean.shape[1]
     ndev = pc.nz * pc.nx * seqn
     rd = D // ndev
-    chunks = []
-    own = []
-    if near:
-        wholes = w_refs + [tiles_ref]
-        firsts = pieces[:n_first] + pieces[-1:]
-        groups = [(firsts, wholes)] + [([p], [w]) for p, w in zip(pieces[n_first:-1], later)]
-    else:
-        groups = [(pieces, [tiles_ref])]
-    for sources, targets in groups:
-        chunks.append(gather_phases(pc, cp, sources, targets))
-        mine = []
-        for source, target in zip(sources, targets):
-            mine.append(
-                pltpu.make_async_copy(
-                    source, target.at[pc.z, pc.x, pc.y, pc.c], local_sem.at[sum(map(len, own)) + len(mine)]
-                )
-            )
-        own.append(mine)
+    mine = (pc.z, pc.x, pc.y, pc.c)
+    packs = [pack_ref, gain_ref] if near else [gain_ref]
+    first = gather_phases(pc, cp, [p.at[mine] for p in packs], packs, ["both", "xy"][-len(packs) :])
+    later_phases = gather_phases(pc, cp, pieces[n_first:], later, ["xy", "yx", "both"][:n_later])
+    own_first = [
+        pltpu.make_async_copy(p, pack_ref.at[mine + (pl.ds(k * rd, rd),)], local_sem.at[k])
+        for k, p in enumerate(pieces[:n_first])
+    ]
+    own_later = [
+        pltpu.make_async_copy(p, w.at[mine], local_sem.at[n_first + k])
+        for k, (p, w) in enumerate(zip(pieces[n_first:], later))
+    ]
     means = []
     for o in range(1, seqn):
         to, fr = (seq + o) % seqn, (seq + seqn - o) % seqn
         v = all_mean.at[pl.ds(seq * spt, spt)]
         means.append(cp.make(v, v, all_mean.at[pl.ds(fr * spt, spt)], (dp, to)))
     i, n = pl.program_id(0), pl.num_programs(0) // 2
+    w_refs = w_out if near else w_in
 
     @pl.when(i == 0)
     def _():
+        for copy in own_first + own_later:
+            copy.start()
+        slab = jnp.concatenate([ga_own[...], gm_own[...]], axis=0).astype(f32)
+        gain_ref[mine] = jnp.concatenate(
+            [jnp.concatenate([slab, jnp.zeros((2, max(128 - rd, 0)), f32)], axis=1)[:, :128], jnp.zeros((14, 128), f32)], axis=0
+        ).astype(bf)
         seq_peers = [(dp, (seq + o) % seqn) for o in range(1, seqn)]
         zx = [pc.at(**{a: to}) for a in ("z", "x") for _, to, _ in pc.partners(a)]
         pc.greet(zx + seq_peers)
-        start(chunks[0][0])
-        for mine in own:
-            for copy in mine:
-                copy.start()
+        pc.meet(zx + seq_peers)
+        for copy in own_first:
+            copy.wait()
+        start(first[0])
 
     x = x_ref[...].astype(f32)
     r = lax.rsqrt(jnp.mean(x * x, axis=1, keepdims=True) + EPS)
@@ -222,73 +224,61 @@
             row = jnp.sum(xr[s * SPAN : (s + 1) * SPAN], axis=0, keepdims=True) * (1.0 / SPAN)
             own_mean[s % spt, pl.ds(i * nseq + s // spt, 1), :] = row
 
+    @pl.when(i == 1)
+    def _():
+        finish(first[0])
+        start(first[1])
+        for copy in own_later:
+            copy.wait()
+        if near:
+            start(later_phases[0])
+
     @pl.when(i == n - 1)
     def _():
-        for mine in own:
-            for copy in mine:
-                copy.wait()
-        c0 = chunks[0]
-        finish(c0[0])
-        start(c0[1])
+        finish(first[1])
+        start(first[2])
         all_mean[pl.ds(seq * spt, spt)] = own_mean[...].astype(bf)
         start(means)
-        if near:
-            start(chunks[1][0])
-        finish(c0[1])
-        start(c0[2])
+        finish(first[2])
+        start(first[3])
         finish(means)
         mean_ref[...] = all_mean[...]
-        finish(c0[2])
-        start(c0[3])
-        finish(c0[3])
-        for w_ref, out in zip(w_refs, first_out):
-            out[...] = w_ref[...]
-        tiles = tiles_ref[...].reshape(ndev * 8, tiles_ref.shape[-1])[:, :128]
-        ga_ref[...] = gain_row(tiles, 0, ndev, rd)
-        gm_ref[...] = gain_row(tiles, 1, ndev, rd)
-        mb = (all_mean[...].astype(f32).reshape(spans_all * seqs, D) * ga_ref[...]).astype(bf)
-        for w_ref, out in ((w_refs[1], ks_ref), (w_refs[2], vs_ref)):
-            sums = dot(mb, w_ref[...].reshape(D, D))
-            tmp_ref[...] = jnp.zeros_like(tmp_ref)
-            for t in range(spans_all):
-                tmp_ref[:, t, :] = sums[t * seqs : (t + 1) * seqs]
-            out[...] = tmp_ref[...].astype(bf)
-
-    if near:
-        up, down, last = chunks[1], chunks[2], chunks[3]
-        plan = [
-            (0, [up[0]], [up[1], down[0], last[0]]),
-            (2, [up[1]], [up[2]]),
-            (4, [up[2], down[0], last[0]], [up[3], down[1]]),
-            (6, [up[3], down[1]], [down[2]]),
-            (8, [down[2]], [down[3], last[1]]),
-            (9, [last[1]], [last[2]]),
-            (10, [last[2]], [last[3]]),
-        ]
-        for at, ends, begins in plan:
+        to = lax.broadcasted_iota(jnp.int32, (seqs * FARP, spans_all * seqs), 0)
+        fr = lax.broadcasted_iota(jnp.int32, (seqs * FARP, spans_all * seqs), 1)
+        order = jnp.where((to % FARP == fr // seqs) & (to // FARP == fr % seqs), 1.0, 0.0).astype(bf)
+        ordered = dot(order, all_mean[...].reshape(spans_all * seqs, D))
+        finish(first[3])
+        slabs = gain_ref[...].reshape(ndev * 16, 128)
+        ga_ref[...] = gain_row(slabs, 0, ndev, rd)
+        gm_ref[...] = gain_row(slabs, 1, ndev, rd)
+        for k in range(n_first):
+            w_out[k][...] = pack_ref[:, :, :, :, k * rd : (k + 1) * rd, :].reshape(D, D)
+        mb = (ordered * ga_ref[...]).astype(bf)
+        ks_ref[...] = dot(mb, w_refs[1][...]).astype(bf).reshape(seqs, FARP, D)
+        vs_ref[...] = dot(mb, w_refs[2][...]).astype(bf).reshape(seqs, FARP, D)
+
+    if near:
+        for k, at in ((1, 0), (2, 2), (3, 5)):
 
             @pl.when(i == n + at)
-            def _(ends=ends, begins=begins):
-                for c in ends:
-                    finish(c)
-                for c in begins:
-                    start(c)
+            def _(k=k):
+                finish(later_phases[k - 1])
+                start(later_phases[k])
 
     @pl.when(i >= n)
     def _():
         j = i - n
         xn = (xr * ga_ref[...]).astype(bf)
-        q_ref[...] = (dot(xn, w_refs[0][...].reshape(D, D)).astype(bf) * (HD**-0.5)).astype(bf)
-        k_ref[...] = dot(xn, w_refs[1][...].reshape(D, D)).astype(bf)
-        v_ref[...] = dot(xn, w_refs[2][...].reshape(D, D)).astype(bf)
+        q_ref[...] = (dot(xn, w_refs[0][...]).astype(bf) * (HD**-0.5)).astype(bf)
+        k_ref[...] = dot(xn, w_refs[1][...]).astype(bf)
+        v_ref[...] = dot(xn, w_refs[2][...]).astype(bf)
         attend_forward(slots, j, seq, q_ref, k_ref, v_ref, ks_ref, vs_ref, att_ref, lse_ref)
 
     if near:
 
         @pl.when(i == 2 * n - 1)
         def _():
-            finish(chunks[2][3])
-            finish(chunks[3][3])
+            finish(later_phases[3])
 
 
 def attend_forward(slots, j, seq, q_ref, k_ref, v_ref, ks_ref, vs_ref, att_ref, lse_ref):
@@ -319,7 +309,8 @@
     def combine(u, en, ef, m, l):
         rows, ln, sq = where(u)
         p = u[1]
-        at = (dot(v_ref[rows, ln], en, 0, 0) + dot(vs_ref[sq, :, ln], ef, 0, 0)) * (1.0 / l)
+        ve = jnp.concatenate([v_ref[rows, ln], vs_ref[sq, :, ln]], axis=0)
+        at = dot(ve, jnp.concatenate([en, ef], axis=0), 0, 0) * (1.0 / l)
         att_ref[rows, ln] = jnp.concatenate([at[:HD, :SPAN], at[HD:, SPAN:]], axis=0).astype(bf).T
         total = m + jnp.log(l)
         lse_ref[2 * p : 2 * p + 1, rows] = total[:, :SPAN]
@@ -331,13 +322,16 @@
 
 def staged(units, first, second, third):
     a, b = {}, {}
-    for t in range(len(units) + 2):
-        if t < len(units):
-            a[t] = first(units[t])
-        if 0 <= t - 1 < len(units):
-            b[t - 1] = second(units[t - 1], a.pop(t - 1))
-        if 0 <= t - 2:
-            third(units[t - 2], *b.pop(t - 2))
+    for t in range(0, len(units) + 4, 2):
+        for k in (t, t + 1):
+            if k < len(units):
+                a[k] = first(units[k])
+        for k in (t - 2, t - 1):
+            if 0 <= k < len(units):
+                b[k] = second(units[k], a.pop(k))
+        for k in (t - 4, t - 3):
+            if 0 <= k < len(units):
+                third(units[k], *b.pop(k))
 
 
 def front_call(dims, slots, block, x, w_first, w_later, gains, near):
@@ -345,44 +339,46 @@
     seqs, spt = n_tok // slots, slots // SPAN
     nz, nx, ny, nc = dims
     n = n_tok // block
+    ndev = nz * nx * ny * nc
     spans_all = spt * ny * nc
     hbm = pl.BlockSpec(memory_space=pl.ANY)
     summ = (seqs, FARP, D)
     per_piece = (nz - 1) + 2 * (nx - 1) + 2 * (ny - 1) + (nc - 1)
-    n_pieces = len(w_first) + len(w_later) + 1 if near else 1
-    copies = n_pieces * per_piece + ny * nc - 1
-    tok = pl.BlockSpec((block, D), lambda i: (jnp.maximum(i - n, 0), 0))
-    args = [x] + (list(w_first) + list(w_later) if near else []) + [gains] + ([] if near else list(w_first))
-    in_specs = [pl.BlockSpec((block, D), lambda i: (i % n, 0))] + [hbm] * n_pieces
-    if not near:
-        in_specs += [full(w.shape) for w in w_first]
+    n_first, n_later = (len(w_first), len(w_later)) if near else (0, 0)
+    rows = sum(w.shape[0] for w in w_first) if near else 16
+    copies = (2 + n_later) * per_piece + ny * nc - 1
+    late = lambda i: jnp.maximum(i - n, 0)
+    tok = pl.BlockSpec((block, D), lambda i: (late(i), 0))
+    in_specs = [pl.BlockSpec((block, D), lambda i: (i % n, 0)), full((1, D // ndev)), full((1, D // ndev))]
+    in_specs += [hbm] * (n_first + n_later) if near else [full(w.shape) for w in w_first]
     row = sds((1, D), f32)
     return pl.pallas_call(
-        partial(front_kernel, dims, slots, len(w_first) if near else 0, len(w_later) if near else 0),
+        partial(front_kernel, dims, slots, n_first, n_later),
         grid=(2 * n,),
         in_specs=in_specs,
         out_specs=[tok] * 4
-        + [pl.BlockSpec((H, block), lambda i: (0, jnp.maximum(i - n, 0))), full(summ), full(summ)]
+        + [pl.BlockSpec((H, block), lambda i: (0, late(i))), full(summ), full(summ)]
         + [full((spans_all, seqs, D)), full((1, D)), full((1, D))]
-        + ([full(dims + w.shape) for w in w_first] + [hbm] * len(w_later) if near else []),
+        + [full((D, D))] * n_first
+        + [hbm] * n_later,
         out_shape=[sds((n_tok, D), bf)] * 4
         + [sds((H, n_tok), f32), sds(summ, bf), sds(summ, bf), sds((spans_all, seqs, D), bf), row, row]
-        + ([sds(dims + w.shape, w.dtype) for w in (*w_first, *w_later)] if near else []),
-        scratch_shapes=([pltpu.VMEM(dims + w.shape, w.dtype) for w in w_first] if near else [])
-        + [
-            pltpu.VMEM(dims + gains.shape, f32),
+        + [sds((D, D), bf)] * n_first
+        + [sds(dims + w.shape, w.dtype) for w in w_later[:n_later]],
+        scratch_shapes=[
+            pltpu.VMEM(dims + (rows, D), bf),
+            pltpu.VMEM(dims + (16, 128), bf),
             pltpu.VMEM((spt, seqs, D), f32),
             pltpu.VMEM((spans_all, seqs, D), bf),
-            pltpu.VMEM(summ, f32),
-            pltpu.SemaphoreType.DMA((n_pieces,)),
-            pltpu.SemaphoreType.DMA((copies,)),
-            pltpu.SemaphoreType.DMA((copies,)),
+            pltpu.SemaphoreType.DMA((max(n_first + n_later, 1),)),
+            pltpu.SemaphoreType.DMA((max(copies, 1),)),
+            pltpu.SemaphoreType.DMA((max(copies, 1),)),
         ],
         compiler_params=pltpu.CompilerParams(
             vmem_limit_bytes=VMEM_LIMIT, collective_id=0, has_side_effects=True,
             dimension_semantics=("arbitrary",),
         ),
-    )(*args)
+    )(x, *gains, *w_first, *w_later)
 
 
 def mlp_kernel(chunk, slots, ndev, len_ref, x_ref, att_ref, cot_ref, wo_ref, wu_ref, wd_ref, gm_ref,
@@ -478,15 +474,16 @@
     @staticmethod
     def scratch(dims, rows, width):
         nz, nx, ny, nc = dims
-        half, most = width // 2, max(nx, ny)
+        most = max(nx, ny)
+        half = (rows // 2, width) if rows % 32 == 0 else (rows, width // 2)
         return [
             pltpu.VMEM((nc - 1, nz, nx, ny, rows, width), bf),
             pltpu.VMEM((nz, nx, ny, rows, width), bf),
-            pltpu.VMEM((nx - 1, nz, ny, rows, half), bf),
-            pltpu.VMEM((ny - 1, nz, nx, rows, half), bf),
-            pltpu.VMEM((2, nz, most, rows, half), bf),
-            pltpu.VMEM((ny - 1, nz, rows, half), bf),
-            pltpu.VMEM((nx - 1, nz, rows, half), bf),
+            pltpu.VMEM((nx - 1, nz, ny) + half, bf),
+            pltpu.VMEM((ny - 1, nz, nx) + half, bf),
+            pltpu.VMEM((2, nz, most) + half, bf),
+            pltpu.VMEM((ny - 1, nz) + half, bf),
+            pltpu.VMEM((nx - 1, nz) + half, bf),
             pltpu.VMEM((nz, rows, width), bf),
             pltpu.VMEM((nz - 1, rows, width), bf),
         ]
@@ -499,16 +496,17 @@
     def __init__(self, pc, cp, g, mine, out, scratch):
         self.pc, self.mine, self.out, self.bufs = pc, mine, out, scratch
         got1, held1, got2a, got2b, held2, got3a, got3b, held3, got4 = scratch
-        a, b = halves(g)
+        a, b = self.a, self.b = shares(*g.shape[-2:])
+        every = slice(None)
         self.one = [
             cp.make(g.at[:, :, :, to], got1.at[o - 1], got1.at[o - 1], pc.at(c=to))
             for o, to, _ in pc.partners("c")
         ]
         self.two = [
-            cp.make(held1.at[:, to, :, :, a], got2a.at[o - 1], got2a.at[o - 1], pc.at(x=to))
+            cp.make(held1.at[(every, to, every) + a], got2a.at[o - 1], got2a.at[o - 1], pc.at(x=to))
             for o, to, _ in pc.partners("x")
         ] + [
-            cp.make(held1.at[:, :, to, :, b], got2b.at[o - 1], got2b.at[o - 1], pc.at(y=to))
+            cp.make(held1.at[(every, every, to) + b], got2b.at[o - 1], got2b.at[o - 1], pc.at(y=to))
             for o, to, _ in pc.partners("y")
         ]
         self.three = [
@@ -524,6 +522,8 @@
 
     @staticmethod
     def total(acc, got, n):
+        if n == 2:
+            return acc + got[0]
         acc = acc.astype(f32)
         for o in range(n - 1):
             acc = acc + got[o].astype(f32)
@@ -532,31 +532,31 @@
     def step(self, k):
         pc = self.pc
         got1, held1, got2a, got2b, held2, got3a, got3b, held3, got4 = self.bufs
-        half = held1.shape[-1] // 2
+        every = slice(None)
         if k == 0:
             start(self.one)
         elif k == 1:
             finish(self.one)
             for z in range(pc.nz):
                 for x in range(pc.nx):
-                    acc = self.mine(z, x).astype(f32)
+                    acc = self.mine(z, x)
                     for o in range(pc.nc - 1):
-                        acc = acc + got1[o, z, x].astype(f32)
-                    held1[z, x] = acc.astype(bf)
+                        acc = acc + got1[o, z, x]
+                    held1[z, x] = acc
             start(self.two)
         elif k == 2:
             finish(self.two)
-            held2[0, :, : pc.ny] = self.total(held1[:, pc.x, :, :, :half], got2a, pc.nx).astype(bf)
-            held2[1, :, : pc.nx] = self.total(held1[:, :, pc.y, :, half:], got2b, pc.ny).astype(bf)
+            held2[0, :, : pc.ny] = self.total(held1[(every, pc.x, every) + self.a], got2a, pc.nx).astype(bf)
+            held2[1, :, : pc.nx] = self.total(held1[(every, every, pc.y) + self.b], got2b, pc.ny).astype(bf)
             start(self.three)
         elif k == 3:
             finish(self.three)
-            held3[:, :, :half] = self.total(held2[0, :, pc.y], got3a, pc.ny).astype(bf)
-            held3[:, :, half:] = self.total(held2[1, :, pc.x], got3b, pc.nx).astype(bf)
+            held3[(every,) + self.a] = self.total(held2[0, :, pc.y], got3a, pc.ny).astype(bf)
+            held3[(every,) + self.b] = self.total(held2[1, :, pc.x], got3b, pc.nx).astype(bf)
             start(self.four)
         else:
             finish(self.four)
-            self.out[...] = self.total(held3[pc.z], got4, pc.nz)
+            self.out[...] = self.total(held3[pc.z], got4, pc.nz).astype(f32)
 
 
 def back_kernel(dims, slots, pack, near, *refs):
@@ -597,25 +597,26 @@
         big = Scatter(pc, cp, g1_ref, lambda z, x: own1[z, x], outs[0], bufs1)
         small = Scatter(pc, cp, g2_ref, lambda z, x: g2_ref[z, x, :, pc.c], outs[1], bufs2)
 
+    seq_peers = [(dp, (seq + o) % seqn) for o in range(1, seqn)]
+    zx = [pc.at(**{a: to}) for a in ("z", "x") for _, to, _ in pc.partners(a)]
+
     @pl.when(i == 0)
     def _():
-        seq_peers = [(dp, (seq + o) % seqn) for o in range(1, seqn)]
-        zx = [pc.at(**{a: to}) for a in ("z", "x") for _, to, _ in pc.partners(a)]
         pc.greet(zx + seq_peers)
         if near:
             own_copy.start()
-            big.step(0)
         for acc in (aq, ak, av):
             acc[...] = jnp.zeros_like(acc)
 
-    if near:
-
-        @pl.when(i == 2)
-        def _():
+    @pl.when(i == 1)
+    def _():
+        pc.meet(zx + seq_peers)
+        if near:
             own_copy.wait()
-            big.step(1)
-
-        for k, at in ((2, 6), (3, 8), (4, 11)):
+            big.step(0)
+
+    if near:
+        for k, at in ((1, n // 3), (2, 2 * n // 3), (3, n - 1), (4, n + 1)):
 
             @pl.when(i == at)
             def _(k=k):
@@ -655,8 +656,24 @@
         if near:
             small.step(0)
 
+    def products(j):
+        tok = pl.ds(pl.multiple_of(j * T, T), T)
+        dxn = dot(dq_ref[tok, :], wq_ref[...], 1, 1)
+        dxn = dxn + dot(dk_ref[tok, :], wk_ref[...], 1, 1)
+        return dxn + dot(dv_ref[tok, :], wv_ref[...], 1, 1)
+
+    def to_input(j, dxn):
+        parts = []
+        for s in range(T // SPAN):
+            row = far_ref[s % spt, pl.ds(j * nseq + s // spt, 1), :]
+            parts.append(dxn[s * SPAN : (s + 1) * SPAN] + row)
+        gd = jnp.concatenate(parts, axis=0) * ga
+        coef = jnp.mean(gd * xr, axis=1, keepdims=True)
+        din_ref[...] = (dmid_ref[...].astype(f32) + r * (gd - xr * coef)).astype(bf)
+
     @pl.when(i == n)
     def _():
+        dxn = products(0)
         finish(far)
         tot = []
         for h in range(2):
@@ -666,28 +683,18 @@
             tot.append(acc.astype(bf).reshape(spt * seqs, D))
         rows = dot(tot[0], wk_ref[...], 1, 1) + dot(tot[1], wv_ref[...], 1, 1)
         far_ref[...] = (rows * (1.0 / SPAN)).reshape(spt, seqs, D)
-
-    if near:
-        for k, at in ((1, 1), (2, 5), (3, 8)):
+        to_input(0, dxn)
+
+    if near:
+        for k, at in ((1, 1), (2, n // 2), (3, 2 * n // 3)):
 
             @pl.when(i == n + at)
             def _(k=k):
                 small.step(k)
 
-    @pl.when(i >= n)
-    def _():
-        j = i - n
-        tok = pl.ds(pl.multiple_of(j * T, T), T)
-        dxn = dot(dq_ref[tok, :], wq_ref[...], 1, 1)
-        dxn = dxn + dot(dk_ref[tok, :], wk_ref[...], 1, 1)
-        dxn = dxn + dot(dv_ref[tok, :], wv_ref[...], 1, 1)
-        parts = []
-        for s in range(T // SPAN):
-            row = far_ref[s % spt, pl.ds(j * nseq + s // spt, 1), :]
-            parts.append(dxn[s * SPAN : (s + 1) * SPAN] + row)
-        gd = jnp.concatenate(parts, axis=0) * ga
-        coef = jnp.mean(gd * xr, axis=1, keepdims=True)
-        din_ref[...] = (dmid_ref[...].astype(f32) + r * (gd - xr * coef)).astype(bf)
+    @pl.when(i > n)
+    def _():
+        to_input(i - n, products(i - n))
 
     if near:
 
@@ -730,8 +737,10 @@
         rows, ln, sq = where(u)
         qbd, dbd = pair_diag(q_ref[rows, ln]), pair_diag(da_ref[rows, ln])
         dv = dot(jnp.concatenate([pn, pf], axis=0), dbd)
-        dk = dot(jnp.concatenate([dsn, dsf], axis=0), qbd)
-        dq = dot(k_ref[rows, ln], dsn, 0, 0) + dot(ks_ref[sq, :, ln], dsf, 0, 0)
+        ds = jnp.concatenate([dsn, dsf], axis=0)
+        dk = dot(ds, qbd)
+        ke = jnp.concatenate([k_ref[rows, ln], ks_ref[sq, :, ln]], axis=0)
+        dq = dot(ke, ds, 0, 0)
         dq = jnp.concatenate([dq[:HD, :SPAN], dq[HD:, SPAN:]], axis=0) * (HD**-0.5)
         dq_ref[rows, ln] = dq.astype(bf).T
         dk_ref[rows, ln] = dk[:SPAN].astype(bf)
@@ -789,7 +798,7 @@
     else:
         out_specs.append(full((3, D, D)))
         out_shape.append(sds((3, D, D), f32))
-    scratch += [pltpu.SemaphoreType.DMA((copies,))] * 2
+    scratch += [pltpu.SemaphoreType.DMA((max(copies, 1),))] * 2
     return pl.pallas_call(
         partial(back_kernel, dims, slots, pack, near),
         grid=(2 * n,),
@@ -804,6 +813,50 @@
     )(*args)
 
 
+def last_kernel(rd, rf, din_ref, m_ref, a_ref, wq_ref, wk_ref, wv_ref, wu_ref, ga_ref, gm_ref,
+                out_ref, gq_ref, gk_ref, gv_ref, go_ref, gu_ref, gd_ref, gga_ref, ggm_ref):
+    out_ref[...] = din_ref[...].astype(f32)
+    D = out_ref.shape[1]
+    FF = gu_ref.shape[1]
+
+    @pl.when(pl.program_id(0) == 0)
+    def _():
+        attn = jnp.zeros((rd, 1), f32)
+        for j, (w_ref, g_ref) in enumerate(((wq_ref, gq_ref), (wk_ref, gk_ref), (wv_ref, gv_ref))):
+            g = a_ref[j * rd : (j + 1) * rd, :]
+            g_ref[...] = g
+            attn = attn + jnp.sum(g * w_ref[...].astype(f32), axis=1, keepdims=True)
+        go_ref[...] = m_ref[:rd, :]
+        up = jnp.zeros((rd, 1), f32)
+        for j in range(FF // D):
+            g = m_ref[rd * (j + 1) : rd * (j + 2), :]
+            gu_ref[:, j * D : (j + 1) * D] = g
+            up = up + jnp.sum(g * wu_ref[:, j * D : (j + 1) * D].astype(f32), axis=1, keepdims=True)
+        gd_ref[...] = m_ref[rd * (FF // D + 1) :, :]
+        for total, gain, out in ((attn, ga_ref, gga_ref), (up, gm_ref, ggm_ref)):
+            row = jnp.broadcast_to(total, (rd, 128)).T[:1, :]
+            out[...] = row[:, :rd] / gain[...].astype(f32)
+
+
+def last_call(block, din, sums_m, sums_a, wq, wk, wv, wu, ga, gm):
+    n_tok, D = din.shape
+    rd, FF = wu.shape
+    rf = sums_m.shape[0] - rd * (FF // D + 1)
+    tok = pl.BlockSpec((block, D), lambda i: (i, 0))
+    args = [sums_m, sums_a, wq, wk, wv, wu, ga, gm]
+    shapes = [(rd, D)] * 4 + [(rd, FF), (rf, D), (1, rd), (1, rd)]
+    return pl.pallas_call(
+        partial(last_kernel, rd, rf),
+        grid=(n_tok // block,),
+        in_specs=[tok] + [full(a.shape) for a in args],
+        out_specs=[tok] + [full(s) for s in shapes],
+        out_shape=[sds((n_tok, D), f32)] + [sds(s, f32) for s in shapes],
+        compiler_params=pltpu.CompilerParams(
+            vmem_limit_bytes=VMEM_LIMIT, dimension_semantics=("arbitrary",)
+        ),
+    )(din, *args)
+
+
 def body(dims, inputs, lengths, cotangent, w_query, w_key, w_value, w_out, w_up, w_down, gain_attn, gain_mlp):
     seqs, slots, D = inputs.shape
     nz, nx, ny, nc = dims
@@ -811,13 +864,12 @@
     FF = w_up.shape[1]
     rd, rf = w_query.shape[0], w_down.shape[0]
     n_tok = seqs * slots
-    block = 512
+    block = 1024
     x = inputs.reshape(n_tok, D)
     cot = cotangent.reshape(n_tok, D)
-    gains = jnp.zeros((8, 256), f32)
-    gains = gains.at[0, :rd].set(gain_attn.astype(f32)).at[1, :rd].set(gain_mlp.astype(f32))
+    gains = [g.reshape(1, rd) for g in (gain_attn, gain_mlp)]
     everyone = ("dp", "seq")
-    near = rd % 16 == 0 and n_tok // block >= 12
+    near = rd % 16 == 0 and n_tok // block >= 6
     if near:
         w_first, w_later = (w_query, w_key, w_value), (w_up, w_down, w_out)
     else:
@@ -828,22 +880,20 @@
         w_first, w_later = (wq, wk, wv), ()
     q, k, v, att, lse, ks, vs, mean, ga, gm, *later = front_call(dims, slots, block, x, w_first, w_later, gains, near)
     if near:
-        *firsts, wu, wd, wo = (w.reshape(-1, w.shape[-1]) for w in later)
-        wq, wk, wv = firsts
+        wq, wk, wv, wu, wd, wo = (w.reshape(-1, w.shape[-1]) for w in later)
     pack = ndev if near else 32
-    output, datt, dmid, sums_m = mlp_call(512, slots, 2 * block, pack, lengths, x, att, cot, wo, wu, wd, gm)
+    output, datt, dmid, sums_m = mlp_call(512, slots, block, pack, lengths, x, att, cot, wo, wu, wd, gm)
     grad_in, *sums = back_call(
         dims, slots, block, pack, near, x, q, k, v, datt, lse, dmid, mean, ks, vs, wq, wk, wv, ga, sums_m
     )
-    pd, pf = D // pack, FF // pack
-    last = pd * (FF // D + 1) + pf
-    if near:
-        sums_m, sums_a = sums
-        g_out = sums_m[:pd]
-        g_up = jnp.concatenate([sums_m[pd * (j + 1) : pd * (j + 2)] for j in range(FF // D)], axis=1)
-        g_down = sums_m[pd * (FF // D + 1) : last]
-        g_q, g_k, g_v = (sums_a[j * pd : (j + 1) * pd] for j in range(3))
+    if near:
+        grad_in, g_q, g_k, g_v, g_out, g_up, g_down, g_ga, g_gm = last_call(
+            n_tok // 3, grad_in, *sums, w_query, w_key, w_value, w_up, *gains
+        )
+        g_ga, g_gm = g_ga.reshape(rd), g_gm.reshape(rd)
     else:
+        pd, pf = D // pack, FF // pack
+        last = pd * (FF // D + 1) + pf
 
         def scattered(a):
             return lax.psum_scatter(a.astype(f32), everyone, scatter_dimension=0, tiled=True)
@@ -854,12 +904,13 @@
         )
         g_down = scattered(sums_m[:, pd * (FF // D + 1) : last].reshape(FF, D))
         g_q, g_k, g_v = (scattered(sums[0][j]) for j in range(3))
-    g_ga = jnp.sum(
-        w_query.astype(f32) * g_q + w_key.astype(f32) * g_k + w_value.astype(f32) * g_v, axis=1
-    ) / gain_attn.astype(f32)
-    g_gm = jnp.sum(w_up.astype(f32) * g_up, axis=1) / gain_mlp.astype(f32)
+        g_ga = jnp.sum(
+            w_query.astype(f32) * g_q + w_key.astype(f32) * g_k + w_value.astype(f32) * g_v, axis=1
+        ) / gain_attn.astype(f32)
+        g_gm = jnp.sum(w_up.astype(f32) * g_up, axis=1) / gain_mlp.astype(f32)
+        grad_in = grad_in.astype(f32)
     return (
-        output.reshape(inputs.shape), grad_in.astype(f32).reshape(inputs.shape),
+        output.reshape(inputs.shape), grad_in.reshape(inputs.shape),
         g_q, g_k, g_v, g_out, g_up, g_down, g_ga, g_gm,
     )
 

time: 267 us -> 239 us (0.90)
  other arithmetic: 14.1 us -> 0 us
  Pallas kernels: 249 us -> 238 us
    reshape x1 -> x0, other arithmetic: 9.28 us -> none  [body(): grad_in.astype(f32).reshape(inputs.shape)]
    pallas_call x1, Pallas kernels: 75.1 us -> 69 us  [back_call(): pl.pallas_call(partial(back_kernel, dims, slots, pack, near), grid=(2 * n...]
    pallas_call x1 -> x2, Pallas kernels: 71.8 us -> 67.3 us  [the longest x1 59.5 us: front_call(): pl.pallas_call(partial(front_kernel, dims, slots, n_first, n_later), grid...]
where the time goes in v3:
time: 239 us
  Pallas kernels  238 us (100%)
    pallas_call x1, Pallas kernels, mlp_call(): pl.pallas_call(partial(mlp_kernel, chunk, slots, ndev), grid=(n_tok // bl...  102 us
    pallas_call x1, Pallas kernels, back_call(): pl.pallas_call(partial(back_kernel, dims, slots, pack, near), grid=(2 * n...  69 us
    pallas_call x1, Pallas kernels, front_call(): pl.pallas_call(partial(front_kernel, dims, slots, n_first, n_later), grid...  59.5 us
    pallas_call x1, Pallas kernels, last_call(): pl.pallas_call(partial(last_kernel, rd, rf), grid=(n_tok // block,), in_s...  7.77 us

profile of v3, /device:TPU:0, one launch (start us, length us, event | category | flops | bytes accessed | tf_op | source)
XLA Modules:
  0.0 239.2 jit_solution(3218081281062421269)
XLA Ops:
  0.6 59.5 %shard_map.186 = (bf16[6144,512]{1,0:T(8,128)(2,1)}, bf16[6144,512]{1,0:T(8,128)(2,1)}, bf16[6144,512]{1,0:T(8,128)(2,1)}, bf16[6144,512]{1,0:T(8,128)(2,1)}, f3...) custom-call(bf16[6144,512]{1,0:T(8,128)(2,1)} %bitcast.12, ...), custom_call_target="tpu_custom_call" | custom-call | tf_op jit(solution)/shard_map/pallas_call | solution.py:355
  60.1 102.1 %shard_map.187 = (bf16[6144,512]{1,0:T(8,128)(2,1)}, bf16[6144,512]{1,0:T(8,128)(2,1)}, bf16[6144,512]{1,0:T(8,128)(2,1)}, bf16[32,144,512]{2,1,0:T(8,128)(2,1)}) custom-call(s32[24]{0:T(128)} %len_ref.1, bf16[6144,512]{1,0:T(8,128)(2,1)} %bitcast.13, bf16[6144,512]{1,0:T(8,128)(2,1)} %get-tuple-element.42.att_ref, bf16[6144,512]{1,0:T(8,128)(2,1)} %bitcast.15, ...), custom_call_target="tpu_custom_call" | custom-call | tf_op jit(solution)/shard_map/pallas_call | solution.py:459
  162.2 69.0 %shard_map.188 = (bf16[6144,512]{1,0:T(8,128)(2,1)}, f32[144,512]{1,0:T(8,128)}, f32[48,512]{1,0:T(8,128)}) custom-call(bf16[6144,512]{1,0:T(8,128)(2,1)} %bitcast.14, bf16[6144,512]{1,0:T(8,128)(2,1)} %get-tuple-element.48.refs_1_, bf16[6144,512]{1,0:T(8,128)(2,1)} %get-tuple-element.49.refs_2_, bf16[6144,512]{1,0:T(8,128)(2,1)} %get-tuple-element.50.refs_3_, ...), custom_call_target="tpu_custom_call" | custom-call | tf_op jit(solution)/shard_map/pallas_call | solution.py:802
  231.3 7.8 %shard_map.189 = (f32[6144,512]{1,0:T(8,128)}, f32[16,512]{1,0:T(8,128)}, f32[16,512]{1,0:T(8,128)}, f32[16,512]{1,0:T(8,128)}, f32[16,512]{1,0:T(8,128)}, /*ind...) custom-call(bf16[6144,512]{1,0:T(8,128)(2,1)} %get-tuple-element.62.din_ref, ...), custom_call_target="tpu_custom_call" | custom-call | tf_op jit(solution)/shard_map/pallas_call | solution.py:848

commit v4 on v3

--- a/solution.py
+++ b/solution.py
@@ -36,6 +36,12 @@
     lane = lax.broadcasted_iota(jnp.int32, a.shape, 1)
     zero = jnp.zeros_like(a)
     return jnp.concatenate([jnp.where(lane < HD, a, zero), jnp.where(lane >= HD, a, zero)], axis=0)
+
+
+def unit_rows(x_ref):
+    x = x_ref[...].astype(f32)
+    r = lax.rsqrt(jnp.mean(x * x, axis=1, keepdims=True) + EPS)
+    return x * r, r
 
 
 def causal_mask():
@@ -202,10 +208,10 @@
     def _():
         for copy in own_first + own_later:
             copy.start()
-        slab = jnp.concatenate([ga_own[...], gm_own[...]], axis=0).astype(f32)
-        gain_ref[mine] = jnp.concatenate(
-            [jnp.concatenate([slab, jnp.zeros((2, max(128 - rd, 0)), f32)], axis=1)[:, :128], jnp.zeros((14, 128), f32)], axis=0
-        ).astype(bf)
+        slab = jnp.concatenate([ga_own[...], gm_own[...]], axis=0).astype(f32)[:, :128]
+        if rd < 128:
+            slab = jnp.concatenate([slab, jnp.zeros((2, 128 - rd), f32)], axis=1)
+        gain_ref[mine] = jnp.concatenate([slab, jnp.zeros((14, 128), f32)], axis=0).astype(bf)
         seq_peers = [(dp, (seq + o) % seqn) for o in range(1, seqn)]
         zx = [pc.at(**{a: to}) for a in ("z", "x") for _, to, _ in pc.partners(a)]
         pc.greet(zx + seq_peers)
@@ -213,25 +219,22 @@
         for copy in own_first:
             copy.wait()
         start(first[0])
-
-    x = x_ref[...].astype(f32)
-    r = lax.rsqrt(jnp.mean(x * x, axis=1, keepdims=True) + EPS)
-    xr = x * r
-
-    @pl.when(i < n)
-    def _():
-        for s in range(T // SPAN):
-            row = jnp.sum(xr[s * SPAN : (s + 1) * SPAN], axis=0, keepdims=True) * (1.0 / SPAN)
-            own_mean[s % spt, pl.ds(i * nseq + s // spt, 1), :] = row
-
-    @pl.when(i == 1)
-    def _():
-        finish(first[0])
-        start(first[1])
         for copy in own_later:
             copy.wait()
         if near:
             start(later_phases[0])
+
+    @pl.when(i < n)
+    def _():
+        xr, _ = unit_rows(x_ref)
+        for s in range(T // SPAN):
+            row = jnp.sum(xr[s * SPAN : (s + 1) * SPAN], axis=0, keepdims=True) * (1.0 / SPAN)
+            own_mean[s % spt, pl.ds(i * nseq + s // spt, 1), :] = row
+
+    @pl.when(i == 1)
+    def _():
+        finish(first[0])
+        start(first[1])
 
     @pl.when(i == n - 1)
     def _():
@@ -241,6 +244,9 @@
         start(means)
         finish(first[2])
         start(first[3])
+        if near:
+            finish(later_phases[0])
+            start(later_phases[1])
         finish(means)
         mean_ref[...] = all_mean[...]
         to = lax.broadcasted_iota(jnp.int32, (seqs * FARP, spans_all * seqs), 0)
@@ -258,7 +264,7 @@
         vs_ref[...] = dot(mb, w_refs[2][...]).astype(bf).reshape(seqs, FARP, D)
 
     if near:
-        for k, at in ((1, 0), (2, 2), (3, 5)):
+        for k, at in ((2, 1), (3, 4)):
 
             @pl.when(i == n + at)
             def _(k=k):
@@ -268,11 +274,26 @@
     @pl.when(i >= n)
     def _():
         j = i - n
-        xn = (xr * ga_ref[...]).astype(bf)
-        q_ref[...] = (dot(xn, w_refs[0][...]).astype(bf) * (HD**-0.5)).astype(bf)
-        k_ref[...] = dot(xn, w_refs[1][...]).astype(bf)
-        v_ref[...] = dot(xn, w_refs[2][...]).astype(bf)
-        attend_forward(slots, j, seq, q_ref, k_ref, v_ref, ks_ref, vs_ref, att_ref, lse_ref)
+        xn = (unit_rows(x_ref)[0] * ga_ref[...]).astype(bf)
+        sub = T // 4
+        cuts = [(k, h) for k in range(3) for h in (slice(0, D // 2), slice(D // 2, D))]
+
+        def project(b):
+            rows = slice(b * sub, (b + 1) * sub)
+
+            def part(k, h):
+                y = dot(xn[rows], w_refs[k][:, h]).astype(bf)
+                (q_ref, k_ref, v_ref)[k][rows, h] = (y * (HD**-0.5)).astype(bf) if k == 0 else y
+
+            return [partial(part, k, h) for k, h in cuts]
+
+        for work in project(0):
+            work()
+        each = sub // SPAN * (D // 128)
+        beside = {}
+        for b in range(1, 4):
+            beside.update(spread_out(project(b), (b - 1) * each, b * each - 1))
+        attend_forward(slots, j, seq, q_ref, k_ref, v_ref, ks_ref, vs_ref, att_ref, lse_ref, beside)
 
     if near:
 
@@ -281,7 +302,7 @@
             finish(later_phases[3])
 
 
-def attend_forward(slots, j, seq, q_ref, k_ref, v_ref, ks_ref, vs_ref, att_ref, lse_ref):
+def attend_forward(slots, j, seq, q_ref, k_ref, v_ref, ks_ref, vs_ref, att_ref, lse_ref, beside):
     T, D = q_ref.shape
     spt, nseq = slots // SPAN, T // slots
     causal = causal_mask()
@@ -317,13 +338,15 @@
         lse_ref[2 * p + 1 : 2 * p + 2, rows] = total[:, SPAN:]
 
     units = [(s, p) for s in range(T // SPAN) for p in range(D // 128)]
-    staged(units, scores, weigh, combine)
-
-
-def staged(units, first, second, third):
+    staged(units, scores, weigh, combine, beside)
+
+
+def staged(units, first, second, third, beside=None):
     a, b = {}, {}
     for t in range(0, len(units) + 4, 2):
         for k in (t, t + 1):
+            for work in (beside or {}).get(k, ()):
+                work()
             if k < len(units):
                 a[k] = first(units[k])
         for k in (t - 2, t - 1):
@@ -332,6 +355,13 @@
         for k in (t - 4, t - 3):
             if 0 <= k < len(units):
                 third(units[k], *b.pop(k))
+
+
+def spread_out(works, begin, end):
+    out = {}
+    for j, work in enumerate(works):
+        out.setdefault(begin + j * (end - begin) // len(works), []).append(work)
+    return out
 
 
 def front_call(dims, slots, block, x, w_first, w_later, gains, near):
@@ -572,7 +602,8 @@
     (g1_ref,) = take(1) if near else (None,)
     (din_ref,) = take(1)
     outs = take(2 if near else 1)
-    aq, ak, av, dq_ref, dk_ref, dv_ref, dks_ref, dvs_ref, far_send, far_got, far_ref = take(11)
+    aq, ak, av, dq_ref, dk_ref, dv_ref, dks_ref, dvs_ref, far_ref = take(9)
+    far_send, far_got = take(2), take(2)
     if near:
         (g2_ref, own1) = take(2)
         bufs1, bufs2 = take(9), take(9)
@@ -587,11 +618,11 @@
     spans_all, seqs, _ = mean_ref.shape
     i, n = pl.program_id(0), pl.num_programs(0) // 2
     far = []
-    for o in range(1, seqn):
-        to = (seq + o) % seqn
-        far.append(
-            cp.make(far_send.at[:, pl.ds(to * spt, spt)], far_got.at[o - 1], far_got.at[o - 1], (dp, to))
-        )
+    for send, got in zip(far_send, far_got):
+        far.append([])
+        for o in range(1, seqn):
+            to = (seq + o) % seqn
+            far[-1].append(cp.make(send.at[:, pl.ds(to * spt, spt)], got.at[o - 1], got.at[o - 1], (dp, to)))
     if near:
         own_copy = pltpu.make_async_copy(g1_ref.at[:, :, :, pc.c], own1, own_sem.at[0])
         big = Scatter(pc, cp, g1_ref, lambda z, x: own1[z, x], outs[0], bufs1)
@@ -607,47 +638,68 @@
             own_copy.start()
         for acc in (aq, ak, av):
             acc[...] = jnp.zeros_like(acc)
-
-    @pl.when(i == 1)
-    def _():
         pc.meet(zx + seq_peers)
         if near:
+            big.step(0)
             own_copy.wait()
-            big.step(0)
-
-    if near:
-        for k, at in ((1, n // 3), (2, 2 * n // 3), (3, n - 1), (4, n + 1)):
+
+    if near:
+        for k, at in ((1, 1), (2, n // 2), (3, n - 1), (4, n + n // 3)):
 
             @pl.when(i == at)
             def _(k=k):
                 big.step(k)
 
-    x = x_ref[...].astype(f32)
-    r = lax.rsqrt(jnp.mean(x * x, axis=1, keepdims=True) + EPS)
-    xr = x * r
     ga = ga_ref[...]
 
+    groups = ((0, seqs - nseq), (seqs - nseq, seqs))
+
+    def send_far(g):
+        lo, hi = groups[g]
+        for t in range(spans_all):
+            far_send[g][0, t] = dks_ref[lo:hi, t, :].astype(bf)
+            far_send[g][1, t] = dvs_ref[lo:hi, t, :].astype(bf)
+        start(far[g])
+
+    @pl.when(i == n - 1)
+    def _():
+        send_far(0)
+
     @pl.when(i < n)
     def _():
         tok = pl.ds(pl.multiple_of(i * T, T), T)
+        sub = T // 1
+        xt = (unit_rows(x_ref)[0] * ga).astype(bf).T
+        cuts = [(k, h) for k in range(3) for h in (slice(0, D // 2), slice(D // 2, D))]
+
+        def gather_terms(b):
+            rows = pl.ds(pl.multiple_of(i * T + b * sub, sub), sub)
+
+            def part(k, h):
+                (aq, ak, av)[k][:, h] += dot(xt[:, b * sub : (b + 1) * sub], (dq_ref, dk_ref, dv_ref)[k][rows, h])
+
+            return [partial(part, k, h) for k, h in cuts]
+
+        each = sub // SPAN * (D // 128)
+        beside = {}
+        for b in range(1 - 1):
+            beside.update(spread_out(gather_terms(b), (b + 1) * each + 4, (b + 2) * each + 4))
         attend_backward(slots, i, seq, spans_all, q_ref, k_ref, v_ref, da_ref, ks_ref, vs_ref, lse_ref,
-                        dq_ref.at[tok], dk_ref.at[tok], dv_ref.at[tok], dks_ref, dvs_ref)
-        xt = (xr * ga).astype(bf).T
-        aq[...] += dot(xt, dq_ref[tok, :])
-        ak[...] += dot(xt, dk_ref[tok, :])
-        av[...] += dot(xt, dv_ref[tok, :])
+                        dq_ref.at[tok], dk_ref.at[tok], dv_ref.at[tok], dks_ref, dvs_ref, beside)
+        for work in gather_terms(1 - 1):
+            work()
 
     @pl.when(i == n - 1)
     def _():
-        for t in range(spans_all):
-            far_send[0, t] = dks_ref[:, t, :].astype(bf)
-            far_send[1, t] = dvs_ref[:, t, :].astype(bf)
-        start(far)
-        mb = (mean_ref[...].astype(f32).reshape(spans_all * seqs, D) * ga).astype(bf)
-        fk = far_send[0].reshape(spans_all * seqs, D)
-        fv = far_send[1].reshape(spans_all * seqs, D)
+        send_far(1)
+        mean = mean_ref[...].astype(f32)
+        terms = [jnp.zeros((D, D), f32)] * 2
+        for g, (lo, hi) in enumerate(groups):
+            mb = (mean[:, lo:hi].reshape(spans_all * (hi - lo), D) * ga).astype(bf)
+            for h in range(2):
+                terms[h] = terms[h] + dot(mb, far_send[g][h].reshape(spans_all * (hi - lo), D), 0, 0)
         rows = D // pack
-        parts = (aq[...], ak[...] + dot(mb, fk, 0, 0), av[...] + dot(mb, fv, 0, 0))
+        parts = (aq[...], ak[...] + terms[0], av[...] + terms[1])
         for j, part in enumerate(parts):
             if near:
                 g2_ref[:, :, :, :, j * rows : (j + 1) * rows, :] = part.astype(bf).reshape(dims + (rows, D))
@@ -668,21 +720,23 @@
             row = far_ref[s % spt, pl.ds(j * nseq + s // spt, 1), :]
             parts.append(dxn[s * SPAN : (s + 1) * SPAN] + row)
         gd = jnp.concatenate(parts, axis=0) * ga
+        xr, r = unit_rows(x_ref)
         coef = jnp.mean(gd * xr, axis=1, keepdims=True)
         din_ref[...] = (dmid_ref[...].astype(f32) + r * (gd - xr * coef)).astype(bf)
 
     @pl.when(i == n)
     def _():
         dxn = products(0)
-        finish(far)
-        tot = []
-        for h in range(2):
-            acc = far_send[h, pl.ds(seq * spt, spt)].astype(f32)
-            for o in range(seqn - 1):
-                acc = acc + far_got[o, h].astype(f32)
-            tot.append(acc.astype(bf).reshape(spt * seqs, D))
-        rows = dot(tot[0], wk_ref[...], 1, 1) + dot(tot[1], wv_ref[...], 1, 1)
-        far_ref[...] = (rows * (1.0 / SPAN)).reshape(spt, seqs, D)
+        for g, (lo, hi) in enumerate(groups):
+            finish(far[g])
+            tot = []
+            for h in range(2):
+                acc = far_send[g][h, pl.ds(seq * spt, spt)].astype(f32)
+                for o in range(seqn - 1):
+                    acc = acc + far_got[g][o, h].astype(f32)
+                tot.append(acc.astype(bf).reshape(spt * (hi - lo), D))
+            rows = dot(tot[0], wk_ref[...], 1, 1) + dot(tot[1], wv_ref[...], 1, 1)
+            far_ref[:, lo:hi, :] = (rows * (1.0 / SPAN)).reshape(spt, hi - lo, D)
         to_input(0, dxn)
 
     if near:
@@ -704,7 +758,7 @@
 
 
 def attend_backward(slots, i, seq, spans_all, q_ref, k_ref, v_ref, da_ref, ks_ref, vs_ref, lse_ref,
-                    dq_ref, dk_ref, dv_ref, dks_ref, dvs_ref):
+                    dq_ref, dk_ref, dv_ref, dks_ref, dvs_ref, beside):
     T, D = q_ref.shape
     spt, nseq = slots // SPAN, T // slots
     causal = causal_mask()
@@ -754,14 +808,14 @@
             dvs_ref[sq, :, ln] += fv
 
     units = [(s, p) for s in range(T // SPAN) for p in range(D // 128)]
-    staged(units, scores, weigh, combine)
+    staged(units, scores, weigh, combine, beside)
 
 
 def back_call(dims, slots, block, pack, near, x, q, k, v, da, lse, dmid, mean, ks, vs, wq, wk, wv, ga, g1):
     n_tok, D = x.shape
     nz, nx, ny, nc = dims
     n = n_tok // block
-    spt = slots // SPAN
+    spt, nseq = slots // SPAN, block // slots
     spans_all, seqs, _ = mean.shape
     seqn = ny * nc
     vm = pltpu.VMEM
@@ -780,11 +834,13 @@
     out_specs, out_shape = [late], [sds((n_tok, D), bf)]
     scratch = [vm((D, D), f32)] * 3 + [vm((n_tok, D), bf)] * 3 + [vm((seqs, spans_all, D), f32)] * 2
     scratch += [
-        vm((2, spans_all, seqs, D), bf),
-        vm((seqn - 1, 2, spt, seqs, D), bf),
         vm((spt, seqs, D), f32),
+        vm((2, spans_all, seqs - nseq, D), bf),
+        vm((2, spans_all, nseq, D), bf),
+        vm((max(seqn - 1, 1), 2, spt, seqs - nseq, D), bf),
+        vm((max(seqn - 1, 1), 2, spt, nseq, D), bf),
     ]
-    copies = seqn - 1
+    copies = 2 * (seqn - 1)
     if near:
         rows1 = g1.shape[1]
         args.append(g1.reshape(dims + g1.shape[1:]))

time: 239 us -> 234 us (0.979)
  Pallas kernels: 238 us -> 233 us
    pallas_call x1, Pallas kernels: 69 us -> 66.3 us  [back_call(): pl.pallas_call(partial(back_kernel, dims, slots, pack, near), grid=(2 * n...]
where the time goes in v4:
time: 234 us
  Pallas kernels  233 us (100%)
    pallas_call x1, Pallas kernels, mlp_call(): pl.pallas_call(partial(mlp_kernel, chunk, slots, ndev), grid=(n_tok // bl...  102 us
    pallas_call x1, Pallas kernels, back_call(): pl.pallas_call(partial(back_kernel, dims, slots, pack, near), grid=(2 * n...  66.3 us
    pallas_call x1, Pallas kernels, front_call(): pl.pallas_call(partial(front_kernel, dims, slots, n_first, n_later), grid...  57.3 us
    pallas_call x1, Pallas kernels, last_call(): pl.pallas_call(partial(last_kernel, rd, rf), grid=(n_tok // block,), in_s...  7.77 us

profile of v4, /device:TPU:0, one launch (start us, length us, event | category | flops | bytes accessed | tf_op | source)
XLA Modules:
  0.0 234.2 jit_solution(17784155439119975099)
XLA Ops:
  0.6 57.3 %shard_map.186 = (bf16[6144,512]{1,0:T(8,128)(2,1)}, bf16[6144,512]{1,0:T(8,128)(2,1)}, bf16[6144,512]{1,0:T(8,128)(2,1)}, bf16[6144,512]{1,0:T(8,128)(2,1)}, f3...) custom-call(bf16[6144,512]{1,0:T(8,128)(2,1)} %bitcast.12, ...), custom_call_target="tpu_custom_call" | custom-call | tf_op jit(solution)/shard_map/pallas_call | solution.py:385
  57.9 102.1 %shard_map.187 = (bf16[6144,512]{1,0:T(8,128)(2,1)}, bf16[6144,512]{1,0:T(8,128)(2,1)}, bf16[6144,512]{1,0:T(8,128)(2,1)}, bf16[32,144,512]{2,1,0:T(8,128)(2,1)}) custom-call(s32[24]{0:T(128)} %len_ref.1, bf16[6144,512]{1,0:T(8,128)(2,1)} %bitcast.13, bf16[6144,512]{1,0:T(8,128)(2,1)} %get-tuple-element.42.att_ref, bf16[6144,512]{1,0:T(8,128)(2,1)} %bitcast.15, ...), custom_call_target="tpu_custom_call" | custom-call | tf_op jit(solution)/shard_map/pallas_call | solution.py:489
  160.0 66.3 %shard_map.188 = (bf16[6144,512]{1,0:T(8,128)(2,1)}, f32[144,512]{1,0:T(8,128)}, f32[48,512]{1,0:T(8,128)}) custom-call(bf16[6144,512]{1,0:T(8,128)(2,1)} %bitcast.14, bf16[6144,512]{1,0:T(8,128)(2,1)} %get-tuple-element.48.refs_1_, bf16[6144,512]{1,0:T(8,128)(2,1)} %get-tuple-element.49.refs_2_, bf16[6144,512]{1,0:T(8,128)(2,1)} %get-tuple-element.50.refs_3_, ...), custom_call_target="tpu_custom_call" | custom-call | tf_op jit(solution)/shard_map/pallas_call | solution.py:858
  226.3 7.8 %shard_map.189 = (f32[6144,512]{1,0:T(8,128)}, f32[16,512]{1,0:T(8,128)}, f32[16,512]{1,0:T(8,128)}, f32[16,512]{1,0:T(8,128)}, f32[16,512]{1,0:T(8,128)}, /*ind...) custom-call(bf16[6144,512]{1,0:T(8,128)(2,1)} %get-tuple-element.62.din_ref, ...), custom_call_target="tpu_custom_call" | custom-call | tf_op jit(solution)/shard_map/pallas_call | solution.py:904

commit v5 on v4

--- a/solution.py
+++ b/solution.py
@@ -13,7 +13,7 @@
 EPS = 1e-06
 K0 = 0.7978845608028654
 K1 = 0.044715
-FARP = 16
+FARP = 8
 f32 = jnp.float32
 bf = jnp.bfloat16
 MESH = pl.DeviceIdType.MESH
@@ -641,13 +641,14 @@
         pc.meet(zx + seq_peers)
         if near:
             big.step(0)
-            own_copy.wait()
 
     if near:
         for k, at in ((1, 1), (2, n // 2), (3, n - 1), (4, n + n // 3)):
 
             @pl.when(i == at)
             def _(k=k):
+                if k == 1:
+                    own_copy.wait()
                 big.step(k)
 
     ga = ga_ref[...]

time: 234 us -> 234 us (level)
  no operation moved by 1% of the time
where the time goes in v5:
time: 234 us
  Pallas kernels  233 us (100%)
    pallas_call x1, Pallas kernels, mlp_call(): pl.pallas_call(partial(mlp_kernel, chunk, slots, ndev), grid=(n_tok // bl...  102 us
    pallas_call x1, Pallas kernels, back_call(): pl.pallas_call(partial(back_kernel, dims, slots, pack, near), grid=(2 * n...  65.9 us
    pallas_call x1, Pallas kernels, front_call(): pl.pallas_call(partial(front_kernel, dims, slots, n_first, n_later), grid...  57 us
    pallas_call x1, Pallas kernels, last_call(): pl.pallas_call(partial(last_kernel, rd, rf), grid=(n_tok // block,), in_s...  7.77 us

profile of v5, /device:TPU:0, one launch (start us, length us, event | category | flops | bytes accessed | tf_op | source)
XLA Modules:
  0.0 233.6 jit_solution(5794486331301556922)
XLA Ops:
  0.6 57.0 %shard_map.186 = (bf16[6144,512]{1,0:T(8,128)(2,1)}, bf16[6144,512]{1,0:T(8,128)(2,1)}, bf16[6144,512]{1,0:T(8,128)(2,1)}, bf16[6144,512]{1,0:T(8,128)(2,1)}, f3...) custom-call(bf16[6144,512]{1,0:T(8,128)(2,1)} %bitcast.12, ...), custom_call_target="tpu_custom_call" | custom-call | tf_op jit(solution)/shard_map/pallas_call | solution.py:385
  57.6 102.1 %shard_map.187 = (bf16[6144,512]{1,0:T(8,128)(2,1)}, bf16[6144,512]{1,0:T(8,128)(2,1)}, bf16[6144,512]{1,0:T(8,128)(2,1)}, bf16[32,144,512]{2,1,0:T(8,128)(2,1)}) custom-call(s32[24]{0:T(128)} %len_ref.1, bf16[6144,512]{1,0:T(8,128)(2,1)} %bitcast.13, bf16[6144,512]{1,0:T(8,128)(2,1)} %get-tuple-element.42.att_ref, bf16[6144,512]{1,0:T(8,128)(2,1)} %bitcast.15, ...), custom_call_target="tpu_custom_call" | custom-call | tf_op jit(solution)/shard_map/pallas_call | solution.py:489
  159.7 65.9 %shard_map.188 = (bf16[6144,512]{1,0:T(8,128)(2,1)}, f32[144,512]{1,0:T(8,128)}, f32[48,512]{1,0:T(8,128)}) custom-call(bf16[6144,512]{1,0:T(8,128)(2,1)} %bitcast.14, bf16[6144,512]{1,0:T(8,128)(2,1)} %get-tuple-element.48.refs_1_, bf16[6144,512]{1,0:T(8,128)(2,1)} %get-tuple-element.49.refs_2_, bf16[6144,512]{1,0:T(8,128)(2,1)} %get-tuple-element.50.refs_3_, ...), custom_call_target="tpu_custom_call" | custom-call | tf_op jit(solution)/shard_map/pallas_call | solution.py:859
  225.6 7.8 %shard_map.189 = (f32[6144,512]{1,0:T(8,128)}, f32[16,512]{1,0:T(8,128)}, f32[16,512]{1,0:T(8,128)}, f32[16,512]{1,0:T(8,128)}, f32[16,512]{1,0:T(8,128)}, /*ind...) custom-call(bf16[6144,512]{1,0:T(8,128)(2,1)} %get-tuple-element.62.din_ref, ...), custom_call_target="tpu_custom_call" | custom-call | tf_op jit(solution)/shard_map/pallas_call | solution.py:905

commit v6 on v4

--- a/solution.py
+++ b/solution.py
@@ -82,7 +82,8 @@
 
     def partners(self, axis):
         me, n = self.line(axis)
-        return [(o, (me + o) % n, (me + n - o) % n) for o in range(1, n)]
+        order = sorted(range(1, n), key=lambda o: abs(2 * o - n))
+        return [(o, (me + o) % n, (me + n - o) % n) for o in order]
 
     def greet(self, others):
         for other in others:

time: 234 us -> 234 us (level)
  no operation moved by 1% of the time
where the time goes in v6:
time: 234 us; the launch traced here: 233 us
  Pallas kernels  232 us (99%)
    pallas_call x1, Pallas kernels, mlp_call(): pl.pallas_call(partial(mlp_kernel, chunk, slots, ndev), grid=(n_tok // bl...  102 us
    pallas_call x1, Pallas kernels, back_call(): pl.pallas_call(partial(back_kernel, dims, slots, pack, near), grid=(2 * n...  65.3 us
    pallas_call x1, Pallas kernels, front_call(): pl.pallas_call(partial(front_kernel, dims, slots, n_first, n_later), grid...  57.3 us
    pallas_call x1, Pallas kernels, last_call(): pl.pallas_call(partial(last_kernel, rd, rf), grid=(n_tok // block,), in_s...  7.77 us

profile of v6, /device:TPU:0, one launch (start us, length us, event | category | flops | bytes accessed | tf_op | source)
XLA Modules:
  0.0 233.3 jit_solution(17549639281949430986)
XLA Ops:
  0.6 57.3 %shard_map.186 = (bf16[6144,512]{1,0:T(8,128)(2,1)}, bf16[6144,512]{1,0:T(8,128)(2,1)}, bf16[6144,512]{1,0:T(8,128)(2,1)}, bf16[6144,512]{1,0:T(8,128)(2,1)}, f3...) custom-call(bf16[6144,512]{1,0:T(8,128)(2,1)} %bitcast.12, ...), custom_call_target="tpu_custom_call" | custom-call | tf_op jit(solution)/shard_map/pallas_call | solution.py:386
  57.9 102.1 %shard_map.187 = (bf16[6144,512]{1,0:T(8,128)(2,1)}, bf16[6144,512]{1,0:T(8,128)(2,1)}, bf16[6144,512]{1,0:T(8,128)(2,1)}, bf16[32,144,512]{2,1,0:T(8,128)(2,1)}) custom-call(s32[24]{0:T(128)} %len_ref.1, bf16[6144,512]{1,0:T(8,128)(2,1)} %bitcast.13, bf16[6144,512]{1,0:T(8,128)(2,1)} %get-tuple-element.42.att_ref, bf16[6144,512]{1,0:T(8,128)(2,1)} %bitcast.15, ...), custom_call_target="tpu_custom_call" | custom-call | tf_op jit(solution)/shard_map/pallas_call | solution.py:490
  160.0 65.3 %shard_map.188 = (bf16[6144,512]{1,0:T(8,128)(2,1)}, f32[144,512]{1,0:T(8,128)}, f32[48,512]{1,0:T(8,128)}) custom-call(bf16[6144,512]{1,0:T(8,128)(2,1)} %bitcast.14, bf16[6144,512]{1,0:T(8,128)(2,1)} %get-tuple-element.48.refs_1_, bf16[6144,512]{1,0:T(8,128)(2,1)} %get-tuple-element.49.refs_2_, bf16[6144,512]{1,0:T(8,128)(2,1)} %get-tuple-element.50.refs_3_, ...), custom_call_target="tpu_custom_call" | custom-call | tf_op jit(solution)/shard_map/pallas_call | solution.py:859
  225.3 7.8 %shard_map.189 = (f32[6144,512]{1,0:T(8,128)}, f32[16,512]{1,0:T(8,128)}, f32[16,512]{1,0:T(8,128)}, f32[16,512]{1,0:T(8,128)}, f32[16,512]{1,0:T(8,128)}, /*ind...) custom-call(bf16[6144,512]{1,0:T(8,128)(2,1)} %get-tuple-element.62.din_ref, ...), custom_call_target="tpu_custom_call" | custom-call | tf_op jit(solution)/shard_map/pallas_call | solution.py:905
